TPU v7x, 128 devices: a whole 4x4x4 slice. The times are simulated.
128 devices in a mesh: space: 32 (over z, x, core), chan: 4 (over y).
Axes of the slice: x: 4, y: 4, z: 4, core: 2. Of those that a mesh axis runs over, the one named last changes fastest.
Arguments:
- inputs: bfloat16 [512, 64, 2, 128], P('chan', 'space'), may hold values from -6 to 6
- weight_one: bfloat16 [512, 27, 512], P(None, None, 'chan'), may hold values from -0.0546875 to 0.0546875
- weight_two: bfloat16 [512, 27, 512], P(None, None, 'chan'), may hold values from -0.0546875 to 0.0546875
- cotangent: bfloat16 [512, 64, 2, 128], P('chan', 'space'), may hold values from -6 to 6
Outputs:
- result: bfloat16 [512, 64, 2, 128], P('chan', 'space')
- input_grad: bfloat16 [512, 64, 2, 128], P('chan', 'space')
- grad_one: float32 [512, 27, 512], P('space', None, 'chan')
- grad_two: float32 [512, 27, 512], P('space', None, 'chan')
All inputs are finite; a program needn't handle non-finite values.
Results may differ from a plain program's by a relative error of at most 0.02.
Values may be sent and summed in bfloat16 or wider, within the bound.
No kernel may reach another device: no remote copies, remote signals or barrier semaphores. Data moves between devices by JAX's collectives and lax.ppermute only.
A program may use at most 192 MiB of HBM per device.

v0:
```python
import functools

import jax
import jax.numpy as jnp
from jax import lax
from jax.experimental import pallas as pl
from jax.experimental.pallas import tpu as pltpu
from jax.sharding import PartitionSpec as P

BF16 = jnp.bfloat16
F32 = jnp.float32
TAPS = [(i, k) for i in range(3) for k in range(3)]
LANES = (slice(128, 384), slice(0, 256))


def call(kernel, out_shapes, operands, scratch=(), flops=0):
    nbytes = sum(a.size * a.dtype.itemsize for a in operands)
    nbytes += sum(a.size * a.dtype.itemsize for a in out_shapes)
    return pl.pallas_call(
        kernel,
        out_shape=tuple(out_shapes),
        in_specs=[pl.BlockSpec(memory_space=pltpu.VMEM)] * len(operands),
        out_specs=tuple(pl.BlockSpec(memory_space=pltpu.VMEM) for _ in out_shapes),
        scratch_shapes=list(scratch),
        compiler_params=pltpu.CompilerParams(vmem_limit_bytes=40 * 1024 * 1024),
        cost_estimate=pl.CostEstimate(flops=flops, bytes_accessed=nbytes, transcendentals=0),
    )(*operands)


def shape(dims, dtype):
    return jax.ShapeDtypeStruct(dims, dtype)


def row_shift(block, down):
    rows = block.shape[0]
    place = lax.broadcasted_iota(jnp.int32, block.shape, 0) % 128
    if down:
        return jnp.where(place == 0, 0.0, pltpu.roll(block, 1, 0))
    return jnp.where(place == 127, 0.0, pltpu.roll(block, rows - 1, 0))


def three_shifts(haloed):
    wide = haloed.astype(F32)
    return (row_shift(wide, False).astype(BF16), haloed, row_shift(wide, True).astype(BF16))


def conv_kernel(own, r1, r2, r3, weight, core_out, inner_out, outer_out, keep_out, send_out, field, flipped):
    y = lax.axis_index("chan")
    core = lax.axis_index("space") % 2
    for step, part in enumerate((own, r1, r2, r3)):
        place = (y ^ step) * 128
        for b in range(2):
            at = pl.multiple_of(b * 512 + place, 128)
            field[:, pl.ds(at, 128)] = part[:, b * 128 : b * 128 + 128]
    values = field[...]
    total = None
    for k in range(3):
        part = []
        for i in range(3):
            tap = 3 * i + k
            rhs = jnp.concatenate([weight[tap, :, LANES[0]], weight[tap, :, LANES[1]]], axis=0)
            part.append(jnp.dot(values, rhs, preferred_element_type=F32))
        planes = jnp.concatenate(
            [
                part[2][:128],
                part[1][:128] + part[2][128:],
                part[0][:128] + part[1][128:],
                part[0][128:],
            ],
            axis=0,
        )
        if k == 0:
            planes = row_shift(planes, True)
        elif k == 2:
            planes = row_shift(planes, False)
        total = planes if total is None else total + planes
    core_out[...] = total[128:384]
    low = total[:128].astype(BF16)
    high = total[384:].astype(BF16)
    first = core == 0
    inner_out[...] = jnp.where(first, high, low)
    outer_out[...] = jnp.where(first, low, high)
    for b in range(2):
        turned = values[:, b * 512 : b * 512 + 512].T
        for group in range(16):
            for half in range(2):
                source = group * 32 + half * 16
                flipped[half, group * 16 : group * 16 + 16, b * 256 : b * 256 + 256] = turned[
                    source : source + 16
                ]
    keep_out[...] = flipped[core]
    send_out[...] = flipped[1 - core]


def conv(own, others, weight):
    outs = [
        shape((256, 256), F32),
        shape((128, 256), BF16),
        shape((128, 256), BF16),
        shape((256, 512), BF16),
        shape((256, 512), BF16),
    ]
    scratch = [pltpu.VMEM((256, 1024), BF16), pltpu.VMEM((2, 256, 512), BF16)]
    return call(conv_kernel, outs, (own, *others, weight), scratch, flops=2 * 9 * 256 * 1024 * 256)


def conv_t_kernel(own, inner, outer, weight, o0, o1, o2, o3, haloed_out):
    y = lax.axis_index("chan")
    first = lax.axis_index("space") % 2 == 0
    low = jnp.where(first, outer[...], inner[...])
    high = jnp.where(first, inner[...], outer[...])
    haloed = jnp.concatenate([low, own[...], high], axis=0)
    haloed_out[...] = haloed
    moved = three_shifts(haloed)
    lhs = jnp.concatenate([moved[k][(2 - i) * 128 : (2 - i) * 128 + 256] for i, k in TAPS], axis=1)
    for step, out in enumerate((o0, o1, o2, o3)):
        rows = pl.ds(pl.multiple_of((y ^ step) * 128, 128), 128)
        rhs = jnp.concatenate(
            [
                jnp.concatenate([weight[3 * i + k, rows, LANES[b]] for i, k in TAPS], axis=1)
                for b in range(2)
            ],
            axis=0,
        )
        out[...] = lax.dot_general(
            lhs, rhs, (((1,), (1,)), ((), ())), preferred_element_type=F32
        ).astype(out.dtype)


def conv_t(own, inner, outer, weight):
    outs = [shape((256, 256), F32)] + [shape((256, 256), BF16)] * 3 + [shape((512, 256), BF16)]
    return call(
        conv_t_kernel, outs, (own, inner, outer, weight), flops=2 * 9 * 256 * 256 * 1024
    )


def middle_kernel(
    own, inner, outer, g0, g1, g2, g3, hidden_out, grad_out, inner_out, outer_out
):
    core = lax.axis_index("space") % 2
    first = core == 0
    zero = jnp.where(first, outer[...], inner[...]).astype(F32)
    one = jnp.where(first, inner[...], outer[...]).astype(F32)
    pre = own[...] + jnp.concatenate([zero, one], axis=0)
    hidden_grad = g0[...] + g1[...].astype(F32) + g2[...].astype(F32) + g3[...].astype(F32)
    sig = jax.nn.sigmoid(pre)
    hidden_out[...] = (pre * sig).astype(BF16)
    grad = (hidden_grad * sig * (1.0 + pre * (1.0 - sig))).astype(BF16)
    grad_out[...] = grad
    inner_out[...] = jnp.where(first, grad[128:], grad[:128])
    outer_out[...] = jnp.where(first, grad[:128], grad[128:])


def middle(own, inner, outer, parts):
    outs = [shape((256, 256), BF16)] * 2 + [shape((128, 256), BF16)] * 2
    return call(middle_kernel, outs, (own, inner, outer, *parts), flops=256 * 256 * 20)


def wprod_kernel(stage, v_own, v_far, d_own, d_far, o0, o1, o2, o3, total):
    near = three_shifts(d_own[...])
    far = three_shifts(d_far[...])
    for i, k in TAPS:
        at = (2 - i) * 128
        rhs = jnp.concatenate([near[k][at : at + 256], far[k][at : at + 256]], axis=0)
        halves = []
        for b in range(2):
            lanes = slice(b * 256, b * 256 + 256)
            lhs = jnp.concatenate([v_own[:, lanes], v_far[:, lanes]], axis=1)
            halves.append(jnp.dot(lhs, rhs, preferred_element_type=F32))
        tap = 3 * i + k
        total[tap, :, 0:128] = halves[1][:, :128]
        total[tap, :, 128:256] = halves[1][:, 128:] + halves[0][:, :128]
        total[tap, :, 256:384] = halves[0][:, 128:]
    space = lax.axis_index("space")
    if stage == "z":
        me = space // 8
        for step, out in enumerate((o0, o1, o2, o3)):
            rows = pl.ds(pl.multiple_of((me ^ step) * 64, 64), 64)
            out[...] = total[:, rows, :].astype(out.dtype)
    else:
        me = (space // 2) % 4
        for step, out in enumerate((o0, o1, o2, o3)):
            for z in range(4):
                rows = pl.ds(pl.multiple_of(z * 64 + (me ^ step) * 16, 16), 16)
                out[:, z * 16 : z * 16 + 16, :] = total[:, rows, :].astype(out.dtype)


def wprod(stage, v_own, v_far, d_own, d_far):
    outs = [shape((9, 64, 384), F32)] + [shape((9, 64, 384), BF16)] * 3
    return call(
        functools.partial(wprod_kernel, stage),
        outs,
        (v_own, v_far, d_own, d_far),
        [pltpu.VMEM((9, 256, 384), F32)],
        flops=2 * 18 * 256 * 512 * 256,
    )


def second_kernel(stage, own, r1, r2, r3, o0, o1, o2, o3, total):
    total[...] = own[...] + r1[...].astype(F32) + r2[...].astype(F32) + r3[...].astype(F32)
    space = lax.axis_index("space")
    me = (space // 2) % 4 if stage == "x" else space // 8
    for step, out in enumerate((o0, o1, o2, o3)):
        rows = pl.ds(pl.multiple_of((me ^ step) * 16, 16), 16)
        out[...] = total[:, rows, :].astype(out.dtype)


def second(stage, parts):
    outs = [shape((9, 16, 384), F32)] + [shape((9, 16, 384), BF16)] * 3
    return call(
        functools.partial(second_kernel, stage), outs, parts, [pltpu.VMEM((9, 64, 384), F32)]
    )


def last_kernel(own, r1, r2, r3, out):
    for i, k in TAPS:
        tap = 3 * i + k
        total = own[tap] + r1[tap].astype(F32) + r2[tap].astype(F32) + r3[tap].astype(F32)
        for j in range(3):
            out[:, 9 * i + 3 * j + k, :] = total[:, (2 - j) * 128 : (2 - j) * 128 + 128]


def last(parts):
    return call(last_kernel, [shape((16, 27, 128), F32)], parts)[0]


def chip(z, x, core):
    return (z * 4 + x) * 2 + core


EVERY = [(z, x, core) for z in range(4) for x in range(4) for core in range(2)]


def over_chan(step):
    return [(i, i ^ step) for i in range(4)]


def over(stage, step):
    if stage == "z":
        return [(chip(z, x, c), chip(z ^ step, x, c)) for z, x, c in EVERY]
    return [(chip(z, x, c), chip(z, x ^ step, c)) for z, x, c in EVERY]


CORES = [(i, i ^ 1) for i in range(32)]
NEIGHBOURS = [(i, i + 1 if i % 2 else i - 1) for i in range(1, 31)]


def swap_halo(inner, outer):
    return lax.ppermute(inner, "space", CORES), lax.ppermute(outer, "space", NEIGHBOURS)


def cells_major(field):
    return field.transpose(1, 3, 2, 0).reshape(256, 256)


def channels_major(block):
    return block.reshape(2, 128, 2, 128).transpose(3, 0, 2, 1).astype(BF16)


def relaid(weight):
    split = weight.reshape(512, 3, 3, 3, 128)[:, :, ::-1]
    return split.transpose(1, 3, 0, 2, 4).reshape(9, 512, 384)


def gather_chan(block):
    return [lax.ppermute(block, "chan", over_chan(step)) for step in (1, 2, 3)]


def scatter_chan(parts):
    return [parts[0]] + [
        lax.ppermute(parts[step], "chan", over_chan(step)) for step in (1, 2, 3)
    ]


def scatter_space(stage, parts):
    return [parts[0]] + [
        lax.ppermute(parts[step], "space", over(stage, step)) for step in (1, 2, 3)
    ]


def add_halo(own, inner, outer):
    first = lax.axis_index("space") % 2 == 0
    zero = jnp.where(first, outer, inner).astype(F32)
    one = jnp.where(first, inner, outer).astype(F32)
    return own + jnp.concatenate([zero, one], axis=0)


def body(inputs, weight_one, weight_two, cotangent):
    core = lax.axis_index("space") % 2
    x_own = cells_major(inputs)
    c_own = cells_major(cotangent)
    x_others = gather_chan(x_own)
    c_inner, c_outer = swap_halo(
        lax.dynamic_slice_in_dim(c_own, (1 - core) * 128, 128, 0),
        lax.dynamic_slice_in_dim(c_own, core * 128, 128, 0),
    )
    w_two = relaid(weight_two)
    w_one = relaid(weight_one)
    *hidden_parts, c_haloed = conv_t(c_own, c_inner, c_outer, w_two)
    hidden_parts = scatter_chan(hidden_parts)
    c_far = lax.ppermute(c_haloed, "space", CORES)

    pre, low, high, x_keep, x_send = conv(x_own, x_others, w_one)
    low, high = swap_halo(low, high)
    x_far = lax.ppermute(x_send, "space", CORES)
    hidden, grad, g_inner, g_outer = middle(pre, low, high, hidden_parts)

    g_inner, g_outer = swap_halo(g_inner, g_outer)
    h_others = gather_chan(hidden)
    *input_parts, g_haloed = conv_t(grad, g_inner, g_outer, w_one)
    input_parts = scatter_chan(input_parts)
    g_far = lax.ppermute(g_haloed, "space", CORES)
    one = scatter_space("x", wprod("x", x_keep, x_far, g_haloed, g_far))

    result, low, high, h_keep, h_send = conv(hidden, h_others, w_two)
    low, high = swap_halo(low, high)
    h_far = lax.ppermute(h_send, "space", CORES)
    two = scatter_space("z", wprod("z", h_keep, h_far, c_haloed, c_far))

    grad_one = last(scatter_space("z", second("z", one)))
    grad_two = last(scatter_space("x", second("x", two)))
    input_grad = sum(part.astype(F32) for part in input_parts)
    return (
        channels_major(add_halo(result, low, high)),
        channels_major(input_grad),
        grad_one,
        grad_two,
    )


def solution(mesh):
    placed = (
        P("chan", "space", None, None),
        P(None, None, "chan"),
        P(None, None, "chan"),
        P("chan", "space", None, None),
    )
    return jax.shard_map(
        body,
        mesh=mesh,
        in_specs=placed,
        out_specs=(
            P("chan", "space", None, None),
            P("chan", "space", None, None),
            P("space", None, "chan"),
            P("space", None, "chan"),
        ),
        check_vma=False,
    )
```

profile of v0, /device:TPU:0, one launch (start us, length us, event | category | flops | bytes accessed | tf_op | source)
XLA Modules:
  0.0 143.6 jit_solution(12061218629813765193)
XLA Ops:
  0.6 1.1 copy.26
  1.7 0.7 copy.43
  2.4 3.1 %collective-permute-start.2 = (bf16[256,256]{1,0:T(8,128)(2,1)}, bf16[256,256]{1,0:T(8,128)(2,1)}, u32[]{:S(2)}, u32[]{:S(2)}) collective-permute-start(bf16[256,256]{1,0:T(8,128)(2,1)} %bitcast.21.own), channel_id=1, source_target_pairs={{0,3},{1,2},{2,1},{3,0},{4,7},{5,6},{6,5},{7,4},{8,11},{9,10},{10,... | collective-permute-start | bytes 393224 | tf_op jit(solution)/shard_map/ppermute | solution.py:266
  5.5 0.6 collective-permute-start.1
  6.5 1.1 copy.29
  7.6 0.7 constant_dynamic-slice_fusion
  8.3 1.3 collective-permute-start.6
  9.6 2.4 %collective-permute-start.5 = (bf16[128,256]{1,0:T(8,128)(2,1)}, bf16[128,256]{1,0:T(8,128)(2,1)}, u32[]{:S(2)}, u32[]{:S(2)}) collective-permute-start(bf16[128,256]{1,0:T(8,128)(2,1)} %get-tuple-element.99), channel_id=1, source_target_pairs={{0,4},{4,0},{8,12},{12,8},{16,20},{20,16},{24,28},{28,24},{32,36},... | collective-permute-start | bytes 196616 | tf_op jit(solution)/shard_map/ppermute | solution.py:249
  12.0 4.3 %reverse_bitcast_fusion.1 = bf16[3,3,512,3,128]{4,2,1,3,0:T(8,128)(2,1)} fusion(bf16[512,3,3,3,128]{4,0,3,2,1:T(8,128)(2,1)} %bitcast.26), kind=kLoop, calls=%fused_computation.1 | loop fusion | bytes 7077888 | tf_op jit(solution)/shard_map/transpose | solution.py:262
  16.5 6.2 %copy.27 = bf16[3,3,512,3,128]{2,4,3,1,0:T(8,128)(2,1)} copy(bf16[3,3,512,3,128]{4,2,1,3,0:T(8,128)(2,1)} %reverse_bitcast_fusion.1) | data formatting | bytes 7077888 | tf_op jit(solution)/shard_map/transpose | solution.py:262
  22.6 5.7 %copy.28.weight = bf16[9,512,384]{2,1,0:T(8,128)(2,1)} copy(bf16[9,512,384]{1,2,0:T(8,128)(2,1)} %bitcast.24) | data formatting | bytes 7077888 | tf_op jit(solution)/shard_map/reshape | solution.py:262
  28.4 3.7 %copy.30 = bf16[3,3,512,3,128]{2,4,3,1,0:T(8,128)(2,1)} copy(bf16[3,3,512,3,128]{4,2,1,3,0:T(8,128)(2,1)S(1)} %reverse_bitcast_fusion) | data formatting | bytes 7077888 | tf_op jit(solution)/shard_map/transpose | solution.py:262
  32.1 4.4 %copy.31.weight = bf16[9,512,384]{2,1,0:T(8,128)(2,1)S(1)} copy(bf16[9,512,384]{1,2,0:T(8,128)(2,1)} %bitcast.25) | data formatting | bytes 7077888 | tf_op jit(solution)/shard_map/reshape | solution.py:262
  36.6 1.0 copy-done.4
  37.6 2.3 %shard_map.76 = (f32[256,256]{1,0:T(8,128)S(1)}, bf16[256,256]{1,0:T(8,128)(2,1)S(1)}, bf16[256,256]{1,0:T(8,128)(2,1)S(1)}, bf16[256,256]{1,0:T(8,128)(2,1)S(1)}, bf16[512,256]{1,0:T(8,128)(2,1)S(1)}) custom-call(bf16[256,256]{1,0:T(8,128)(2,1)S(1)} %bitcast.23, bf16[128,256]{1,0:T(8,128)(2,1)} %collective-permute-done.5.inner, ...), custom_call_target="tpu_custom_call" | custom-call | flops 1207959552 | bytes 4718592 | tf_op jit(solution)/shard_map/pallas_call | solution.py:19
  40.0 1.7 %collective-permute-start.7 = (bf16[256,256]{1,0:T(8,128)(2,1)S(1)}, bf16[256,256]{1,0:T(8,128)(2,1)S(1)}, u32[]{:S(2)}, u32[]{:S(2)}) collective-permute-start(bf16[256,256]{1,0:T(8,128)(2,1)S(1)} %get-tuple-element.48), channel_id=1, source_target_pairs={{0,1},{1,0},{2,3},{3,2},{4,5},{5,4},{6,7},{7,6},{8,9},{9,8},{10,11... | collective-permute-start | bytes 393224 | tf_op jit(solution)/shard_map/ppermute | solution.py:271
  41.6 2.9 %collective-permute-start.8 = (bf16[256,256]{1,0:T(8,128)(2,1)S(1)}, bf16[256,256]{1,0:T(8,128)(2,1)S(1)}, u32[]{:S(2)}, u32[]{:S(2)}) collective-permute-start(bf16[256,256]{1,0:T(8,128)(2,1)S(1)} %get-tuple-element.49), channel_id=1, source_target_pairs={{0,2},{1,3},{2,0},{3,1},{4,6},{5,7},{6,4},{7,5},{8,10},{9,11},{10,... | collective-permute-start | bytes 393224 | tf_op jit(solution)/shard_map/ppermute | solution.py:271
  44.7 2.6 %shard_map.75 = (f32[256,256]{1,0:T(8,128)S(1)}, bf16[128,256]{1,0:T(8,128)(2,1)S(1)}, bf16[128,256]{1,0:T(8,128)(2,1)S(1)}, bf16[256,512]{1,0:T(8,128)(2,1)S(1)}, bf16[256,512]{1,0:T(8,128)(2,1)S(1)}) custom-call(bf16[256,256]{1,0:T(8,128)(2,1)} %bitcast.21.own, bf16[256,256]{1,0:T(8,128)(2,1)} %collective-permute-done.r1, ...), custom_call_target="tpu_custom_call" | custom-call | flops 1207959552 | bytes 4980736 | tf_op jit(solution)/shard_map/pallas_call | solution.py:19
  47.5 0.7 collective-permute-start.4
  48.7 2.1 %collective-permute-done.8.g2 = bf16[256,256]{1,0:T(8,128)(2,1)S(1)} collective-permute-done((bf16[256,256]{1,0:T(8,128)(2,1)S(1)}, bf16[256,256]{1,0:T(8,128)(2,1)S(1)}, u32[]{:S(2)}, u32[]{:S(2)}) %collective-permute-start.8) | collective-permute-done | bytes 131104 | tf_op jit(solution)/shard_map/ppermute | solution.py:271
  50.8 2.2 %collective-permute-done.9.g3 = bf16[256,256]{1,0:T(8,128)(2,1)S(1)} collective-permute-done((bf16[256,256]{1,0:T(8,128)(2,1)S(1)}, bf16[256,256]{1,0:T(8,128)(2,1)S(1)}, u32[]{:S(2)}, u32[]{:S(2)}) %collective-permute-start.9) | collective-permute-done | bytes 131104 | tf_op jit(solution)/shard_map/ppermute | solution.py:271
  53.2 0.7 collective-permute-start.15
  53.9 0.7 collective-permute-start.16
  54.5 2.9 %collective-permute-start.20 = (bf16[256,512]{1,0:T(8,128)(2,1)S(1)}, bf16[256,512]{1,0:T(8,128)(2,1)S(1)}, u32[]{:S(2)}, u32[]{:S(2)}) collective-permute-start(bf16[256,512]{1,0:T(8,128)(2,1)S(1)} %get-tuple-element.63), channel_id=1, source_target_pairs={{0,4},{4,0},{8,12},{12,8},{16,20},{20,16},{24,28},{28,24},{32,36},... | collective-permute-start | bytes 786440 | tf_op jit(solution)/shard_map/ppermute | solution.py:305
  57.5 2.1 %shard_map.79 = (f32[256,256]{1,0:T(8,128)S(1)}, bf16[256,256]{1,0:T(8,128)(2,1)S(1)}, bf16[256,256]{1,0:T(8,128)(2,1)}, bf16[256,256]{1,0:T(8,128)(2,1)}, bf16[512,256]{1,0:T(8,128)(2,1)S(1)}) custom-call(bf16[256,256]{1,0:T(8,128)(2,1)S(1)} %get-tuple-element.55.own, bf16[128,256]{1,0:T(8,128)(2,1)S(1)} %collective-permute-done.15.inner, ...), custom_call_target="tpu_custom_call" | custom-call | flops 1207959552 | bytes 4718592 | tf_op jit(solution)/shard_map/pallas_call | solution.py:19
  59.6 2.0 %collective-permute-start.21 = (bf16[512,256]{1,0:T(8,128)(2,1)S(1)}, bf16[512,256]{1,0:T(8,128)(2,1)S(1)}, u32[]{:S(2)}, u32[]{:S(2)}) collective-permute-start(bf16[512,256]{1,0:T(8,128)(2,1)S(1)} %get-tuple-element.64.d_own), channel_id=1, source_target_pairs={{0,4},{4,0},{8,12},{12,8},{16,20},{20,16},{24,28},{28,24},{32,36},... | collective-permute-start | bytes 786440 | tf_op jit(solution)/shard_map/ppermute | solution.py:312
  61.6 3.0 %collective-permute-start.12 = (bf16[256,256]{1,0:T(8,128)(2,1)S(1)}, bf16[256,256]{1,0:T(8,128)(2,1)S(1)}, u32[]{:S(2)}, u32[]{:S(2)}) collective-permute-start(bf16[256,256]{1,0:T(8,128)(2,1)S(1)} %get-tuple-element.51.own), channel_id=1, source_target_pairs={{0,3},{1,2},{2,1},{3,0},{4,7},{5,6},{6,5},{7,4},{8,11},{9,10},{10,... | collective-permute-start | bytes 393224 | tf_op jit(solution)/shard_map/ppermute | solution.py:266
  64.6 1.1 collective-permute-start.10
  65.7 2.6 %shard_map.80 = (f32[9,64,384]{2,1,0:T(8,128)S(1)}, bf16[9,64,384]{2,1,0:T(8,128)(2,1)}, bf16[9,64,384]{2,1,0:T(8,128)(2,1)}, bf16[9,64,384]{2,1,0:T(8,128)(2,1)}) custom-call(bf16[256,512]{1,0:T(8,128)(2,1)S(1)} %get-tuple-element.62.v_own, bf16[256,512]{1,0:T(8,128)(2,1)S(1)} %collective-permute-done.20.v_far, ...), custom_call_target="tpu_custom_call" | custom-call | flops 1207959552 | bytes 3260416 | tf_op jit(solution)/shard_map/pallas_call | solution.py:19
  68.3 1.6 %collective-permute-start.22 = (bf16[9,64,384]{2,1,0:T(8,128)(2,1)}, bf16[9,64,384]{2,1,0:T(8,128)(2,1)}, u32[]{:S(2)}, u32[]{:S(2)}) collective-permute-start(bf16[9,64,384]{2,1,0:T(8,128)(2,1)} %get-tuple-element.66), channel_id=1, source_target_pairs={{0,8},{4,12},{8,0},{12,4},{16,24},{20,28},{24,16},{28,20},{32,40},... | collective-permute-start | bytes 1327112 | tf_op jit(solution)/shard_map/ppermute | solution.py:277
  70.4 6.7 %collective-permute-start.23 = (bf16[9,64,384]{2,1,0:T(8,128)(2,1)}, bf16[9,64,384]{2,1,0:T(8,128)(2,1)}, u32[]{:S(2)}, u32[]{:S(2)}) collective-permute-start(bf16[9,64,384]{2,1,0:T(8,128)(2,1)} %get-tuple-element.67), channel_id=1, source_target_pairs={{0,16},{4,20},{8,24},{12,28},{16,0},{20,4},{24,8},{28,12},{32,48},... | collective-permute-start | bytes 1327112 | tf_op jit(solution)/shard_map/ppermute | solution.py:277
  77.1 2.8 %collective-permute-start.24 = (bf16[9,64,384]{2,1,0:T(8,128)(2,1)}, bf16[9,64,384]{2,1,0:T(8,128)(2,1)}, u32[]{:S(2)}, u32[]{:S(2)}) collective-permute-start(bf16[9,64,384]{2,1,0:T(8,128)(2,1)} %get-tuple-element.68), channel_id=1, source_target_pairs={{0,24},{4,28},{8,16},{12,20},{16,8},{20,12},{24,0},{28,4},{32,56},... | collective-permute-start | bytes 1327112 | tf_op jit(solution)/shard_map/ppermute | solution.py:277
  79.8 2.2 %shard_map.78 = (f32[256,256]{1,0:T(8,128)S(1)}, bf16[128,256]{1,0:T(8,128)(2,1)S(1)}, bf16[128,256]{1,0:T(8,128)(2,1)}, bf16[256,512]{1,0:T(8,128)(2,1)S(1)}, bf16[256,512]{1,0:T(8,128)(2,1)S(1)}) custom-call(bf16[256,256]{1,0:T(8,128)(2,1)S(1)} %get-tuple-element.51.own, bf16[256,256]{1,0:T(8,128)(2,1)S(1)} %collective-permute-done.10.r1, ...), custom_call_target="tpu_custom_call" | custom-call | flops 1207959552 | bytes 4980736 | tf_op jit(solution)/shard_map/pallas_call | solution.py:19
  82.0 0.7 copy-done.7
  82.7 0.6 copy-done.12
  83.4 0.7 copy-done.14
  84.1 0.7 copy-done.10
  84.8 5.9 %collective-permute-done.17 = bf16[256,256]{1,0:T(8,128)(2,1)S(1)} collective-permute-done((bf16[256,256]{1,0:T(8,128)(2,1)S(1)}, bf16[256,256]{1,0:T(8,128)(2,1)S(1)}, u32[]{:S(2)}, u32[]{:S(2)}) %collective-permute-start.17) | collective-permute-done | bytes 131104 | tf_op jit(solution)/shard_map/ppermute | solution.py:271
  90.7 1.2 collective-permute-start.18
  91.9 1.7 %collective-permute-start.19 = (bf16[256,256]{1,0:T(8,128)(2,1)}, bf16[256,256]{1,0:T(8,128)(2,1)S(1)}, u32[]{:S(2)}, u32[]{:S(2)}) collective-permute-start(bf16[256,256]{1,0:T(8,128)(2,1)} %get-tuple-element.61), channel_id=1, source_target_pairs={{0,3},{1,2},{2,1},{3,0},{4,7},{5,6},{6,5},{7,4},{8,11},{9,10},{10,... | collective-permute-start | bytes 393224 | tf_op jit(solution)/shard_map/ppermute | solution.py:271
  93.6 0.9 copy-done.9
  94.6 0.9 copy-done.11
  95.5 0.9 copy-done.15
  96.5 2.6 %shard_map.83 = (f32[9,64,384]{2,1,0:T(8,128)S(1)}, bf16[9,64,384]{2,1,0:T(8,128)(2,1)}, bf16[9,64,384]{2,1,0:T(8,128)(2,1)}, bf16[9,64,384]{2,1,0:T(8,128)(2,1)}) custom-call(bf16[256,512]{1,0:T(8,128)(2,1)S(1)} %copy-done.15, bf16[256,512]{1,0:T(8,128)(2,1)S(1)} %collective-permute-done.28.v_far, bf16[512,256]{1,0:T(8,128)(2,1)S(1)} %copy-done.9, ...), custom_call_target="tpu_custom_call" | custom-call | flops 1207959552 | bytes 3260416 | tf_op jit(solution)/shard_map/pallas_call | solution.py:19
  99.1 1.3 collective-permute-start.13
  100.4 0.9 collective-permute-start.14
  101.3 1.9 %collective-permute-start.30 = (bf16[9,64,384]{2,1,0:T(8,128)(2,1)}, bf16[9,64,384]{2,1,0:T(8,128)(2,1)S(1)}, u32[]{:S(2)}, u32[]{:S(2)}) collective-permute-start(bf16[9,64,384]{2,1,0:T(8,128)(2,1)} %get-tuple-element.77), channel_id=1, source_target_pairs={{0,32},{4,36},{8,40},{12,44},{16,48},{20,52},{24,56},{28,60},{32,0... | collective-permute-start | bytes 1327112 | tf_op jit(solution)/shard_map/ppermute | solution.py:277
  103.3 3.4 %collective-permute-start.31 = (bf16[9,64,384]{2,1,0:T(8,128)(2,1)}, bf16[9,64,384]{2,1,0:T(8,128)(2,1)S(1)}, u32[]{:S(2)}, u32[]{:S(2)}) collective-permute-start(bf16[9,64,384]{2,1,0:T(8,128)(2,1)} %get-tuple-element.78), channel_id=1, source_target_pairs={{0,64},{4,68},{8,72},{12,76},{16,80},{20,84},{24,88},{28,92},{32,9... | collective-permute-start | bytes 1327112 | tf_op jit(solution)/shard_map/ppermute | solution.py:277
  106.7 1.7 %add_convert_fusion = bf16[256,256]{1,0:T(8,128)(2,1)} fusion(bf16[256,256]{1,0:T(8,128)(2,1)} %copy-done.20, bf16[256,256]{1,0:T(8,128)(2,1)} %copy-done.19, f32[256,256]{1,0:T(8,128)S(1)} %copy-done.6, bf16[256,256]{1,0:T(8,128)(2,1)S(1)} %copy-done.18), kind=kLoop, calls=%fused_computation.2 | loop fusion | flops 458752 | bytes 786432 | tf_op jit(solution)/shard_map/convert_element_type | solution.py:257
  108.3 0.9 convert_element_type.36
  109.3 0.8 copy.35
  110.1 2.3 %shard_map.81 = (f32[9,16,384]{2,1,0:T(8,128)S(1)}, bf16[9,16,384]{2,1,0:T(8,128)(2,1)S(1)}, bf16[9,16,384]{2,1,0:T(8,128)(2,1)}, bf16[9,16,384]{2,1,0:T(8,128)(2,1)S(1)}) custom-call(f32[9,64,384]{2,1,0:T(8,128)S(1)} %copy-done.2, bf16[9,64,384]{2,1,0:T(8,128)(2,1)} %collective-permute-done.22.r1, bf16[9,64,384]{2,1,0:T(8,128)(2,1)} %collective-permute-done.23.r2, ...), custom_call_target="tpu_custom_call" | custom-call | bytes 2764800 | tf_op jit(solution)/shard_map/pallas_call | solution.py:19
  112.5 0.9 broadcast_select_fusion.1
  113.3 4.7 %collective-permute-start.26 = (bf16[9,16,384]{2,1,0:T(8,128)(2,1)}, bf16[9,16,384]{2,1,0:T(8,128)(2,1)S(1)}, u32[]{:S(2)}, u32[]{:S(2)}) collective-permute-start(bf16[9,16,384]{2,1,0:T(8,128)(2,1)} %get-tuple-element.71), channel_id=1, source_target_pairs={{0,64},{4,68},{8,72},{12,76},{16,80},{20,84},{24,88},{28,92},{32,9... | collective-permute-start | bytes 331784 | tf_op jit(solution)/shard_map/ppermute | solution.py:277
  118.4 9.0 %collective-permute-done.31.r2 = bf16[9,64,384]{2,1,0:T(8,128)(2,1)S(1)} collective-permute-done((bf16[9,64,384]{2,1,0:T(8,128)(2,1)}, bf16[9,64,384]{2,1,0:T(8,128)(2,1)S(1)}, u32[]{:S(2)}, u32[]{:S(2)}) %collective-permute-start.31) | collective-permute-done | bytes 442400 | tf_op jit(solution)/shard_map/ppermute | solution.py:277
  127.4 5.6 %collective-permute-done.32.r3 = bf16[9,64,384]{2,1,0:T(8,128)(2,1)S(1)} collective-permute-done((bf16[9,64,384]{2,1,0:T(8,128)(2,1)}, bf16[9,64,384]{2,1,0:T(8,128)(2,1)S(1)}, u32[]{:S(2)}, u32[]{:S(2)}) %collective-permute-start.32) | collective-permute-done | bytes 442400 | tf_op jit(solution)/shard_map/ppermute | solution.py:277
  133.0 1.1 shard_map.84
  134.4 2.0 %collective-permute-start.34 = (bf16[9,16,384]{2,1,0:T(8,128)(2,1)}, bf16[9,16,384]{2,1,0:T(8,128)(2,1)S(1)}, u32[]{:S(2)}, u32[]{:S(2)}) collective-permute-start(bf16[9,16,384]{2,1,0:T(8,128)(2,1)} %get-tuple-element.82), channel_id=1, source_target_pairs={{0,16},{4,20},{8,24},{12,28},{16,0},{20,4},{24,8},{28,12},{32,48},... | collective-permute-start | bytes 331784 | tf_op jit(solution)/shard_map/ppermute | solution.py:277
  136.4 2.3 %collective-permute-start.35 = (bf16[9,16,384]{2,1,0:T(8,128)(2,1)}, bf16[9,16,384]{2,1,0:T(8,128)(2,1)S(1)}, u32[]{:S(2)}, u32[]{:S(2)}) collective-permute-start(bf16[9,16,384]{2,1,0:T(8,128)(2,1)} %get-tuple-element.83), channel_id=1, source_target_pairs={{0,24},{4,28},{8,16},{12,20},{16,8},{20,12},{24,0},{28,4},{32,56},... | collective-permute-start | bytes 331784 | tf_op jit(solution)/shard_map/ppermute | solution.py:277
  138.8 1.0 add_convert_fusion.1
  139.8 0.8 copy.33
  140.8 0.8 copy.36
  141.6 1.0 collective-permute-done.35.r3
  142.8 0.8 copy.37
  (81 shorter events, 3.6 us)
Async XLA Ops:
  2.4 42.1 %collective-permute-start.2 = (bf16[256,256]{1,0:T(8,128)(2,1)}, bf16[256,256]{1,0:T(8,128)(2,1)}, u32[]{:S(2)}, u32[]{:S(2)}) collective-permute-start(bf16[256,256]{1,0:T(8,128)(2,1)} %bitcast.21.own), channel_id=1, source_target_pairs={{0,3},{1,2},{2,1},{3,0},{4,7},{5,6},{6,5},{7,4},{8,11},{9,10},{10,... | collective-permute-start | bytes 393224 | tf_op jit(solution)/shard_map/ppermute | solution.py:266
  5.5 39.3 %collective-permute-start.1 = (bf16[256,256]{1,0:T(8,128)(2,1)}, bf16[256,256]{1,0:T(8,128)(2,1)}, u32[]{:S(2)}, u32[]{:S(2)}) collective-permute-start(bf16[256,256]{1,0:T(8,128)(2,1)} %bitcast.21.own), channel_id=1, source_target_pairs={{0,2},{1,3},{2,0},{3,1},{4,6},{5,7},{6,4},{7,5},{8,10},{9,11},{10,... | collective-permute-start | bytes 393224 | tf_op jit(solution)/shard_map/ppermute | solution.py:266
  6.1 38.6 %collective-permute-start = (bf16[256,256]{1,0:T(8,128)(2,1)}, bf16[256,256]{1,0:T(8,128)(2,1)}, u32[]{:S(2)}, u32[]{:S(2)}) collective-permute-start(bf16[256,256]{1,0:T(8,128)(2,1)} %bitcast.21.own), channel_id=1, source_target_pairs={{0,1},{1,0},{2,3},{3,2},{4,5},{5,4},{6,7},{7,6},{8,9},{9,8},{10,11... | collective-permute-start | bytes 393224 | tf_op jit(solution)/shard_map/ppermute | solution.py:266
  7.6 8.6 %copy-start.3 = (bf16[32,8,2,128]{3,1,2,0:T(8,128)(2,1)}, bf16[32,8,2,128]{3,1,2,0:T(8,128)(2,1)S(1)}, u32[]{:S(2)}) copy-start(bf16[32,8,2,128]{3,1,2,0:T(8,128)(2,1)S(1)} %copy.42) | copy-start | bytes 393220
  8.3 28.2 %collective-permute-start.6 = (bf16[128,256]{1,0:T(8,128)(2,1)}, bf16[128,256]{1,0:T(8,128)(2,1)}, u32[]{:S(2)}, u32[]{:S(2)}) collective-permute-start(bf16[128,256]{1,0:T(8,128)(2,1)} %get-tuple-element.98), channel_id=1, source_target_pairs={{4,8},{8,4},{12,16},{16,12},{20,24},{24,20},{28,32},{32,28},{36,40... | collective-permute-start | bytes 196616 | tf_op jit(solution)/shard_map/ppermute | solution.py:249
  9.6 27.0 %collective-permute-start.5 = (bf16[128,256]{1,0:T(8,128)(2,1)}, bf16[128,256]{1,0:T(8,128)(2,1)}, u32[]{:S(2)}, u32[]{:S(2)}) collective-permute-start(bf16[128,256]{1,0:T(8,128)(2,1)} %get-tuple-element.99), channel_id=1, source_target_pairs={{0,4},{4,0},{8,12},{12,8},{16,20},{20,16},{24,28},{28,24},{32,36},... | collective-permute-start | bytes 196616 | tf_op jit(solution)/shard_map/ppermute | solution.py:249
  12.0 4.3 %copy-start.16 = (bf16[512,27,128]{2,0,1:T(8,128)(2,1)S(1)}, bf16[512,27,128]{2,0,1:T(8,128)(2,1)}, u32[]{:S(2)}) copy-start(bf16[512,27,128]{2,0,1:T(8,128)(2,1)} %param.6) | copy-start | bytes 10616836
  36.5 8.2 %copy-start = (bf16[9,512,384]{2,1,0:T(8,128)(2,1)S(1)}, bf16[9,512,384]{2,1,0:T(8,128)(2,1)}, u32[]{:S(2)}) copy-start(bf16[9,512,384]{2,1,0:T(8,128)(2,1)} %copy.28.weight) | copy-start | bytes 10616836
  36.5 1.1 copy-start.4
  39.9 25.8 %copy-start.8 = (bf16[512,256]{1,0:T(8,128)(2,1)}, bf16[512,256]{1,0:T(8,128)(2,1)S(1)}, u32[]{:S(2)}) copy-start(bf16[512,256]{1,0:T(8,128)(2,1)S(1)} %get-tuple-element.75.d_own) | copy-start | bytes 786436
  40.0 8.8 %collective-permute-start.7 = (bf16[256,256]{1,0:T(8,128)(2,1)S(1)}, bf16[256,256]{1,0:T(8,128)(2,1)S(1)}, u32[]{:S(2)}, u32[]{:S(2)}) collective-permute-start(bf16[256,256]{1,0:T(8,128)(2,1)S(1)} %get-tuple-element.48), channel_id=1, source_target_pairs={{0,1},{1,0},{2,3},{3,2},{4,5},{5,4},{6,7},{7,6},{8,9},{9,8},{10,11... | collective-permute-start | bytes 393224 | tf_op jit(solution)/shard_map/ppermute | solution.py:271
  41.6 9.2 %collective-permute-start.8 = (bf16[256,256]{1,0:T(8,128)(2,1)S(1)}, bf16[256,256]{1,0:T(8,128)(2,1)S(1)}, u32[]{:S(2)}, u32[]{:S(2)}) collective-permute-start(bf16[256,256]{1,0:T(8,128)(2,1)S(1)} %get-tuple-element.49), channel_id=1, source_target_pairs={{0,2},{1,3},{2,0},{3,1},{4,6},{5,7},{6,4},{7,5},{8,10},{9,11},{10,... | collective-permute-start | bytes 393224 | tf_op jit(solution)/shard_map/ppermute | solution.py:271
  44.5 8.5 %collective-permute-start.9 = (bf16[256,256]{1,0:T(8,128)(2,1)S(1)}, bf16[256,256]{1,0:T(8,128)(2,1)S(1)}, u32[]{:S(2)}, u32[]{:S(2)}) collective-permute-start(bf16[256,256]{1,0:T(8,128)(2,1)S(1)} %get-tuple-element.50), channel_id=1, source_target_pairs={{0,3},{1,2},{2,1},{3,0},{4,7},{5,6},{6,5},{7,4},{8,11},{9,10},{10,... | collective-permute-start | bytes 393224 | tf_op jit(solution)/shard_map/ppermute | solution.py:271
  47.4 1.3 collective-permute-start.3
  47.5 1.2 collective-permute-start.4
  53.2 4.3 %collective-permute-start.15 = (bf16[128,256]{1,0:T(8,128)(2,1)S(1)}, bf16[128,256]{1,0:T(8,128)(2,1)S(1)}, u32[]{:S(2)}, u32[]{:S(2)}) collective-permute-start(bf16[128,256]{1,0:T(8,128)(2,1)S(1)} %get-tuple-element.56), channel_id=1, source_target_pairs={{0,4},{4,0},{8,12},{12,8},{16,20},{20,16},{24,28},{28,24},{32,36},... | collective-permute-start | bytes 196616 | tf_op jit(solution)/shard_map/ppermute | solution.py:249
  53.9 3.6 %collective-permute-start.16 = (bf16[128,256]{1,0:T(8,128)(2,1)S(1)}, bf16[128,256]{1,0:T(8,128)(2,1)S(1)}, u32[]{:S(2)}, u32[]{:S(2)}) collective-permute-start(bf16[128,256]{1,0:T(8,128)(2,1)S(1)} %get-tuple-element.57), channel_id=1, source_target_pairs={{4,8},{8,4},{12,16},{16,12},{20,24},{24,20},{28,32},{32,28},{36,40... | collective-permute-start | bytes 196616 | tf_op jit(solution)/shard_map/ppermute | solution.py:249
  54.5 11.2 %collective-permute-start.20 = (bf16[256,512]{1,0:T(8,128)(2,1)S(1)}, bf16[256,512]{1,0:T(8,128)(2,1)S(1)}, u32[]{:S(2)}, u32[]{:S(2)}) collective-permute-start(bf16[256,512]{1,0:T(8,128)(2,1)S(1)} %get-tuple-element.63), channel_id=1, source_target_pairs={{0,4},{4,0},{8,12},{12,8},{16,20},{20,16},{24,28},{28,24},{32,36},... | collective-permute-start | bytes 786440 | tf_op jit(solution)/shard_map/ppermute | solution.py:305
  59.6 22.4 %copy-start.5 = (f32[256,256]{1,0:T(8,128)}, f32[256,256]{1,0:T(8,128)S(1)}, u32[]{:S(2)}) copy-start(f32[256,256]{1,0:T(8,128)S(1)} %get-tuple-element.58) | copy-start | bytes 786436
  59.6 6.1 %collective-permute-start.21 = (bf16[512,256]{1,0:T(8,128)(2,1)S(1)}, bf16[512,256]{1,0:T(8,128)(2,1)S(1)}, u32[]{:S(2)}, u32[]{:S(2)}) collective-permute-start(bf16[512,256]{1,0:T(8,128)(2,1)S(1)} %get-tuple-element.64.d_own), channel_id=1, source_target_pairs={{0,4},{4,0},{8,12},{12,8},{16,20},{20,16},{24,28},{28,24},{32,36},... | collective-permute-start | bytes 786440 | tf_op jit(solution)/shard_map/ppermute | solution.py:312
  61.6 8.8 %collective-permute-start.12 = (bf16[256,256]{1,0:T(8,128)(2,1)S(1)}, bf16[256,256]{1,0:T(8,128)(2,1)S(1)}, u32[]{:S(2)}, u32[]{:S(2)}) collective-permute-start(bf16[256,256]{1,0:T(8,128)(2,1)S(1)} %get-tuple-element.51.own), channel_id=1, source_target_pairs={{0,3},{1,2},{2,1},{3,0},{4,7},{5,6},{6,5},{7,4},{8,11},{9,10},{10,... | collective-permute-start | bytes 393224 | tf_op jit(solution)/shard_map/ppermute | solution.py:266
  64.6 12.5 %collective-permute-start.11 = (bf16[256,256]{1,0:T(8,128)(2,1)S(1)}, bf16[256,256]{1,0:T(8,128)(2,1)S(1)}, u32[]{:S(2)}, u32[]{:S(2)}) collective-permute-start(bf16[256,256]{1,0:T(8,128)(2,1)S(1)} %get-tuple-element.51.own), channel_id=1, source_target_pairs={{0,2},{1,3},{2,0},{3,1},{4,6},{5,7},{6,4},{7,5},{8,10},{9,11},{10,... | collective-permute-start | bytes 393224 | tf_op jit(solution)/shard_map/ppermute | solution.py:266
  64.6 15.2 %collective-permute-start.10 = (bf16[256,256]{1,0:T(8,128)(2,1)S(1)}, bf16[256,256]{1,0:T(8,128)(2,1)S(1)}, u32[]{:S(2)}, u32[]{:S(2)}) collective-permute-start(bf16[256,256]{1,0:T(8,128)(2,1)S(1)} %get-tuple-element.51.own), channel_id=1, source_target_pairs={{0,1},{1,0},{2,3},{3,2},{4,5},{5,4},{6,7},{7,6},{8,9},{9,8},{10,11... | collective-permute-start | bytes 393224 | tf_op jit(solution)/shard_map/ppermute | solution.py:266
  65.7 18.4 %collective-permute-start.29 = (bf16[512,256]{1,0:T(8,128)(2,1)S(1)}, bf16[512,256]{1,0:T(8,128)(2,1)S(1)}, u32[]{:S(2)}, u32[]{:S(2)}) collective-permute-start(bf16[512,256]{1,0:T(8,128)(2,1)S(1)} %get-tuple-element.75.d_own), channel_id=1, source_target_pairs={{0,4},{4,0},{8,12},{12,8},{16,20},{20,16},{24,28},{28,24},{32,36},... | collective-permute-start | bytes 786440 | tf_op jit(solution)/shard_map/ppermute | solution.py:301
  68.3 13.7 %copy-start.1 = (f32[9,64,384]{2,1,0:T(8,128)}, f32[9,64,384]{2,1,0:T(8,128)S(1)}, u32[]{:S(2)}) copy-start(f32[9,64,384]{2,1,0:T(8,128)S(1)} %get-tuple-element.65.own) | copy-start | bytes 2654212
  68.3 33.0 %collective-permute-start.22 = (bf16[9,64,384]{2,1,0:T(8,128)(2,1)}, bf16[9,64,384]{2,1,0:T(8,128)(2,1)}, u32[]{:S(2)}, u32[]{:S(2)}) collective-permute-start(bf16[9,64,384]{2,1,0:T(8,128)(2,1)} %get-tuple-element.66), channel_id=1, source_target_pairs={{0,8},{4,12},{8,0},{12,4},{16,24},{20,28},{24,16},{28,20},{32,40},... | collective-permute-start | bytes 1327112 | tf_op jit(solution)/shard_map/ppermute | solution.py:277
  70.4 32.9 %collective-permute-start.23 = (bf16[9,64,384]{2,1,0:T(8,128)(2,1)}, bf16[9,64,384]{2,1,0:T(8,128)(2,1)}, u32[]{:S(2)}, u32[]{:S(2)}) collective-permute-start(bf16[9,64,384]{2,1,0:T(8,128)(2,1)} %get-tuple-element.67), channel_id=1, source_target_pairs={{0,16},{4,20},{8,24},{12,28},{16,0},{20,4},{24,8},{28,12},{32,48},... | collective-permute-start | bytes 1327112 | tf_op jit(solution)/shard_map/ppermute | solution.py:277
  77.1 29.6 %collective-permute-start.24 = (bf16[9,64,384]{2,1,0:T(8,128)(2,1)}, bf16[9,64,384]{2,1,0:T(8,128)(2,1)}, u32[]{:S(2)}, u32[]{:S(2)}) collective-permute-start(bf16[9,64,384]{2,1,0:T(8,128)(2,1)} %get-tuple-element.68), channel_id=1, source_target_pairs={{0,24},{4,28},{8,16},{12,20},{16,8},{20,12},{24,0},{28,4},{32,56},... | collective-permute-start | bytes 1327112 | tf_op jit(solution)/shard_map/ppermute | solution.py:277
  82.0 0.7 copy-start.7
  82.7 0.6 copy-start.12
  83.3 0.7 copy-start.14
  84.1 22.6 %copy-start.6 = (f32[256,256]{1,0:T(8,128)S(1)}, f32[256,256]{1,0:T(8,128)}, u32[]{:S(2)}) copy-start(f32[256,256]{1,0:T(8,128)} %copy-done.5) | copy-start | bytes 786436
  84.1 26.0 %copy-start.2 = (f32[9,64,384]{2,1,0:T(8,128)S(1)}, f32[9,64,384]{2,1,0:T(8,128)}, u32[]{:S(2)}) copy-start(f32[9,64,384]{2,1,0:T(8,128)} %copy-done.1) | copy-start | bytes 2654212
  84.1 7.9 %collective-permute-start.28 = (bf16[256,512]{1,0:T(8,128)(2,1)S(1)}, bf16[256,512]{1,0:T(8,128)(2,1)S(1)}, u32[]{:S(2)}, u32[]{:S(2)}) collective-permute-start(bf16[256,512]{1,0:T(8,128)(2,1)S(1)} %get-tuple-element.74), channel_id=1, source_target_pairs={{0,4},{4,0},{8,12},{12,8},{16,20},{20,16},{24,28},{28,24},{32,36},... | collective-permute-start | bytes 786440 | tf_op jit(solution)/shard_map/ppermute | solution.py:317
  84.1 0.7 copy-start.10
  84.8 5.9 %collective-permute-start.17 = (bf16[256,256]{1,0:T(8,128)(2,1)S(1)}, bf16[256,256]{1,0:T(8,128)(2,1)S(1)}, u32[]{:S(2)}, u32[]{:S(2)}) collective-permute-start(bf16[256,256]{1,0:T(8,128)(2,1)S(1)} %get-tuple-element.59), channel_id=1, source_target_pairs={{0,1},{1,0},{2,3},{3,2},{4,5},{5,4},{6,7},{7,6},{8,9},{9,8},{10,11... | collective-permute-start | bytes 393224 | tf_op jit(solution)/shard_map/ppermute | solution.py:271
  90.7 1.2 copy-start.17
  90.7 8.4 %collective-permute-start.18 = (bf16[256,256]{1,0:T(8,128)(2,1)}, bf16[256,256]{1,0:T(8,128)(2,1)S(1)}, u32[]{:S(2)}, u32[]{:S(2)}) collective-permute-start(bf16[256,256]{1,0:T(8,128)(2,1)} %get-tuple-element.60), channel_id=1, source_target_pairs={{0,2},{1,3},{2,0},{3,1},{4,6},{5,7},{6,4},{7,5},{8,10},{9,11},{10,... | collective-permute-start | bytes 393224 | tf_op jit(solution)/shard_map/ppermute | solution.py:271
  91.9 8.5 %collective-permute-start.19 = (bf16[256,256]{1,0:T(8,128)(2,1)}, bf16[256,256]{1,0:T(8,128)(2,1)S(1)}, u32[]{:S(2)}, u32[]{:S(2)}) collective-permute-start(bf16[256,256]{1,0:T(8,128)(2,1)} %get-tuple-element.61), channel_id=1, source_target_pairs={{0,3},{1,2},{2,1},{3,0},{4,7},{5,6},{6,5},{7,4},{8,11},{9,10},{10,... | collective-permute-start | bytes 393224 | tf_op jit(solution)/shard_map/ppermute | solution.py:271
  93.6 0.9 copy-start.9
  94.6 0.9 copy-start.11
  95.5 0.9 copy-start.15
  96.5 3.9 %copy-start.13 = (bf16[128,256]{1,0:T(8,128)(2,1)S(1)}, bf16[128,256]{1,0:T(8,128)(2,1)}, u32[]{:S(2)}) copy-start(bf16[128,256]{1,0:T(8,128)(2,1)} %copy-done.12) | copy-start | bytes 196612
  96.5 10.2 %copy-start.18 = (bf16[256,256]{1,0:T(8,128)(2,1)S(1)}, bf16[256,256]{1,0:T(8,128)(2,1)}, u32[]{:S(2)}) copy-start(bf16[256,256]{1,0:T(8,128)(2,1)} %copy-done.17) | copy-start | bytes 393220
  99.1 2.2 %copy-start.19 = (bf16[256,256]{1,0:T(8,128)(2,1)}, bf16[256,256]{1,0:T(8,128)(2,1)S(1)}, u32[]{:S(2)}) copy-start(bf16[256,256]{1,0:T(8,128)(2,1)S(1)} %collective-permute-done.18) | copy-start | bytes 393220
  99.1 13.2 %collective-permute-start.13 = (bf16[128,256]{1,0:T(8,128)(2,1)}, bf16[128,256]{1,0:T(8,128)(2,1)}, u32[]{:S(2)}, u32[]{:S(2)}) collective-permute-start(bf16[128,256]{1,0:T(8,128)(2,1)} %get-tuple-element.53), channel_id=1, source_target_pairs={{4,8},{8,4},{12,16},{16,12},{20,24},{24,20},{28,32},{32,28},{36,40... | collective-permute-start | bytes 196616 | tf_op jit(solution)/shard_map/ppermute | solution.py:249
  100.4 2.8 %copy-start.20 = (bf16[256,256]{1,0:T(8,128)(2,1)}, bf16[256,256]{1,0:T(8,128)(2,1)S(1)}, u32[]{:S(2)}) copy-start(bf16[256,256]{1,0:T(8,128)(2,1)S(1)} %collective-permute-done.19) | copy-start | bytes 393220
  100.4 12.0 %collective-permute-start.14 = (bf16[128,256]{1,0:T(8,128)(2,1)S(1)}, bf16[128,256]{1,0:T(8,128)(2,1)}, u32[]{:S(2)}, u32[]{:S(2)}) collective-permute-start(bf16[128,256]{1,0:T(8,128)(2,1)S(1)} %copy-done.13), channel_id=1, source_target_pairs={{0,4},{4,0},{8,12},{12,8},{16,20},{20,16},{24,28},{28,24},{32,36},... | collective-permute-start | bytes 196616 | tf_op jit(solution)/shard_map/ppermute | solution.py:249
  101.3 16.7 %collective-permute-start.30 = (bf16[9,64,384]{2,1,0:T(8,128)(2,1)}, bf16[9,64,384]{2,1,0:T(8,128)(2,1)S(1)}, u32[]{:S(2)}, u32[]{:S(2)}) collective-permute-start(bf16[9,64,384]{2,1,0:T(8,128)(2,1)} %get-tuple-element.77), channel_id=1, source_target_pairs={{0,32},{4,36},{8,40},{12,44},{16,48},{20,52},{24,56},{28,60},{32,0... | collective-permute-start | bytes 1327112 | tf_op jit(solution)/shard_map/ppermute | solution.py:277
  103.3 24.1 %collective-permute-start.31 = (bf16[9,64,384]{2,1,0:T(8,128)(2,1)}, bf16[9,64,384]{2,1,0:T(8,128)(2,1)S(1)}, u32[]{:S(2)}, u32[]{:S(2)}) collective-permute-start(bf16[9,64,384]{2,1,0:T(8,128)(2,1)} %get-tuple-element.78), channel_id=1, source_target_pairs={{0,64},{4,68},{8,72},{12,76},{16,80},{20,84},{24,88},{28,92},{32,9... | collective-permute-start | bytes 1327112 | tf_op jit(solution)/shard_map/ppermute | solution.py:277
  106.6 26.3 %collective-permute-start.32 = (bf16[9,64,384]{2,1,0:T(8,128)(2,1)}, bf16[9,64,384]{2,1,0:T(8,128)(2,1)S(1)}, u32[]{:S(2)}, u32[]{:S(2)}) collective-permute-start(bf16[9,64,384]{2,1,0:T(8,128)(2,1)} %get-tuple-element.79), channel_id=1, source_target_pairs={{0,96},{4,100},{8,104},{12,108},{16,112},{20,116},{24,120},{28,124... | collective-permute-start | bytes 1327112 | tf_op jit(solution)/shard_map/ppermute | solution.py:277
  112.4 24.1 %collective-permute-start.25 = (bf16[9,16,384]{2,1,0:T(8,128)(2,1)S(1)}, bf16[9,16,384]{2,1,0:T(8,128)(2,1)S(1)}, u32[]{:S(2)}, u32[]{:S(2)}) collective-permute-start(bf16[9,16,384]{2,1,0:T(8,128)(2,1)S(1)} %get-tuple-element.70), channel_id=1, source_target_pairs={{0,32},{4,36},{8,40},{12,44},{16,48},{20,52},{24,56},{28,60},{32,0... | collective-permute-start | bytes 331784 | tf_op jit(solution)/shard_map/ppermute | solution.py:277
  113.3 27.2 %collective-permute-start.26 = (bf16[9,16,384]{2,1,0:T(8,128)(2,1)}, bf16[9,16,384]{2,1,0:T(8,128)(2,1)S(1)}, u32[]{:S(2)}, u32[]{:S(2)}) collective-permute-start(bf16[9,16,384]{2,1,0:T(8,128)(2,1)} %get-tuple-element.71), channel_id=1, source_target_pairs={{0,64},{4,68},{8,72},{12,76},{16,80},{20,84},{24,88},{28,92},{32,9... | collective-permute-start | bytes 331784 | tf_op jit(solution)/shard_map/ppermute | solution.py:277
  118.0 22.6 %collective-permute-start.27 = (bf16[9,16,384]{2,1,0:T(8,128)(2,1)S(1)}, bf16[9,16,384]{2,1,0:T(8,128)(2,1)S(1)}, u32[]{:S(2)}, u32[]{:S(2)}) collective-permute-start(bf16[9,16,384]{2,1,0:T(8,128)(2,1)S(1)} %get-tuple-element.72), channel_id=1, source_target_pairs={{0,96},{4,100},{8,104},{12,108},{16,112},{20,116},{24,120},{28,124... | collective-permute-start | bytes 331784 | tf_op jit(solution)/shard_map/ppermute | solution.py:277
  134.1 7.5 %collective-permute-start.33 = (bf16[9,16,384]{2,1,0:T(8,128)(2,1)}, bf16[9,16,384]{2,1,0:T(8,128)(2,1)S(1)}, u32[]{:S(2)}, u32[]{:S(2)}) collective-permute-start(bf16[9,16,384]{2,1,0:T(8,128)(2,1)} %get-tuple-element.81), channel_id=1, source_target_pairs={{0,8},{4,12},{8,0},{12,4},{16,24},{20,28},{24,16},{28,20},{32,40},... | collective-permute-start | bytes 331784 | tf_op jit(solution)/shard_map/ppermute | solution.py:277
  134.4 7.2 %collective-permute-start.34 = (bf16[9,16,384]{2,1,0:T(8,128)(2,1)}, bf16[9,16,384]{2,1,0:T(8,128)(2,1)S(1)}, u32[]{:S(2)}, u32[]{:S(2)}) collective-permute-start(bf16[9,16,384]{2,1,0:T(8,128)(2,1)} %get-tuple-element.82), channel_id=1, source_target_pairs={{0,16},{4,20},{8,24},{12,28},{16,0},{20,4},{24,8},{28,12},{32,48},... | collective-permute-start | bytes 331784 | tf_op jit(solution)/shard_map/ppermute | solution.py:277
  136.4 6.2 %collective-permute-start.35 = (bf16[9,16,384]{2,1,0:T(8,128)(2,1)}, bf16[9,16,384]{2,1,0:T(8,128)(2,1)S(1)}, u32[]{:S(2)}, u32[]{:S(2)}) collective-permute-start(bf16[9,16,384]{2,1,0:T(8,128)(2,1)} %get-tuple-element.83), channel_id=1, source_target_pairs={{0,24},{4,28},{8,16},{12,20},{16,8},{20,12},{24,0},{28,4},{32,56},... | collective-permute-start | bytes 331784 | tf_op jit(solution)/shard_map/ppermute | solution.py:277
where the time goes:
time: 144 us
  starting transfers between devices  55 us (38%)
  local copies, waits for them, and re-layouts  38.9 us (27%)
  waiting for transfers between devices  26.9 us (19%)
  Pallas kernels  18.4 us (13%)
  other arithmetic  3.55 us (2%)
    ppermute x12, starting transfers between devices, scatter_space(): lax.ppermute(parts[step], 'space', over(stage, step))  26.2 us
    pallas_call x11, Pallas kernels, call(): pl.pallas_call(kernel, out_shape=tuple(out_shapes), in_specs=[pl.BlockSpe...  18.4 us
    ppermute x12, waiting for transfers between devices, scatter_space(): lax.ppermute(parts[step], 'space', over(stage, step))  15.6 us
    transpose x4, local copies, waits for them, and re-layouts, relaid(): return split.transpose(1, 3, 0, 2, 4).reshape(9, 512, 384)  14.4 us
    ppermute x6, waiting for transfers between devices, scatter_chan(): lax.ppermute(parts[step], 'chan', over_chan(step))  10.2 us
    reshape x2, local copies, waits for them, and re-layouts, relaid(): return split.transpose(1, 3, 0, 2, 4).reshape(9, 512, 384)  10.1 us
    unnamed x46, local copies, waits for them, and re-layouts  9.01 us
    ppermute x6, starting transfers between devices, gather_chan(): return [lax.ppermute(block, 'chan', over_chan(step)) for step in (1, 2, 3)]  8.19 us
  transfers between devices with their start and end apart: 36, of which 9 were waited for; matrix products, arithmetic and copies ran while one was open for 23% of the time, Pallas kernels for 13%

commit v1 on v0

--- a/solution.py
+++ b/solution.py
@@ -9,11 +9,16 @@
 
 BF16 = jnp.bfloat16
 F32 = jnp.float32
+MIB = 1024 * 1024
 TAPS = [(i, k) for i in range(3) for k in range(3)]
-LANES = (slice(128, 384), slice(0, 256))
-
-
-def call(kernel, out_shapes, operands, scratch=(), flops=0):
+MET = ((1, 0), (2, 1))
+
+
+def pair(weight, i, k, b, rows=slice(None)):
+    return [weight[9 * i + 3 * j + k, rows, :] for j in MET[b]]
+
+
+def call(kernel, out_shapes, operands, scratch=(), flops=0, vmem=16):
     nbytes = sum(a.size * a.dtype.itemsize for a in operands)
     nbytes += sum(a.size * a.dtype.itemsize for a in out_shapes)
     return pl.pallas_call(
@@ -22,7 +27,7 @@
         in_specs=[pl.BlockSpec(memory_space=pltpu.VMEM)] * len(operands),
         out_specs=tuple(pl.BlockSpec(memory_space=pltpu.VMEM) for _ in out_shapes),
         scratch_shapes=list(scratch),
-        compiler_params=pltpu.CompilerParams(vmem_limit_bytes=40 * 1024 * 1024),
+        compiler_params=pltpu.CompilerParams(vmem_limit_bytes=vmem * MIB),
         cost_estimate=pl.CostEstimate(flops=flops, bytes_accessed=nbytes, transcendentals=0),
     )(*operands)
 
@@ -57,8 +62,9 @@
     for k in range(3):
         part = []
         for i in range(3):
-            tap = 3 * i + k
-            rhs = jnp.concatenate([weight[tap, :, LANES[0]], weight[tap, :, LANES[1]]], axis=0)
+            rhs = jnp.concatenate(
+                [jnp.concatenate(pair(weight, i, k, b), axis=1) for b in range(2)], axis=0
+            )
             part.append(jnp.dot(values, rhs, preferred_element_type=F32))
         planes = jnp.concatenate(
             [
@@ -117,7 +123,7 @@
         rows = pl.ds(pl.multiple_of((y ^ step) * 128, 128), 128)
         rhs = jnp.concatenate(
             [
-                jnp.concatenate([weight[3 * i + k, rows, LANES[b]] for i, k in TAPS], axis=1)
+                jnp.concatenate(sum([pair(weight, i, k, b, rows) for i, k in TAPS], []), axis=1)
                 for b in range(2)
             ],
             axis=0,
@@ -153,7 +159,7 @@
 
 def middle(own, inner, outer, parts):
     outs = [shape((256, 256), BF16)] * 2 + [shape((128, 256), BF16)] * 2
-    return call(middle_kernel, outs, (own, inner, outer, *parts), flops=256 * 256 * 20)
+    return call(middle_kernel, outs, (own, inner, outer, *parts), flops=256 * 256 * 20, vmem=8)
 
 
 def wprod_kernel(stage, v_own, v_far, d_own, d_far, o0, o1, o2, o3, total):
@@ -208,7 +214,7 @@
 def second(stage, parts):
     outs = [shape((9, 16, 384), F32)] + [shape((9, 16, 384), BF16)] * 3
     return call(
-        functools.partial(second_kernel, stage), outs, parts, [pltpu.VMEM((9, 64, 384), F32)]
+        functools.partial(second_kernel, stage), outs, parts, [pltpu.VMEM((9, 64, 384), F32)], vmem=8
     )
 
 
@@ -217,11 +223,11 @@
         tap = 3 * i + k
         total = own[tap] + r1[tap].astype(F32) + r2[tap].astype(F32) + r3[tap].astype(F32)
         for j in range(3):
-            out[:, 9 * i + 3 * j + k, :] = total[:, (2 - j) * 128 : (2 - j) * 128 + 128]
+            out[9 * i + 3 * j + k] = total[:, (2 - j) * 128 : (2 - j) * 128 + 128]
 
 
 def last(parts):
-    return call(last_kernel, [shape((16, 27, 128), F32)], parts)[0]
+    return call(last_kernel, [shape((27, 16, 128), F32)], parts, vmem=4)[0].transpose(1, 0, 2)
 
 
 def chip(z, x, core):
@@ -255,11 +261,6 @@
 
 def channels_major(block):
     return block.reshape(2, 128, 2, 128).transpose(3, 0, 2, 1).astype(BF16)
-
-
-def relaid(weight):
-    split = weight.reshape(512, 3, 3, 3, 128)[:, :, ::-1]
-    return split.transpose(1, 3, 0, 2, 4).reshape(9, 512, 384)
 
 
 def gather_chan(block):
@@ -294,8 +295,8 @@
         lax.dynamic_slice_in_dim(c_own, (1 - core) * 128, 128, 0),
         lax.dynamic_slice_in_dim(c_own, core * 128, 128, 0),
     )
-    w_two = relaid(weight_two)
-    w_one = relaid(weight_one)
+    w_two = weight_two.transpose(1, 0, 2)
+    w_one = weight_one.transpose(1, 0, 2)
     *hidden_parts, c_haloed = conv_t(c_own, c_inner, c_outer, w_two)
     hidden_parts = scatter_chan(hidden_parts)
     c_far = lax.ppermute(c_haloed, "space", CORES)

time: 144 us -> 122 us (0.85)
  local copies, waits for them, and re-layouts: 38.9 us -> 15.7 us
  waiting for transfers between devices: 26.9 us -> 29 us
  Pallas kernels: 18.4 us -> 16.5 us
    transpose x4 -> x0, local copies, waits for them, and re-layouts: 14.4 us -> none  [relaid(): return split.transpose(1, 3, 0, 2, 4).reshape(9, 512, 384)]
    reshape x2 -> x0, local copies, waits for them, and re-layouts: 10.1 us -> none  [relaid(): return split.transpose(1, 3, 0, 2, 4).reshape(9, 512, 384)]
    ppermute x12, waiting for transfers between devices: 15.6 us -> 17.8 us  [scatter_space(): lax.ppermute(parts[step], 'space', over(stage, step))]
    pallas_call x11, Pallas kernels: 18.4 us -> 16.5 us  [call(): pl.pallas_call(kernel, out_shape=tuple(out_shapes), in_specs=[pl.BlockSpe...]
    convert_element_type x4, local copies, waits for them, and re-layouts: 2.55 us -> 4.14 us  [channels_major(): return block.reshape(2, 128, 2, 128).transpose(3, 0, 2, 1).astype(BF16)]
    unnamed x46 -> x40, local copies, waits for them, and re-layouts: 9.01 us -> 9.44 us
  transfers between devices with their start and end apart: 36 -> 36, of which waited for: 9 -> 8; matrix products, arithmetic and copies ran while one was open for 23% -> 7% of each run, Pallas kernels for 13% -> 13%
where the time goes in v1:
time: 122 us; the launch traced here: 121 us
  starting transfers between devices  56.3 us (46%)
  waiting for transfers between devices  29 us (24%)
  Pallas kernels  16.5 us (14%)
  local copies, waits for them, and re-layouts  15.7 us (13%)
  other arithmetic  2.66 us (2%)
    ppermute x12, starting transfers between devices, scatter_space(): lax.ppermute(parts[step], 'space', over(stage, step))  26.4 us
    ppermute x12, waiting for transfers between devices, scatter_space(): lax.ppermute(parts[step], 'space', over(stage, step))  17.8 us
    pallas_call x11, Pallas kernels, call(): pl.pallas_call(kernel, out_shape=tuple(out_shapes), in_specs=[pl.BlockSpe...  16.5 us
    ppermute x6, waiting for transfers between devices, scatter_chan(): lax.ppermute(parts[step], 'chan', over_chan(step))  10.9 us
    ppermute x6, starting transfers between devices, gather_chan(): return [lax.ppermute(block, 'chan', over_chan(step)) for step in (1, 2, 3)]  9.48 us
    unnamed x40, local copies, waits for them, and re-layouts  9.44 us
    ppermute x6, starting transfers between devices, scatter_chan(): lax.ppermute(parts[step], 'chan', over_chan(step))  8.88 us
    convert_element_type x4, local copies, waits for them, and re-layouts, channels_major(): return block.reshape(2, 128, 2, 128).transpose(3, 0, 2, 1).astype(BF16)  4.14 us
  transfers between devices with their start and end apart: 36, of which 8 were waited for; matrix products, arithmetic and copies ran while one was open for 7% of the time, Pallas kernels for 13%

profile of v1, /device:TPU:0, one launch (start us, length us, event | category | flops | bytes accessed | tf_op | source)
XLA Modules:
  0.0 121.1 jit_solution(3910229351125978226)
XLA Ops:
  0.6 1.1 copy.9
  1.9 0.7 collective-permute-start.6
  2.6 1.1 copy.8
  3.7 1.7 %collective-permute-start = (bf16[256,256]{1,0:T(8,128)(2,1)S(1)}, bf16[256,256]{1,0:T(8,128)(2,1)S(1)}, u32[]{:S(2)}, u32[]{:S(2)}) collective-permute-start(bf16[256,256]{1,0:T(8,128)(2,1)S(1)} %bitcast.20), channel_id=1, source_target_pairs={{0,1},{1,0},{2,3},{3,2},{4,5},{5,4},{6,7},{7,6},{8,9},{9,8},{10,11... | collective-permute-start | bytes 393224 | tf_op jit(solution)/shard_map/ppermute | solution.py:267
  5.4 2.9 %collective-permute-start.1 = (bf16[256,256]{1,0:T(8,128)(2,1)S(1)}, bf16[256,256]{1,0:T(8,128)(2,1)S(1)}, u32[]{:S(2)}, u32[]{:S(2)}) collective-permute-start(bf16[256,256]{1,0:T(8,128)(2,1)S(1)} %bitcast.21), channel_id=1, source_target_pairs={{0,2},{1,3},{2,0},{3,1},{4,6},{5,7},{6,4},{7,5},{8,10},{9,11},{10,... | collective-permute-start | bytes 393224 | tf_op jit(solution)/shard_map/ppermute | solution.py:267
  8.3 0.1 collective-permute-start.2
  8.5 2.0 %copy-done.7 = bf16[512,27,128]{2,0,1:T(8,128)(2,1)S(1)} copy-done((bf16[512,27,128]{2,0,1:T(8,128)(2,1)S(1)}, bf16[512,27,128]{2,0,1:T(8,128)(2,1)}, u32[]{:S(2)}) %copy-start.7) | copy-done | bytes 3538968
  10.5 1.4 %shard_map.76 = (f32[256,256]{1,0:T(8,128)S(1)}, bf16[256,256]{1,0:T(8,128)(2,1)S(1)}, bf16[256,256]{1,0:T(8,128)(2,1)S(1)}, bf16[256,256]{1,0:T(8,128)(2,1)S(1)}, bf16[512,256]{1,0:T(8,128)(2,1)S(1)}) custom-call(bf16[256,256]{1,0:T(8,128)(2,1)S(1)} %bitcast.19, bf16[128,256]{1,0:T(8,128)(2,1)S(1)} %collective-permute-done.5.inner, ...), custom_call_target="tpu_custom_call" | custom-call | flops 1207959552 | bytes 4718592 | tf_op jit(solution)/shard_map/pallas_call | solution.py:24
  11.9 0.5 collective-permute-start.7
  12.4 4.1 %collective-permute-start.8 = (bf16[256,256]{1,0:T(8,128)(2,1)S(1)}, bf16[256,256]{1,0:T(8,128)(2,1)S(1)}, u32[]{:S(2)}, u32[]{:S(2)}) collective-permute-start(bf16[256,256]{1,0:T(8,128)(2,1)S(1)} %get-tuple-element.49), channel_id=1, source_target_pairs={{0,2},{1,3},{2,0},{3,1},{4,6},{5,7},{6,4},{7,5},{8,10},{9,11},{10,... | collective-permute-start | bytes 393224 | tf_op jit(solution)/shard_map/ppermute | solution.py:272
  16.6 0.1 collective-permute-start.9
  16.7 1.6 %shard_map.75 = (f32[256,256]{1,0:T(8,128)S(1)}, bf16[128,256]{1,0:T(8,128)(2,1)S(1)}, bf16[128,256]{1,0:T(8,128)(2,1)S(1)}, bf16[256,512]{1,0:T(8,128)(2,1)S(1)}, bf16[256,512]{1,0:T(8,128)(2,1)S(1)}) custom-call(bf16[256,256]{1,0:T(8,128)(2,1)S(1)} %bitcast.23, bf16[256,256]{1,0:T(8,128)(2,1)S(1)} %collective-permute-done.r1, ...), custom_call_target="tpu_custom_call" | custom-call | flops 1207959552 | bytes 4980736 | tf_op jit(solution)/shard_map/pallas_call | solution.py:24
  18.3 1.4 %collective-permute-start.3 = (bf16[128,256]{1,0:T(8,128)(2,1)S(1)}, bf16[128,256]{1,0:T(8,128)(2,1)S(1)}, u32[]{:S(2)}, u32[]{:S(2)}) collective-permute-start(bf16[128,256]{1,0:T(8,128)(2,1)S(1)} %get-tuple-element.45), channel_id=1, source_target_pairs={{0,4},{4,0},{8,12},{12,8},{16,20},{20,16},{24,28},{28,24},{32,36},... | collective-permute-start | bytes 196616 | tf_op jit(solution)/shard_map/ppermute | solution.py:255
  19.7 0.7 collective-permute-start.4
  20.3 0.2 collective-permute-done.3.inner
  20.6 2.2 %collective-permute-done.8.g2 = bf16[256,256]{1,0:T(8,128)(2,1)S(1)} collective-permute-done((bf16[256,256]{1,0:T(8,128)(2,1)S(1)}, bf16[256,256]{1,0:T(8,128)(2,1)S(1)}, u32[]{:S(2)}, u32[]{:S(2)}) %collective-permute-start.8) | collective-permute-done | bytes 131104 | tf_op jit(solution)/shard_map/ppermute | solution.py:272
  22.8 3.2 %collective-permute-done.9.g3 = bf16[256,256]{1,0:T(8,128)(2,1)S(1)} collective-permute-done((bf16[256,256]{1,0:T(8,128)(2,1)S(1)}, bf16[256,256]{1,0:T(8,128)(2,1)S(1)}, u32[]{:S(2)}, u32[]{:S(2)}) %collective-permute-start.9) | collective-permute-done | bytes 131104 | tf_op jit(solution)/shard_map/ppermute | solution.py:272
  26.0 0.2 shard_map.77
  26.2 1.3 %collective-permute-start.15 = (bf16[128,256]{1,0:T(8,128)(2,1)S(1)}, bf16[128,256]{1,0:T(8,128)(2,1)S(1)}, u32[]{:S(2)}, u32[]{:S(2)}) collective-permute-start(bf16[128,256]{1,0:T(8,128)(2,1)S(1)} %get-tuple-element.56), channel_id=1, source_target_pairs={{0,4},{4,0},{8,12},{12,8},{16,20},{20,16},{24,28},{28,24},{32,36},... | collective-permute-start | bytes 196616 | tf_op jit(solution)/shard_map/ppermute | solution.py:255
  27.5 0.7 collective-permute-start.16
  28.1 3.5 %collective-permute-start.20 = (bf16[256,512]{1,0:T(8,128)(2,1)S(1)}, bf16[256,512]{1,0:T(8,128)(2,1)S(1)}, u32[]{:S(2)}, u32[]{:S(2)}) collective-permute-start(bf16[256,512]{1,0:T(8,128)(2,1)S(1)} %get-tuple-element.63), channel_id=1, source_target_pairs={{0,4},{4,0},{8,12},{12,8},{16,20},{20,16},{24,28},{28,24},{32,36},... | collective-permute-start | bytes 786440 | tf_op jit(solution)/shard_map/ppermute | solution.py:306
  31.7 2.1 %shard_map.79 = (f32[256,256]{1,0:T(8,128)S(1)}, bf16[256,256]{1,0:T(8,128)(2,1)}, bf16[256,256]{1,0:T(8,128)(2,1)}, bf16[256,256]{1,0:T(8,128)(2,1)S(1)}, bf16[512,256]{1,0:T(8,128)(2,1)S(1)}) custom-call(bf16[256,256]{1,0:T(8,128)(2,1)S(1)} %get-tuple-element.55.own, bf16[128,256]{1,0:T(8,128)(2,1)S(1)} %collective-permute-done.15.inner, ...), custom_call_target="tpu_custom_call" | custom-call | flops 1207959552 | bytes 4718592 | tf_op jit(solution)/shard_map/pallas_call | solution.py:24
  33.8 1.8 %collective-permute-start.21 = (bf16[512,256]{1,0:T(8,128)(2,1)S(1)}, bf16[512,256]{1,0:T(8,128)(2,1)S(1)}, u32[]{:S(2)}, u32[]{:S(2)}) collective-permute-start(bf16[512,256]{1,0:T(8,128)(2,1)S(1)} %get-tuple-element.64.d_own), channel_id=1, source_target_pairs={{0,4},{4,0},{8,12},{12,8},{16,20},{20,16},{24,28},{28,24},{32,36},... | collective-permute-start | bytes 786440 | tf_op jit(solution)/shard_map/ppermute | solution.py:313
  35.6 3.1 %collective-permute-start.11 = (bf16[256,256]{1,0:T(8,128)(2,1)S(1)}, bf16[256,256]{1,0:T(8,128)(2,1)S(1)}, u32[]{:S(2)}, u32[]{:S(2)}) collective-permute-start(bf16[256,256]{1,0:T(8,128)(2,1)S(1)} %get-tuple-element.51.own), channel_id=1, source_target_pairs={{0,2},{1,3},{2,0},{3,1},{4,6},{5,7},{6,4},{7,5},{8,10},{9,11},{10,... | collective-permute-start | bytes 393224 | tf_op jit(solution)/shard_map/ppermute | solution.py:267
  38.7 1.6 %collective-permute-start.12 = (bf16[256,256]{1,0:T(8,128)(2,1)S(1)}, bf16[256,256]{1,0:T(8,128)(2,1)S(1)}, u32[]{:S(2)}, u32[]{:S(2)}) collective-permute-start(bf16[256,256]{1,0:T(8,128)(2,1)S(1)} %get-tuple-element.51.own), channel_id=1, source_target_pairs={{0,3},{1,2},{2,1},{3,0},{4,7},{5,6},{6,5},{7,4},{8,11},{9,10},{10,... | collective-permute-start | bytes 393224 | tf_op jit(solution)/shard_map/ppermute | solution.py:267
  40.3 2.5 %shard_map.80 = (f32[9,64,384]{2,1,0:T(8,128)S(1)}, bf16[9,64,384]{2,1,0:T(8,128)(2,1)S(1)}, bf16[9,64,384]{2,1,0:T(8,128)(2,1)}, bf16[9,64,384]{2,1,0:T(8,128)(2,1)}) custom-call(bf16[256,512]{1,0:T(8,128)(2,1)S(1)} %get-tuple-element.62.v_own, bf16[256,512]{1,0:T(8,128)(2,1)S(1)} %collective-permute-done.20.v_far, ...), custom_call_target="tpu_custom_call" | custom-call | flops 1207959552 | bytes 3260416 | tf_op jit(solution)/shard_map/pallas_call | solution.py:24
  42.8 1.8 %collective-permute-start.22 = (bf16[9,64,384]{2,1,0:T(8,128)(2,1)S(1)}, bf16[9,64,384]{2,1,0:T(8,128)(2,1)S(1)}, u32[]{:S(2)}, u32[]{:S(2)}) collective-permute-start(bf16[9,64,384]{2,1,0:T(8,128)(2,1)S(1)} %get-tuple-element.66), channel_id=1, source_target_pairs={{0,8},{4,12},{8,0},{12,4},{16,24},{20,28},{24,16},{28,20},{32,40},... | collective-permute-start | bytes 1327112 | tf_op jit(solution)/shard_map/ppermute | solution.py:278
  44.6 7.2 %collective-permute-start.23 = (bf16[9,64,384]{2,1,0:T(8,128)(2,1)}, bf16[9,64,384]{2,1,0:T(8,128)(2,1)S(1)}, u32[]{:S(2)}, u32[]{:S(2)}) collective-permute-start(bf16[9,64,384]{2,1,0:T(8,128)(2,1)} %get-tuple-element.67), channel_id=1, source_target_pairs={{0,16},{4,20},{8,24},{12,28},{16,0},{20,4},{24,8},{28,12},{32,48},... | collective-permute-start | bytes 1327112 | tf_op jit(solution)/shard_map/ppermute | solution.py:278
  51.8 0.7 collective-permute-start.24
  52.4 2.2 %shard_map.78 = (f32[256,256]{1,0:T(8,128)S(1)}, bf16[128,256]{1,0:T(8,128)(2,1)}, bf16[128,256]{1,0:T(8,128)(2,1)}, bf16[256,512]{1,0:T(8,128)(2,1)S(1)}, bf16[256,512]{1,0:T(8,128)(2,1)S(1)}) custom-call(bf16[256,256]{1,0:T(8,128)(2,1)S(1)} %get-tuple-element.51.own, bf16[256,256]{1,0:T(8,128)(2,1)S(1)} %collective-permute-done.10.r1, ...), custom_call_target="tpu_custom_call" | custom-call | flops 1207959552 | bytes 4980736 | tf_op jit(solution)/shard_map/pallas_call | solution.py:24
  54.6 0.7 copy-done.2
  55.3 0.7 copy-done.15
  56.0 0.7 copy-done.11
  56.7 1.6 %collective-permute-start.19 = (bf16[256,256]{1,0:T(8,128)(2,1)S(1)}, bf16[256,256]{1,0:T(8,128)(2,1)S(1)}, u32[]{:S(2)}, u32[]{:S(2)}) collective-permute-start(bf16[256,256]{1,0:T(8,128)(2,1)S(1)} %get-tuple-element.61), channel_id=1, source_target_pairs={{0,3},{1,2},{2,1},{3,0},{4,7},{5,6},{6,5},{7,4},{8,11},{9,10},{10,... | collective-permute-start | bytes 393224 | tf_op jit(solution)/shard_map/ppermute | solution.py:272
  58.4 5.5 %collective-permute-done.19 = bf16[256,256]{1,0:T(8,128)(2,1)S(1)} collective-permute-done((bf16[256,256]{1,0:T(8,128)(2,1)S(1)}, bf16[256,256]{1,0:T(8,128)(2,1)S(1)}, u32[]{:S(2)}, u32[]{:S(2)}) %collective-permute-start.19) | collective-permute-done | bytes 131104 | tf_op jit(solution)/shard_map/ppermute | solution.py:272
  63.9 0.7 copy-done.13
  64.6 2.5 %collective-permute-start.17 = (bf16[256,256]{1,0:T(8,128)(2,1)}, bf16[256,256]{1,0:T(8,128)(2,1)}, u32[]{:S(2)}, u32[]{:S(2)}) collective-permute-start(bf16[256,256]{1,0:T(8,128)(2,1)} %get-tuple-element.59), channel_id=1, source_target_pairs={{0,1},{1,0},{2,3},{3,2},{4,5},{5,4},{6,7},{7,6},{8,9},{9,8},{10,11... | collective-permute-start | bytes 393224 | tf_op jit(solution)/shard_map/ppermute | solution.py:272
  67.1 1.0 copy-done.10
  68.1 0.9 copy-done.12
  69.0 0.9 copy-done.14
  70.0 0.9 copy-done.16
  70.9 2.6 %shard_map.83 = (f32[9,64,384]{2,1,0:T(8,128)S(1)}, bf16[9,64,384]{2,1,0:T(8,128)(2,1)}, bf16[9,64,384]{2,1,0:T(8,128)(2,1)}, bf16[9,64,384]{2,1,0:T(8,128)(2,1)}) custom-call(bf16[256,512]{1,0:T(8,128)(2,1)S(1)} %copy-done.16, bf16[256,512]{1,0:T(8,128)(2,1)S(1)} %copy-done.14, bf16[512,256]{1,0:T(8,128)(2,1)S(1)} %copy-done.10, bf16[512,256]{1,0:T(8,128)(2,1)S(1)} %copy-done.12), custom_call_target="tpu_custom_call" | custom-call | flops 1207959552 | bytes 3260416 | tf_op jit(solution)/shard_map/pallas_call | solution.py:24
  73.5 1.3 %collective-permute-start.13 = (bf16[128,256]{1,0:T(8,128)(2,1)}, bf16[128,256]{1,0:T(8,128)(2,1)}, u32[]{:S(2)}, u32[]{:S(2)}) collective-permute-start(bf16[128,256]{1,0:T(8,128)(2,1)} %get-tuple-element.53), channel_id=1, source_target_pairs={{4,8},{8,4},{12,16},{16,12},{20,24},{24,20},{28,32},{32,28},{36,40... | collective-permute-start | bytes 196616 | tf_op jit(solution)/shard_map/ppermute | solution.py:255
  74.8 0.2 collective-permute-start.14
  74.9 3.4 %collective-permute-start.30 = (bf16[9,64,384]{2,1,0:T(8,128)(2,1)}, bf16[9,64,384]{2,1,0:T(8,128)(2,1)S(1)}, u32[]{:S(2)}, u32[]{:S(2)}) collective-permute-start(bf16[9,64,384]{2,1,0:T(8,128)(2,1)} %get-tuple-element.77), channel_id=1, source_target_pairs={{0,32},{4,36},{8,40},{12,44},{16,48},{20,52},{24,56},{28,60},{32,0... | collective-permute-start | bytes 1327112 | tf_op jit(solution)/shard_map/ppermute | solution.py:278
  78.4 3.9 %collective-permute-start.31 = (bf16[9,64,384]{2,1,0:T(8,128)(2,1)}, bf16[9,64,384]{2,1,0:T(8,128)(2,1)}, u32[]{:S(2)}, u32[]{:S(2)}) collective-permute-start(bf16[9,64,384]{2,1,0:T(8,128)(2,1)} %get-tuple-element.78), channel_id=1, source_target_pairs={{0,64},{4,68},{8,72},{12,76},{16,80},{20,84},{24,88},{28,92},{32,9... | collective-permute-start | bytes 1327112 | tf_op jit(solution)/shard_map/ppermute | solution.py:278
  82.3 1.7 %add_convert_fusion = bf16[256,256]{1,0:T(8,128)(2,1)} fusion(bf16[256,256]{1,0:T(8,128)(2,1)S(1)} %copy-done.18, bf16[256,256]{1,0:T(8,128)(2,1)} %collective-permute-done.18, f32[256,256]{1,0:T(8,128)S(1)} %copy-done.1, bf16[256,256]{1,0:T(8,128)(2,1)} %collective-permute-done.17), kind=kLoop, calls=%fused_computation | loop fusion | flops 458752 | bytes 786432 | tf_op jit(solution)/shard_map/convert_element_type | solution.py:263
  83.9 1.6 %convert_element_type.36 = bf16[2,128,2,128]{3,2,1,0:T(2,128)(2,1)} reshape(bf16[256,256]{1,0:T(8,128)(2,1)} %add_convert_fusion) | data formatting | bytes 262144 | tf_op jit(solution)/shard_map/convert_element_type | solution.py:263
  85.5 1.7 %copy.11 = bf16[2,128,2,128]{1,2,0,3:T(2,128)(2,1)} copy(bf16[2,128,2,128]{3,2,1,0:T(2,128)(2,1)} %convert_element_type.36) | data formatting | bytes 262144 | tf_op jit(solution)/shard_map/convert_element_type | solution.py:263
  87.3 1.0 shard_map.81
  88.3 0.7 copy-done.4
  89.0 0.9 broadcast_select_fusion.1
  90.0 4.7 %collective-permute-start.26 = (bf16[9,16,384]{2,1,0:T(8,128)(2,1)}, bf16[9,16,384]{2,1,0:T(8,128)(2,1)S(1)}, u32[]{:S(2)}, u32[]{:S(2)}) collective-permute-start(bf16[9,16,384]{2,1,0:T(8,128)(2,1)} %get-tuple-element.71), channel_id=1, source_target_pairs={{0,64},{4,68},{8,72},{12,76},{16,80},{20,84},{24,88},{28,92},{32,9... | collective-permute-start | bytes 331784 | tf_op jit(solution)/shard_map/ppermute | solution.py:278
  94.7 9.1 %collective-permute-done.31.r2 = bf16[9,64,384]{2,1,0:T(8,128)(2,1)} collective-permute-done((bf16[9,64,384]{2,1,0:T(8,128)(2,1)}, bf16[9,64,384]{2,1,0:T(8,128)(2,1)}, u32[]{:S(2)}, u32[]{:S(2)}) %collective-permute-start.31) | collective-permute-done | bytes 442400 | tf_op jit(solution)/shard_map/ppermute | solution.py:278
  103.7 4.9 %collective-permute-done.32.r3 = bf16[9,64,384]{2,1,0:T(8,128)(2,1)} collective-permute-done((bf16[9,64,384]{2,1,0:T(8,128)(2,1)}, bf16[9,64,384]{2,1,0:T(8,128)(2,1)}, u32[]{:S(2)}, u32[]{:S(2)}) %collective-permute-start.32) | collective-permute-done | bytes 442400 | tf_op jit(solution)/shard_map/ppermute | solution.py:278
  108.7 1.5 %shard_map.84 = (f32[9,16,384]{2,1,0:T(8,128)S(1)}, bf16[9,16,384]{2,1,0:T(8,128)(2,1)S(1)}, bf16[9,16,384]{2,1,0:T(8,128)(2,1)S(1)}, bf16[9,16,384]{2,1,0:T(8,128)(2,1)S(1)}) custom-call(f32[9,64,384]{2,1,0:T(8,128)S(1)} %get-tuple-element.76.own, bf16[9,64,384]{2,1,0:T(8,128)(2,1)S(1)} %collective-permute-done.30.r1, ...), custom_call_target="tpu_custom_call" | custom-call | bytes 2764800 | tf_op jit(solution)/shard_map/pallas_call | solution.py:24
  110.2 0.8 collective-permute-start.33
  111.0 3.4 %collective-permute-start.34 = (bf16[9,16,384]{2,1,0:T(8,128)(2,1)S(1)}, bf16[9,16,384]{2,1,0:T(8,128)(2,1)S(1)}, u32[]{:S(2)}, u32[]{:S(2)}) collective-permute-start(bf16[9,16,384]{2,1,0:T(8,128)(2,1)S(1)} %get-tuple-element.82), channel_id=1, source_target_pairs={{0,16},{4,20},{8,24},{12,28},{16,0},{20,4},{24,8},{28,12},{32,48},... | collective-permute-start | bytes 331784 | tf_op jit(solution)/shard_map/ppermute | solution.py:278
  114.4 0.5 collective-permute-start.35
  115.0 0.8 copy.10
  115.8 0.7 shard_map.82
  116.6 1.7 %collective-permute-done.34.r2 = bf16[9,16,384]{2,1,0:T(8,128)(2,1)S(1)} collective-permute-done((bf16[9,16,384]{2,1,0:T(8,128)(2,1)S(1)}, bf16[9,16,384]{2,1,0:T(8,128)(2,1)S(1)}, u32[]{:S(2)}, u32[]{:S(2)}) %collective-permute-start.34) | collective-permute-done | bytes 110624 | tf_op jit(solution)/shard_map/ppermute | solution.py:278
  118.3 2.1 %collective-permute-done.35.r3 = bf16[9,16,384]{2,1,0:T(8,128)(2,1)S(1)} collective-permute-done((bf16[9,16,384]{2,1,0:T(8,128)(2,1)S(1)}, bf16[9,16,384]{2,1,0:T(8,128)(2,1)S(1)}, u32[]{:S(2)}, u32[]{:S(2)}) %collective-permute-start.35) | collective-permute-done | bytes 110624 | tf_op jit(solution)/shard_map/ppermute | solution.py:278
  120.4 0.7 shard_map.85
  (69 shorter events, 0.4 us)
Async XLA Ops:
  1.8 6.7 %collective-permute-start.5 = (bf16[128,256]{1,0:T(8,128)(2,1)S(1)}, bf16[128,256]{1,0:T(8,128)(2,1)S(1)}, u32[]{:S(2)}, u32[]{:S(2)}) collective-permute-start(bf16[128,256]{1,0:T(8,128)(2,1)S(1)} %get-tuple-element.87), channel_id=1, source_target_pairs={{0,4},{4,0},{8,12},{12,8},{16,20},{20,16},{24,28},{28,24},{32,36},... | collective-permute-start | bytes 196616 | tf_op jit(solution)/shard_map/ppermute | solution.py:255
  1.9 6.6 %collective-permute-start.6 = (bf16[128,256]{1,0:T(8,128)(2,1)S(1)}, bf16[128,256]{1,0:T(8,128)(2,1)S(1)}, u32[]{:S(2)}, u32[]{:S(2)}) collective-permute-start(bf16[128,256]{1,0:T(8,128)(2,1)S(1)} %get-tuple-element.86), channel_id=1, source_target_pairs={{4,8},{8,4},{12,16},{16,12},{20,24},{24,20},{28,32},{32,28},{36,40... | collective-permute-start | bytes 196616 | tf_op jit(solution)/shard_map/ppermute | solution.py:255
  3.6 13.1 %copy-start.6 = (bf16[512,27,128]{2,0,1:T(8,128)(2,1)S(1)}, bf16[512,27,128]{2,0,1:T(8,128)(2,1)}, u32[]{:S(2)}) copy-start(bf16[512,27,128]{2,0,1:T(8,128)(2,1)} %param.5) | copy-start | bytes 10616836
  3.7 12.9 %collective-permute-start = (bf16[256,256]{1,0:T(8,128)(2,1)S(1)}, bf16[256,256]{1,0:T(8,128)(2,1)S(1)}, u32[]{:S(2)}, u32[]{:S(2)}) collective-permute-start(bf16[256,256]{1,0:T(8,128)(2,1)S(1)} %bitcast.20), channel_id=1, source_target_pairs={{0,1},{1,0},{2,3},{3,2},{4,5},{5,4},{6,7},{7,6},{8,9},{9,8},{10,11... | collective-permute-start | bytes 393224 | tf_op jit(solution)/shard_map/ppermute | solution.py:267
  5.4 11.3 %collective-permute-start.1 = (bf16[256,256]{1,0:T(8,128)(2,1)S(1)}, bf16[256,256]{1,0:T(8,128)(2,1)S(1)}, u32[]{:S(2)}, u32[]{:S(2)}) collective-permute-start(bf16[256,256]{1,0:T(8,128)(2,1)S(1)} %bitcast.21), channel_id=1, source_target_pairs={{0,2},{1,3},{2,0},{3,1},{4,6},{5,7},{6,4},{7,5},{8,10},{9,11},{10,... | collective-permute-start | bytes 393224 | tf_op jit(solution)/shard_map/ppermute | solution.py:267
  8.3 8.4 %collective-permute-start.2 = (bf16[256,256]{1,0:T(8,128)(2,1)S(1)}, bf16[256,256]{1,0:T(8,128)(2,1)S(1)}, u32[]{:S(2)}, u32[]{:S(2)}) collective-permute-start(bf16[256,256]{1,0:T(8,128)(2,1)S(1)} %bitcast.22), channel_id=1, source_target_pairs={{0,3},{1,2},{2,1},{3,0},{4,7},{5,6},{6,5},{7,4},{8,11},{9,10},{10,... | collective-permute-start | bytes 393224 | tf_op jit(solution)/shard_map/ppermute | solution.py:267
  8.5 2.0 %copy-start.7 = (bf16[512,27,128]{2,0,1:T(8,128)(2,1)S(1)}, bf16[512,27,128]{2,0,1:T(8,128)(2,1)}, u32[]{:S(2)}) copy-start(bf16[512,27,128]{2,0,1:T(8,128)(2,1)} %param.6) | copy-start | bytes 10616836
  11.9 28.4 %copy-start.9 = (bf16[512,256]{1,0:T(8,128)(2,1)}, bf16[512,256]{1,0:T(8,128)(2,1)S(1)}, u32[]{:S(2)}) copy-start(bf16[512,256]{1,0:T(8,128)(2,1)S(1)} %get-tuple-element.75.d_own) | copy-start | bytes 786436
  11.9 8.7 %collective-permute-start.7 = (bf16[256,256]{1,0:T(8,128)(2,1)S(1)}, bf16[256,256]{1,0:T(8,128)(2,1)S(1)}, u32[]{:S(2)}, u32[]{:S(2)}) collective-permute-start(bf16[256,256]{1,0:T(8,128)(2,1)S(1)} %get-tuple-element.48), channel_id=1, source_target_pairs={{0,1},{1,0},{2,3},{3,2},{4,5},{5,4},{6,7},{7,6},{8,9},{9,8},{10,11... | collective-permute-start | bytes 393224 | tf_op jit(solution)/shard_map/ppermute | solution.py:272
  12.4 10.3 %collective-permute-start.8 = (bf16[256,256]{1,0:T(8,128)(2,1)S(1)}, bf16[256,256]{1,0:T(8,128)(2,1)S(1)}, u32[]{:S(2)}, u32[]{:S(2)}) collective-permute-start(bf16[256,256]{1,0:T(8,128)(2,1)S(1)} %get-tuple-element.49), channel_id=1, source_target_pairs={{0,2},{1,3},{2,0},{3,1},{4,6},{5,7},{6,4},{7,5},{8,10},{9,11},{10,... | collective-permute-start | bytes 393224 | tf_op jit(solution)/shard_map/ppermute | solution.py:272
  16.6 9.4 %collective-permute-start.9 = (bf16[256,256]{1,0:T(8,128)(2,1)S(1)}, bf16[256,256]{1,0:T(8,128)(2,1)S(1)}, u32[]{:S(2)}, u32[]{:S(2)}) collective-permute-start(bf16[256,256]{1,0:T(8,128)(2,1)S(1)} %get-tuple-element.50), channel_id=1, source_target_pairs={{0,3},{1,2},{2,1},{3,0},{4,7},{5,6},{6,5},{7,4},{8,11},{9,10},{10,... | collective-permute-start | bytes 393224 | tf_op jit(solution)/shard_map/ppermute | solution.py:272
  18.3 2.3 %collective-permute-start.3 = (bf16[128,256]{1,0:T(8,128)(2,1)S(1)}, bf16[128,256]{1,0:T(8,128)(2,1)S(1)}, u32[]{:S(2)}, u32[]{:S(2)}) collective-permute-start(bf16[128,256]{1,0:T(8,128)(2,1)S(1)} %get-tuple-element.45), channel_id=1, source_target_pairs={{0,4},{4,0},{8,12},{12,8},{16,20},{20,16},{24,28},{28,24},{32,36},... | collective-permute-start | bytes 196616 | tf_op jit(solution)/shard_map/ppermute | solution.py:255
  19.7 0.9 collective-permute-start.4
  26.2 5.5 %collective-permute-start.15 = (bf16[128,256]{1,0:T(8,128)(2,1)S(1)}, bf16[128,256]{1,0:T(8,128)(2,1)S(1)}, u32[]{:S(2)}, u32[]{:S(2)}) collective-permute-start(bf16[128,256]{1,0:T(8,128)(2,1)S(1)} %get-tuple-element.56), channel_id=1, source_target_pairs={{0,4},{4,0},{8,12},{12,8},{16,20},{20,16},{24,28},{28,24},{32,36},... | collective-permute-start | bytes 196616 | tf_op jit(solution)/shard_map/ppermute | solution.py:255
  27.5 4.2 %collective-permute-start.16 = (bf16[128,256]{1,0:T(8,128)(2,1)S(1)}, bf16[128,256]{1,0:T(8,128)(2,1)S(1)}, u32[]{:S(2)}, u32[]{:S(2)}) collective-permute-start(bf16[128,256]{1,0:T(8,128)(2,1)S(1)} %get-tuple-element.57), channel_id=1, source_target_pairs={{4,8},{8,4},{12,16},{16,12},{20,24},{24,20},{28,32},{32,28},{36,40... | collective-permute-start | bytes 196616 | tf_op jit(solution)/shard_map/ppermute | solution.py:255
  28.1 12.2 %collective-permute-start.20 = (bf16[256,512]{1,0:T(8,128)(2,1)S(1)}, bf16[256,512]{1,0:T(8,128)(2,1)S(1)}, u32[]{:S(2)}, u32[]{:S(2)}) collective-permute-start(bf16[256,512]{1,0:T(8,128)(2,1)S(1)} %get-tuple-element.63), channel_id=1, source_target_pairs={{0,4},{4,0},{8,12},{12,8},{16,20},{20,16},{24,28},{28,24},{32,36},... | collective-permute-start | bytes 786440 | tf_op jit(solution)/shard_map/ppermute | solution.py:306
  31.7 20.8 %copy-start.8 = (bf16[512,27,128]{2,0,1:T(8,128)(2,1)S(1)}, bf16[512,27,128]{2,0,1:T(8,128)(2,1)}, u32[]{:S(2)}) copy-start(bf16[512,27,128]{2,0,1:T(8,128)(2,1)} %param.6) | copy-start | bytes 10616836
  33.8 18.0 %copy-start = (f32[256,256]{1,0:T(8,128)}, f32[256,256]{1,0:T(8,128)S(1)}, u32[]{:S(2)}) copy-start(f32[256,256]{1,0:T(8,128)S(1)} %get-tuple-element.58) | copy-start | bytes 786436
  33.8 6.6 %collective-permute-start.21 = (bf16[512,256]{1,0:T(8,128)(2,1)S(1)}, bf16[512,256]{1,0:T(8,128)(2,1)S(1)}, u32[]{:S(2)}, u32[]{:S(2)}) collective-permute-start(bf16[512,256]{1,0:T(8,128)(2,1)S(1)} %get-tuple-element.64.d_own), channel_id=1, source_target_pairs={{0,4},{4,0},{8,12},{12,8},{16,20},{20,16},{24,28},{28,24},{32,36},... | collective-permute-start | bytes 786440 | tf_op jit(solution)/shard_map/ppermute | solution.py:313
  35.6 9.0 %collective-permute-start.10 = (bf16[256,256]{1,0:T(8,128)(2,1)S(1)}, bf16[256,256]{1,0:T(8,128)(2,1)S(1)}, u32[]{:S(2)}, u32[]{:S(2)}) collective-permute-start(bf16[256,256]{1,0:T(8,128)(2,1)S(1)} %get-tuple-element.51.own), channel_id=1, source_target_pairs={{0,1},{1,0},{2,3},{3,2},{4,5},{5,4},{6,7},{7,6},{8,9},{9,8},{10,11... | collective-permute-start | bytes 393224 | tf_op jit(solution)/shard_map/ppermute | solution.py:267
  35.6 16.1 %collective-permute-start.11 = (bf16[256,256]{1,0:T(8,128)(2,1)S(1)}, bf16[256,256]{1,0:T(8,128)(2,1)S(1)}, u32[]{:S(2)}, u32[]{:S(2)}) collective-permute-start(bf16[256,256]{1,0:T(8,128)(2,1)S(1)} %get-tuple-element.51.own), channel_id=1, source_target_pairs={{0,2},{1,3},{2,0},{3,1},{4,6},{5,7},{6,4},{7,5},{8,10},{9,11},{10,... | collective-permute-start | bytes 393224 | tf_op jit(solution)/shard_map/ppermute | solution.py:267
  38.7 13.7 %collective-permute-start.12 = (bf16[256,256]{1,0:T(8,128)(2,1)S(1)}, bf16[256,256]{1,0:T(8,128)(2,1)S(1)}, u32[]{:S(2)}, u32[]{:S(2)}) collective-permute-start(bf16[256,256]{1,0:T(8,128)(2,1)S(1)} %get-tuple-element.51.own), channel_id=1, source_target_pairs={{0,3},{1,2},{2,1},{3,0},{4,7},{5,6},{6,5},{7,4},{8,11},{9,10},{10,... | collective-permute-start | bytes 393224 | tf_op jit(solution)/shard_map/ppermute | solution.py:267
  40.3 15.7 %collective-permute-start.29 = (bf16[512,256]{1,0:T(8,128)(2,1)S(1)}, bf16[512,256]{1,0:T(8,128)(2,1)S(1)}, u32[]{:S(2)}, u32[]{:S(2)}) collective-permute-start(bf16[512,256]{1,0:T(8,128)(2,1)S(1)} %get-tuple-element.75.d_own), channel_id=1, source_target_pairs={{0,4},{4,0},{8,12},{12,8},{16,20},{20,16},{24,28},{28,24},{32,36},... | collective-permute-start | bytes 786440 | tf_op jit(solution)/shard_map/ppermute | solution.py:302
  42.8 32.1 %collective-permute-start.22 = (bf16[9,64,384]{2,1,0:T(8,128)(2,1)S(1)}, bf16[9,64,384]{2,1,0:T(8,128)(2,1)S(1)}, u32[]{:S(2)}, u32[]{:S(2)}) collective-permute-start(bf16[9,64,384]{2,1,0:T(8,128)(2,1)S(1)} %get-tuple-element.66), channel_id=1, source_target_pairs={{0,8},{4,12},{8,0},{12,4},{16,24},{20,28},{24,16},{28,20},{32,40},... | collective-permute-start | bytes 1327112 | tf_op jit(solution)/shard_map/ppermute | solution.py:278
  44.6 33.8 %collective-permute-start.23 = (bf16[9,64,384]{2,1,0:T(8,128)(2,1)}, bf16[9,64,384]{2,1,0:T(8,128)(2,1)S(1)}, u32[]{:S(2)}, u32[]{:S(2)}) collective-permute-start(bf16[9,64,384]{2,1,0:T(8,128)(2,1)} %get-tuple-element.67), channel_id=1, source_target_pairs={{0,16},{4,20},{8,24},{12,28},{16,0},{20,4},{24,8},{28,12},{32,48},... | collective-permute-start | bytes 1327112 | tf_op jit(solution)/shard_map/ppermute | solution.py:278
  51.8 30.5 %collective-permute-start.24 = (bf16[9,64,384]{2,1,0:T(8,128)(2,1)}, bf16[9,64,384]{2,1,0:T(8,128)(2,1)S(1)}, u32[]{:S(2)}, u32[]{:S(2)}) collective-permute-start(bf16[9,64,384]{2,1,0:T(8,128)(2,1)} %get-tuple-element.68), channel_id=1, source_target_pairs={{0,24},{4,28},{8,16},{12,20},{16,8},{20,12},{24,0},{28,4},{32,56},... | collective-permute-start | bytes 1327112 | tf_op jit(solution)/shard_map/ppermute | solution.py:278
  54.6 0.7 copy-start.2
  55.3 0.7 copy-start.15
  56.0 7.8 %collective-permute-start.28 = (bf16[256,512]{1,0:T(8,128)(2,1)S(1)}, bf16[256,512]{1,0:T(8,128)(2,1)S(1)}, u32[]{:S(2)}, u32[]{:S(2)}) collective-permute-start(bf16[256,512]{1,0:T(8,128)(2,1)S(1)} %get-tuple-element.74), channel_id=1, source_target_pairs={{0,4},{4,0},{8,12},{12,8},{16,20},{20,16},{24,28},{28,24},{32,36},... | collective-permute-start | bytes 786440 | tf_op jit(solution)/shard_map/ppermute | solution.py:318
  56.0 0.7 copy-start.11
  56.7 7.1 %collective-permute-start.19 = (bf16[256,256]{1,0:T(8,128)(2,1)S(1)}, bf16[256,256]{1,0:T(8,128)(2,1)S(1)}, u32[]{:S(2)}, u32[]{:S(2)}) collective-permute-start(bf16[256,256]{1,0:T(8,128)(2,1)S(1)} %get-tuple-element.61), channel_id=1, source_target_pairs={{0,3},{1,2},{2,1},{3,0},{4,7},{5,6},{6,5},{7,4},{8,11},{9,10},{10,... | collective-permute-start | bytes 393224 | tf_op jit(solution)/shard_map/ppermute | solution.py:272
  63.8 3.2 %copy-start.17 = (bf16[256,256]{1,0:T(8,128)(2,1)}, bf16[256,256]{1,0:T(8,128)(2,1)S(1)}, u32[]{:S(2)}) copy-start(bf16[256,256]{1,0:T(8,128)(2,1)S(1)} %collective-permute-done.19) | copy-start | bytes 393220
  63.8 9.6 %collective-permute-start.18 = (bf16[256,256]{1,0:T(8,128)(2,1)}, bf16[256,256]{1,0:T(8,128)(2,1)}, u32[]{:S(2)}, u32[]{:S(2)}) collective-permute-start(bf16[256,256]{1,0:T(8,128)(2,1)} %get-tuple-element.60), channel_id=1, source_target_pairs={{0,2},{1,3},{2,0},{3,1},{4,6},{5,7},{6,4},{7,5},{8,10},{9,11},{10,... | collective-permute-start | bytes 393224 | tf_op jit(solution)/shard_map/ppermute | solution.py:272
  63.9 0.7 copy-start.13
  64.6 10.2 %collective-permute-start.17 = (bf16[256,256]{1,0:T(8,128)(2,1)}, bf16[256,256]{1,0:T(8,128)(2,1)}, u32[]{:S(2)}, u32[]{:S(2)}) collective-permute-start(bf16[256,256]{1,0:T(8,128)(2,1)} %get-tuple-element.59), channel_id=1, source_target_pairs={{0,1},{1,0},{2,3},{3,2},{4,5},{5,4},{6,7},{7,6},{8,9},{9,8},{10,11... | collective-permute-start | bytes 393224 | tf_op jit(solution)/shard_map/ppermute | solution.py:272
  67.1 15.2 %copy-start.1 = (f32[256,256]{1,0:T(8,128)S(1)}, f32[256,256]{1,0:T(8,128)}, u32[]{:S(2)}) copy-start(f32[256,256]{1,0:T(8,128)} %copy-done) | copy-start | bytes 786436
  67.1 1.0 copy-start.10
  68.1 0.9 copy-start.12
  69.0 0.9 copy-start.14
  70.0 0.9 copy-start.16
  70.9 11.3 %copy-start.18 = (bf16[256,256]{1,0:T(8,128)(2,1)S(1)}, bf16[256,256]{1,0:T(8,128)(2,1)}, u32[]{:S(2)}) copy-start(bf16[256,256]{1,0:T(8,128)(2,1)} %copy-done.17) | copy-start | bytes 393220
  73.5 15.5 %collective-permute-start.13 = (bf16[128,256]{1,0:T(8,128)(2,1)}, bf16[128,256]{1,0:T(8,128)(2,1)}, u32[]{:S(2)}, u32[]{:S(2)}) collective-permute-start(bf16[128,256]{1,0:T(8,128)(2,1)} %get-tuple-element.53), channel_id=1, source_target_pairs={{4,8},{8,4},{12,16},{16,12},{20,24},{24,20},{28,32},{32,28},{36,40... | collective-permute-start | bytes 196616 | tf_op jit(solution)/shard_map/ppermute | solution.py:255
  74.8 14.2 %collective-permute-start.14 = (bf16[128,256]{1,0:T(8,128)(2,1)}, bf16[128,256]{1,0:T(8,128)(2,1)}, u32[]{:S(2)}, u32[]{:S(2)}) collective-permute-start(bf16[128,256]{1,0:T(8,128)(2,1)} %get-tuple-element.54), channel_id=1, source_target_pairs={{0,4},{4,0},{8,12},{12,8},{16,20},{20,16},{24,28},{28,24},{32,36},... | collective-permute-start | bytes 196616 | tf_op jit(solution)/shard_map/ppermute | solution.py:255
  74.9 19.7 %collective-permute-start.30 = (bf16[9,64,384]{2,1,0:T(8,128)(2,1)}, bf16[9,64,384]{2,1,0:T(8,128)(2,1)S(1)}, u32[]{:S(2)}, u32[]{:S(2)}) collective-permute-start(bf16[9,64,384]{2,1,0:T(8,128)(2,1)} %get-tuple-element.77), channel_id=1, source_target_pairs={{0,32},{4,36},{8,40},{12,44},{16,48},{20,52},{24,56},{28,60},{32,0... | collective-permute-start | bytes 1327112 | tf_op jit(solution)/shard_map/ppermute | solution.py:278
  78.4 25.4 %collective-permute-start.31 = (bf16[9,64,384]{2,1,0:T(8,128)(2,1)}, bf16[9,64,384]{2,1,0:T(8,128)(2,1)}, u32[]{:S(2)}, u32[]{:S(2)}) collective-permute-start(bf16[9,64,384]{2,1,0:T(8,128)(2,1)} %get-tuple-element.78), channel_id=1, source_target_pairs={{0,64},{4,68},{8,72},{12,76},{16,80},{20,84},{24,88},{28,92},{32,9... | collective-permute-start | bytes 1327112 | tf_op jit(solution)/shard_map/ppermute | solution.py:278
  82.2 26.4 %collective-permute-start.32 = (bf16[9,64,384]{2,1,0:T(8,128)(2,1)}, bf16[9,64,384]{2,1,0:T(8,128)(2,1)}, u32[]{:S(2)}, u32[]{:S(2)}) collective-permute-start(bf16[9,64,384]{2,1,0:T(8,128)(2,1)} %get-tuple-element.79), channel_id=1, source_target_pairs={{0,96},{4,100},{8,104},{12,108},{16,112},{20,116},{24,120},{28,124... | collective-permute-start | bytes 1327112 | tf_op jit(solution)/shard_map/ppermute | solution.py:278
  87.3 27.7 %copy-start.3 = (f32[256,256]{1,0:T(8,128)S(1)}, f32[256,256]{1,0:T(8,128)}, u32[]{:S(2)}) copy-start(f32[256,256]{1,0:T(8,128)} %copy-done.2) | copy-start | bytes 786436
  88.3 0.7 copy-start.4
  89.0 26.8 %copy-start.5 = (f32[9,16,384]{2,1,0:T(8,128)S(1)}, f32[9,16,384]{2,1,0:T(8,128)}, u32[]{:S(2)}) copy-start(f32[9,16,384]{2,1,0:T(8,128)} %copy-done.4) | copy-start | bytes 663556
  89.0 25.4 %collective-permute-start.25 = (bf16[9,16,384]{2,1,0:T(8,128)(2,1)S(1)}, bf16[9,16,384]{2,1,0:T(8,128)(2,1)S(1)}, u32[]{:S(2)}, u32[]{:S(2)}) collective-permute-start(bf16[9,16,384]{2,1,0:T(8,128)(2,1)S(1)} %get-tuple-element.70), channel_id=1, source_target_pairs={{0,32},{4,36},{8,40},{12,44},{16,48},{20,52},{24,56},{28,60},{32,0... | collective-permute-start | bytes 331784 | tf_op jit(solution)/shard_map/ppermute | solution.py:278
  90.0 25.9 %collective-permute-start.26 = (bf16[9,16,384]{2,1,0:T(8,128)(2,1)}, bf16[9,16,384]{2,1,0:T(8,128)(2,1)S(1)}, u32[]{:S(2)}, u32[]{:S(2)}) collective-permute-start(bf16[9,16,384]{2,1,0:T(8,128)(2,1)} %get-tuple-element.71), channel_id=1, source_target_pairs={{0,64},{4,68},{8,72},{12,76},{16,80},{20,84},{24,88},{28,92},{32,9... | collective-permute-start | bytes 331784 | tf_op jit(solution)/shard_map/ppermute | solution.py:278
  94.6 21.2 %collective-permute-start.27 = (bf16[9,16,384]{2,1,0:T(8,128)(2,1)}, bf16[9,16,384]{2,1,0:T(8,128)(2,1)S(1)}, u32[]{:S(2)}, u32[]{:S(2)}) collective-permute-start(bf16[9,16,384]{2,1,0:T(8,128)(2,1)} %get-tuple-element.72), channel_id=1, source_target_pairs={{0,96},{4,100},{8,104},{12,108},{16,112},{20,116},{24,120},{28,124... | collective-permute-start | bytes 331784 | tf_op jit(solution)/shard_map/ppermute | solution.py:278
  110.2 6.4 %collective-permute-start.33 = (bf16[9,16,384]{2,1,0:T(8,128)(2,1)S(1)}, bf16[9,16,384]{2,1,0:T(8,128)(2,1)S(1)}, u32[]{:S(2)}, u32[]{:S(2)}) collective-permute-start(bf16[9,16,384]{2,1,0:T(8,128)(2,1)S(1)} %get-tuple-element.81), channel_id=1, source_target_pairs={{0,8},{4,12},{8,0},{12,4},{16,24},{20,28},{24,16},{28,20},{32,40},... | collective-permute-start | bytes 331784 | tf_op jit(solution)/shard_map/ppermute | solution.py:278
  111.0 7.4 %collective-permute-start.34 = (bf16[9,16,384]{2,1,0:T(8,128)(2,1)S(1)}, bf16[9,16,384]{2,1,0:T(8,128)(2,1)S(1)}, u32[]{:S(2)}, u32[]{:S(2)}) collective-permute-start(bf16[9,16,384]{2,1,0:T(8,128)(2,1)S(1)} %get-tuple-element.82), channel_id=1, source_target_pairs={{0,16},{4,20},{8,24},{12,28},{16,0},{20,4},{24,8},{28,12},{32,48},... | collective-permute-start | bytes 331784 | tf_op jit(solution)/shard_map/ppermute | solution.py:278
  114.4 6.0 %collective-permute-start.35 = (bf16[9,16,384]{2,1,0:T(8,128)(2,1)S(1)}, bf16[9,16,384]{2,1,0:T(8,128)(2,1)S(1)}, u32[]{:S(2)}, u32[]{:S(2)}) collective-permute-start(bf16[9,16,384]{2,1,0:T(8,128)(2,1)S(1)} %get-tuple-element.83), channel_id=1, source_target_pairs={{0,24},{4,28},{8,16},{12,20},{16,8},{20,12},{24,0},{28,4},{32,56},... | collective-permute-start | bytes 331784 | tf_op jit(solution)/shard_map/ppermute | solution.py:278

commit v2 on v1

v2 whole, which is shorter than its diff:
```python
import functools

import jax
import jax.numpy as jnp
from jax import lax
from jax.experimental import pallas as pl
from jax.experimental.pallas import tpu as pltpu
from jax.sharding import PartitionSpec as P

BF16 = jnp.bfloat16
F32 = jnp.float32
MIB = 1024 * 1024
TAPS = [(i, k) for i in range(3) for k in range(3)]
MET = ((1, 0), (2, 1))


def pair(weight, i, k, b, rows=slice(None)):
    return [weight[9 * i + 3 * j + k, rows, :] for j in MET[b]]


def call(kernel, out_shapes, operands, scratch=(), flops=0, vmem=16):
    nbytes = sum(a.size * a.dtype.itemsize for a in operands)
    nbytes += sum(a.size * a.dtype.itemsize for a in out_shapes)
    return pl.pallas_call(
        kernel,
        out_shape=tuple(out_shapes),
        in_specs=[pl.BlockSpec(memory_space=pltpu.VMEM)] * len(operands),
        out_specs=tuple(pl.BlockSpec(memory_space=pltpu.VMEM) for _ in out_shapes),
        scratch_shapes=list(scratch),
        compiler_params=pltpu.CompilerParams(vmem_limit_bytes=vmem * MIB),
        cost_estimate=pl.CostEstimate(flops=flops, bytes_accessed=nbytes, transcendentals=0),
    )(*operands)


def shape(dims, dtype):
    return jax.ShapeDtypeStruct(dims, dtype)


def row_shift(block, down):
    rows = block.shape[0]
    place = lax.broadcasted_iota(jnp.int32, block.shape, 0) % 128
    if down:
        return jnp.where(place == 0, 0.0, pltpu.roll(block, 1, 0))
    return jnp.where(place == 127, 0.0, pltpu.roll(block, rows - 1, 0))


def three_shifts(haloed):
    wide = haloed.astype(F32)
    return (row_shift(wide, False).astype(BF16), haloed, row_shift(wide, True).astype(BF16))


def layer_call(kernel, outs, operands, weight, scratch, vmem, flops):
    vmem_spec = pl.BlockSpec(memory_space=pltpu.VMEM)
    return pl.pallas_call(
        kernel,
        out_shape=tuple(outs),
        in_specs=[vmem_spec] * (len(operands) + 1),
        out_specs=(vmem_spec,) * len(outs),
        scratch_shapes=scratch,
        compiler_params=pltpu.CompilerParams(vmem_limit_bytes=vmem * MIB),
        cost_estimate=pl.CostEstimate(flops=flops, bytes_accessed=5 * MIB, transcendentals=0),
    )(*operands, weight)


def conv_kernel(own, r1, r2, r3, three, weight, core_out, inner_out, outer_out, *rest):
    *payload, field, turned = rest
    y = lax.axis_index("chan")
    space = lax.axis_index("space")
    first = space % 2 == 0
    z = space // 8
    for step, part in enumerate((own, r1, r2, r3)):
        place = y ^ step
        for b in range(2):
            at = pl.multiple_of(b * 512 + place * 128, 128)
            field[:, pl.ds(at, 128)] = part[:, b * 128 : b * 128 + 128]
        turn(part[...], turned.at[place])
    for step in range(4):
        if len(payload) == 1:
            out, at = payload[0].at[step], step
        else:
            out, at = payload[step], z ^ step
        out[:256, :] = turned[at]
        out[256:, :] = three[...]
    values = field[...]
    sums = None
    for k in range(3):
        part = []
        for i in range(3):
            rhs = jnp.concatenate(
                [jnp.concatenate(pair(weight, i, k, b), axis=1) for b in range(2)], axis=0
            )
            part.append(jnp.dot(values, rhs, preferred_element_type=F32))
        planes = jnp.concatenate(
            [
                part[2][:128],
                part[1][:128] + part[2][128:],
                part[0][:128] + part[1][128:],
                part[0][128:],
            ],
            axis=0,
        )
        if k != 1:
            planes = row_shift(planes, k == 0)
        sums = planes if sums is None else sums + planes
    core_out[...] = sums[128:384]
    low = sums[:128].astype(BF16)
    high = sums[384:].astype(BF16)
    inner_out[...] = jnp.where(first, high, low)
    outer_out[...] = jnp.where(first, low, high)


def conv(own, others, weight, three, whole):
    outs = [shape((256, 256), F32), shape((128, 256), BF16), shape((128, 256), BF16)]
    outs += [shape((4, 640, 256), BF16)] if whole else [shape((640, 256), BF16)] * 4
    scratch = [
        pltpu.VMEM((256, 1024), BF16),
        pltpu.VMEM((4, 256, 256), BF16),
    ]
    core_out, inner, outer, *payload = layer_call(
        conv_kernel, outs, (own, *others, three), weight, scratch, 16, 2 * 9 * 256 * 1024 * 256
    )
    return core_out, inner, outer, payload


def conv_t_kernel(own, inner, outer, weight, *rest):
    *outs, three_out = rest
    y = lax.axis_index("chan")
    first = lax.axis_index("space") % 2 == 0
    low = jnp.where(first, outer[...], inner[...])
    high = jnp.where(first, inner[...], outer[...])
    haloed = jnp.concatenate([low, own[...], high], axis=0)
    three_out[...] = jnp.where(first, haloed[:384], haloed[128:])
    moved = three_shifts(haloed)
    lhs = jnp.concatenate([moved[k][(2 - i) * 128 : (2 - i) * 128 + 256] for i, k in TAPS], axis=1)
    for step in range(4):
        group = step if len(outs) == 1 else y ^ step
        out = outs[0].at[step] if len(outs) == 1 else outs[step]
        rows = pl.ds(group * 128 if len(outs) == 1 else pl.multiple_of(group * 128, 128), 128)
        rhs = jnp.concatenate(
            [
                jnp.concatenate(sum([pair(weight, i, k, b, rows) for i, k in TAPS], []), axis=1)
                for b in range(2)
            ],
            axis=0,
        )
        out[...] = lax.dot_general(
            lhs, rhs, (((1,), (1,)), ((), ())), preferred_element_type=F32
        ).astype(out.dtype)


def conv_t(own, inner, outer, weight, whole):
    if whole:
        outs = [shape((4, 256, 256), BF16)]
    else:
        outs = [shape((256, 256), F32)] + [shape((256, 256), BF16)] * 3
    outs += [shape((384, 256), BF16)]
    *parts, three = layer_call(
        conv_t_kernel, outs, (own, inner, outer), weight, [], 16, 2 * 9 * 256 * 256 * 1024
    )
    return parts, three


def turn(block, out):
    turned = block.T
    for half in range(2):
        for b in range(2):
            for x in range(4):
                source = b * 128 + x * 32 + half * 16
                target = half * 128 + b * 64 + x * 16
                out[target : target + 16, :] = turned[source : source + 16]


def middle_kernel(
    own, inner, outer, g0, g1, g2, g3, hidden_out, grad_out, inner_out, outer_out
):
    first = lax.axis_index("space") % 2 == 0
    zero = jnp.where(first, outer[...], inner[...]).astype(F32)
    one = jnp.where(first, inner[...], outer[...]).astype(F32)
    pre = own[...] + jnp.concatenate([zero, one], axis=0)
    hidden_grad = g0[...] + g1[...].astype(F32) + g2[...].astype(F32) + g3[...].astype(F32)
    sig = jax.nn.sigmoid(pre)
    hidden_out[...] = (pre * sig).astype(BF16)
    grad = (hidden_grad * sig * (1.0 + pre * (1.0 - sig))).astype(BF16)
    grad_out[...] = grad
    inner_out[...] = jnp.where(first, grad[128:], grad[:128])
    outer_out[...] = jnp.where(first, grad[:128], grad[128:])


def middle(own, inner, outer, parts):
    outs = [shape((256, 256), BF16)] * 2 + [shape((128, 256), BF16)] * 2
    return call(middle_kernel, outs, (own, inner, outer, *parts), flops=256 * 256 * 20, vmem=8)


def keep_product(total, tap, product):
    total[tap, :, 0:128] = product[64:, :128]
    total[tap, :, 128:256] = product[64:, 128:] + product[:64, :128]
    total[tap, :, 256:384] = product[:64, 128:]


def wprod_kernel(late_v, v, v_far, d, d_far, o0, o1, o2, o3, d_all, v_all, sums, total, sems):
    space = lax.axis_index("space")
    core, z = space % 2, space // 8
    rows = pl.ds(pl.multiple_of(core * 128, 128), 128)
    started = []
    for step in range(4):
        v_from, d_from = (step, z ^ step) if late_v else (z ^ step, step)
        pieces = []
        for far, (v_slots, d_slots) in enumerate(((v, d), (v_far, d_far))):
            pieces += [
                (v_slots.at[v_from, rows], v_all.at[step, core ^ far]),
                (d_slots.at[d_from, pl.ds(256, 384)], d_all.at[step, core ^ far]),
            ]
        started.append(
            [
                pltpu.make_async_copy(source, target, sems.at[4 * step + at])
                for at, (source, target) in enumerate(pieces)
            ]
        )
    for copies in started:
        for copy in copies:
            copy.start()
    for step, copies in enumerate(started):
        for copy in copies:
            copy.wait()
        lhs = jnp.concatenate([v_all[step, 0], v_all[step, 1]], axis=1)
        moved = three_shifts(d_all[step].reshape(768, 256))
        for i, k in TAPS:
            at = (2 - i) * 128
            product = jnp.dot(lhs, moved[k][at : at + 512], preferred_element_type=F32)
            if step == 0:
                sums[3 * i + k] = product
            else:
                sums[3 * i + k] += product
    for tap in range(9):
        total[tap, :, 0:128] = sums[tap, 64:, :128]
        total[tap, :, 128:256] = sums[tap, 64:, 128:] + sums[tap, :64, :128]
        total[tap, :, 256:384] = sums[tap, :64, 128:]
    x = (space // 2) % 4
    for step, out in enumerate((o0, o1, o2, o3)):
        chosen = pl.ds(pl.multiple_of((x ^ step) * 16, 16), 16)
        out[...] = total[:, chosen, :].astype(out.dtype)


def wprod(late_v, v_slots, d_slots):
    hbm_spec = pl.BlockSpec(memory_space=pltpu.HBM)
    vmem_spec = pl.BlockSpec(memory_space=pltpu.VMEM)
    return pl.pallas_call(
        functools.partial(wprod_kernel, late_v),
        out_shape=(shape((9, 16, 384), F32),) + (shape((9, 16, 384), BF16),) * 3,
        in_specs=[hbm_spec] * 4,
        out_specs=(vmem_spec,) * 4,
        scratch_shapes=[
            pltpu.VMEM((4, 2, 384, 256), BF16),
            pltpu.VMEM((4, 2, 128, 256), BF16),
            pltpu.VMEM((9, 128, 256), F32),
            pltpu.VMEM((9, 64, 384), F32),
            pltpu.SemaphoreType.DMA((16,)),
        ],
        compiler_params=pltpu.CompilerParams(vmem_limit_bytes=24 * MIB),
        cost_estimate=pl.CostEstimate(
            flops=2 * 9 * 128 * 2048 * 256, bytes_accessed=4 * MIB, transcendentals=0
        ),
    )(*v_slots, *d_slots)


def last_kernel(own, r1, r2, r3, out):
    for i, k in TAPS:
        tap = 3 * i + k
        total = own[tap] + r1[tap].astype(F32) + r2[tap].astype(F32) + r3[tap].astype(F32)
        for j in range(3):
            out[9 * i + 3 * j + k] = total[:, (2 - j) * 128 : (2 - j) * 128 + 128]


def last(parts):
    return call(last_kernel, [shape((27, 16, 128), F32)], parts, vmem=4)[0].transpose(1, 0, 2)


def chip(z, x, core):
    return (z * 4 + x) * 2 + core


EVERY = [(z, x, core) for z in range(4) for x in range(4) for core in range(2)]


def over_chan(step):
    return [(i, i ^ step) for i in range(4)]


def over_z(step):
    return [(chip(z, x, c), chip(z ^ step, x, c)) for z, x, c in EVERY]


def over_x(step):
    return [(chip(z, x, c), chip(z, x ^ step, c)) for z, x, c in EVERY]


CORES = [(i, i ^ 1) for i in range(32)]
NEIGHBOURS = [(i, i + 1 if i % 2 else i - 1) for i in range(1, 31)]


def swap_halo(inner, outer):
    return lax.ppermute(inner, "space", CORES), lax.ppermute(outer, "space", NEIGHBOURS)


def cells_major(field):
    return field.transpose(1, 3, 2, 0).reshape(256, 256)


def channels_major(block):
    return block.reshape(2, 128, 2, 128).transpose(3, 0, 2, 1).astype(BF16)


def gather_chan(block):
    return [lax.ppermute(block, "chan", over_chan(step)) for step in (1, 2, 3)]


def scatter_chan(parts):
    return [parts[0]] + [
        lax.ppermute(parts[step], "chan", over_chan(step)) for step in (1, 2, 3)
    ]


def scatter_x(parts):
    return [parts[0]] + [lax.ppermute(parts[step], "space", over_x(step)) for step in (1, 2, 3)]


ALONG_Z = [[chip(z, x, c) for z in range(4)] for x in range(4) for c in range(2)]


def exchange_z(parts):
    return [parts[0]] + [lax.ppermute(parts[step], "space", over_z(step)) for step in (1, 2, 3)]


def with_far(near):
    return [near, lax.ppermute(near, "space", CORES)]


def add_halo(own, inner, outer):
    first = lax.axis_index("space") % 2 == 0
    zero = jnp.where(first, outer, inner).astype(F32)
    one = jnp.where(first, inner, outer).astype(F32)
    return own + jnp.concatenate([zero, one], axis=0)


def body(inputs, weight_one, weight_two, cotangent):
    core = lax.axis_index("space") % 2
    c_own = cells_major(cotangent)
    x_own = cells_major(inputs)
    w_two = weight_two.transpose(1, 0, 2)
    w_one = weight_one.transpose(1, 0, 2)
    c_inner, c_outer = swap_halo(
        lax.dynamic_slice_in_dim(c_own, (1 - core) * 128, 128, 0),
        lax.dynamic_slice_in_dim(c_own, core * 128, 128, 0),
    )
    x_others = gather_chan(x_own)
    hidden_parts, c_three = conv_t(c_own, c_inner, c_outer, w_two, False)
    hidden_parts = scatter_chan(hidden_parts)
    pre, low, high, payload = conv(x_own, x_others, w_one, c_three, True)
    low, high = swap_halo(low, high)
    payload, hidden_parts, low = lax.optimization_barrier((payload, hidden_parts, low))
    early = lax.all_to_all(payload[0], "space", 0, 0, tiled=True, axis_index_groups=ALONG_Z)
    hidden, grad, g_inner, g_outer = middle(pre, low, high, hidden_parts)

    h_others = gather_chan(hidden)
    g_inner, g_outer = swap_halo(g_inner, g_outer)
    h_others, g_inner, early = lax.optimization_barrier((h_others, g_inner, early))
    early = with_far(early)
    input_parts, g_three = conv_t(grad, g_inner, g_outer, w_one, True)
    result, low, high, payload = conv(hidden, h_others, w_two, g_three, False)
    late = jnp.stack(exchange_z(payload))
    low, high = swap_halo(low, high)
    input_parts, low = lax.optimization_barrier((input_parts, low))
    input_parts = lax.all_to_all(input_parts[0], "chan", 0, 0, tiled=True)
    late, input_parts, low, high = lax.optimization_barrier((late, input_parts, low, high))
    late = with_far(late)
    grad_one = last(scatter_x(wprod(False, early, late)))
    grad_two = last(scatter_x(wprod(True, late, early)))
    input_grad = jnp.sum(input_parts.astype(F32), axis=0)
    return (
        channels_major(add_halo(result, low, high)),
        channels_major(input_grad),
        grad_one,
        grad_two,
    )


def solution(mesh):
    placed = (
        P("chan", "space", None, None),
        P(None, None, "chan"),
        P(None, None, "chan"),
        P("chan", "space", None, None),
    )
    return jax.shard_map(
        body,
        mesh=mesh,
        in_specs=placed,
        out_specs=(
            P("chan", "space", None, None),
            P("chan", "space", None, None),
            P("space", None, "chan"),
            P("space", None, "chan"),
        ),
        check_vma=False,
    )
```

time: 122 us -> 107 us (0.88)
  local copies, waits for them, and re-layouts: 15.7 us -> 8.77 us
  waiting for transfers between devices: 29 us -> 23.3 us
  starting transfers between devices: 56.3 us -> 52.1 us
  Pallas kernels: 16.5 us -> 18.4 us
    pallas_call x0 -> x6, Pallas kernels: none -> 15.8 us  [the longest x2 7.95 us: wprod(): pl.pallas_call(functools.partial(wprod_kernel, late_v), out_shape=(shape(...]
    pallas_call x11 -> x3, Pallas kernels: 16.5 us -> 2.63 us  [call(): pl.pallas_call(kernel, out_shape=tuple(out_shapes), in_specs=[pl.BlockSpe...]
    ppermute x16 -> x11, starting transfers between devices: 31.8 us -> 18.9 us  [the longest x6 9.54 us: scatter_x(): lax.ppermute(parts[step], 'space', over_x(step))]
    all_to_all x0 -> x2, starting transfers between devices: none -> 10.1 us  [the longest x1 6.01 us: body(): lax.all_to_all(payload[0], 'space', 0, 0, tiled=True, axis_index_groups=A...]
    ppermute x16 -> x11, waiting for transfers between devices: 17.8 us -> 9.85 us  [the longest x3 5.59 us: exchange_z(): lax.ppermute(parts[step], 'space', over_z(step))]
    all_to_all x0 -> x2, waiting for transfers between devices: none -> 6.6 us  [the longest x1 5.57 us: body(): lax.all_to_all(payload[0], 'space', 0, 0, tiled=True, axis_index_groups=A...]
    ppermute x6 -> x3, waiting for transfers between devices: 10.9 us -> 5.34 us  [scatter_chan(): lax.ppermute(parts[step], 'chan', over_chan(step))]
    ppermute x6 -> x3, starting transfers between devices: 8.88 us -> 4.78 us  [scatter_chan(): lax.ppermute(parts[step], 'chan', over_chan(step))]
  transfers between devices with their start and end apart: 36 -> 30, of which waited for: 8 -> 10; matrix products, arithmetic and copies ran while one was open for 7% -> 5% of each run, Pallas kernels for 13% -> 9%
where the time goes in v2:
time: 107 us; the launch traced here: 106 us
  starting transfers between devices  52.1 us (49%)
  waiting for transfers between devices  23.3 us (22%)
  Pallas kernels  18.4 us (17%)
  local copies, waits for them, and re-layouts  8.77 us (8%)
  other arithmetic  2.5 us (2%)
    ppermute x6, starting transfers between devices, gather_chan(): return [lax.ppermute(block, 'chan', over_chan(step)) for step in (1, 2, 3)]  9.55 us
    ppermute x6, starting transfers between devices, scatter_x(): lax.ppermute(parts[step], 'space', over_x(step))  9.54 us
    pallas_call x2, Pallas kernels, wprod(): pl.pallas_call(functools.partial(wprod_kernel, late_v), out_shape=(shape(...  7.95 us
    ppermute x3, starting transfers between devices, exchange_z(): lax.ppermute(parts[step], 'space', over_z(step))  7.89 us
    pallas_call x4, Pallas kernels, layer_call(): pl.pallas_call(kernel, out_shape=tuple(outs), in_specs=[vmem_spec] * (len...  7.8 us
    ppermute x4, starting transfers between devices, swap_halo(): lax.ppermute(inner, 'space', CORES)  6.08 us
    all_to_all x1, starting transfers between devices, body(): lax.all_to_all(payload[0], 'space', 0, 0, tiled=True, axis_index_groups=A...  6.01 us
    unnamed x15, local copies, waits for them, and re-layouts  5.75 us
  transfers between devices with their start and end apart: 30, of which 10 were waited for; matrix products, arithmetic and copies ran while one was open for 5% of the time, Pallas kernels for 9%

profile of v2, /device:TPU:0, one launch (start us, length us, event | category | flops | bytes accessed | tf_op | source)
XLA Modules:
  0.0 106.0 jit_solution(251588451754195607)
XLA Ops:
  0.6 1.1 %copy.12 = bf16[2,128,2,128]{3,2,1,0:T(2,128)(2,1)S(1)} copy(bf16[2,128,2,128]{1,2,0,3:T(2,128)(2,1)} %bitcast.38) | data formatting | bytes 262144 | tf_op jit(solution)/shard_map/transpose | solution.py:306
  1.8 0.1 collective-permute-start.3
  1.9 0.7 collective-permute-start.4
  2.6 1.1 %copy.11 = bf16[2,128,2,128]{3,2,1,0:T(2,128)(2,1)S(1)} copy(bf16[2,128,2,128]{1,2,0,3:T(2,128)(2,1)} %bitcast.39) | data formatting | bytes 262144 | tf_op jit(solution)/shard_map/transpose | solution.py:306
  3.7 1.7 %collective-permute-start = (bf16[256,256]{1,0:T(8,128)(2,1)S(1)}, bf16[256,256]{1,0:T(8,128)(2,1)S(1)}, u32[]{:S(2)}, u32[]{:S(2)}) collective-permute-start(bf16[256,256]{1,0:T(8,128)(2,1)S(1)} %bitcast.25), channel_id=1, source_target_pairs={{0,1},{1,0},{2,3},{3,2},{4,5},{5,4},{6,7},{7,6},{8,9},{9,8},{10,11... | collective-permute-start | bytes 393224 | tf_op jit(solution)/shard_map/ppermute | solution.py:314
  5.4 2.9 %collective-permute-start.1 = (bf16[256,256]{1,0:T(8,128)(2,1)S(1)}, bf16[256,256]{1,0:T(8,128)(2,1)S(1)}, u32[]{:S(2)}, u32[]{:S(2)}) collective-permute-start(bf16[256,256]{1,0:T(8,128)(2,1)S(1)} %bitcast.26), channel_id=1, source_target_pairs={{0,2},{1,3},{2,0},{3,1},{4,6},{5,7},{6,4},{7,5},{8,10},{9,11},{10,... | collective-permute-start | bytes 393224 | tf_op jit(solution)/shard_map/ppermute | solution.py:314
  8.3 0.1 collective-permute-start.2
  8.4 0.0 collective-permute-done.4.outer
  8.5 2.0 %copy-done.2 = bf16[512,27,128]{2,0,1:T(8,128)(2,1)S(1)} copy-done((bf16[512,27,128]{2,0,1:T(8,128)(2,1)S(1)}, bf16[512,27,128]{2,0,1:T(8,128)(2,1)}, u32[]{:S(2)}) %copy-start.2) | copy-done | bytes 3538968
  10.5 1.4 %shard_map.75 = (f32[256,256]{1,0:T(8,128)S(1)}, bf16[256,256]{1,0:T(8,128)(2,1)S(1)}, bf16[256,256]{1,0:T(8,128)(2,1)S(1)}, bf16[256,256]{1,0:T(8,128)(2,1)S(1)}, bf16[384,256]{1,0:T(8,128)(2,1)S(1)}) custom-call(bf16[256,256]{1,0:T(8,128)(2,1)S(1)} %bitcast.23, bf16[128,256]{1,0:T(8,128)(2,1)S(1)} %collective-permute-done.3.inner, ...), custom_call_target="tpu_custom_call" | custom-call | flops 1207959552 | bytes 5242880 | tf_op jit(solution)/shard_map/pallas_call | solution.py:54
  11.9 0.5 collective-permute-start.5
  12.4 4.1 %collective-permute-start.6 = (bf16[256,256]{1,0:T(8,128)(2,1)S(1)}, bf16[256,256]{1,0:T(8,128)(2,1)S(1)}, u32[]{:S(2)}, u32[]{:S(2)}) collective-permute-start(bf16[256,256]{1,0:T(8,128)(2,1)S(1)} %get-tuple-element.56), channel_id=1, source_target_pairs={{0,2},{1,3},{2,0},{3,1},{4,6},{5,7},{6,4},{7,5},{8,10},{9,11},{10,... | collective-permute-start | bytes 393224 | tf_op jit(solution)/shard_map/ppermute | solution.py:319
  16.5 0.1 collective-permute-start.7
  16.7 0.0 collective-permute-done.1.r2
  16.7 0.0 collective-permute-done.2.r3
  16.7 2.6 %shard_map.76 = (f32[256,256]{1,0:T(8,128)S(1)}, bf16[128,256]{1,0:T(8,128)(2,1)S(1)}, bf16[128,256]{1,0:T(8,128)(2,1)S(1)}, bf16[4,640,256]{2,1,0:T(8,128)(2,1)}) custom-call(bf16[256,256]{1,0:T(8,128)(2,1)S(1)} %bitcast.28, bf16[256,256]{1,0:T(8,128)(2,1)S(1)} %collective-permute-done.r1, bf16[256,256]{1,0:T(8,128)(2,1)S(1)} %collective-permute-done.1.r2, ...), custom_call_target="tpu_custom_call" | custom-call | flops 1207959552 | bytes 5242880 | tf_op jit(solution)/shard_map/pallas_call | solution.py:54
  19.3 1.3 %collective-permute-start.8 = (bf16[128,256]{1,0:T(8,128)(2,1)S(1)}, bf16[128,256]{1,0:T(8,128)(2,1)S(1)}, u32[]{:S(2)}, u32[]{:S(2)}) collective-permute-start(bf16[128,256]{1,0:T(8,128)(2,1)S(1)} %get-tuple-element.58), channel_id=1, source_target_pairs={{0,4},{4,0},{8,12},{12,8},{16,20},{20,16},{24,28},{28,24},{32,36},... | collective-permute-start | bytes 196616 | tf_op jit(solution)/shard_map/ppermute | solution.py:302
  20.6 2.1 %collective-permute-done.6.g2 = bf16[256,256]{1,0:T(8,128)(2,1)S(1)} collective-permute-done((bf16[256,256]{1,0:T(8,128)(2,1)S(1)}, bf16[256,256]{1,0:T(8,128)(2,1)S(1)}, u32[]{:S(2)}, u32[]{:S(2)}) %collective-permute-start.6) | collective-permute-done | bytes 131104 | tf_op jit(solution)/shard_map/ppermute | solution.py:319
  22.7 3.2 %collective-permute-done.7.g3 = bf16[256,256]{1,0:T(8,128)(2,1)S(1)} collective-permute-done((bf16[256,256]{1,0:T(8,128)(2,1)S(1)}, bf16[256,256]{1,0:T(8,128)(2,1)S(1)}, u32[]{:S(2)}, u32[]{:S(2)}) %collective-permute-start.7) | collective-permute-done | bytes 131104 | tf_op jit(solution)/shard_map/ppermute | solution.py:319
  25.9 6.0 %all-to-all-start = ((bf16[4,640,256]{2,1,0:T(8,128)(2,1)}), bf16[4,640,256]{2,1,0:T(8,128)(2,1)S(1)}, u32[]{:S(2)}, u32[]{:S(2)}) async-start(bf16[4,640,256]{2,1,0:T(8,128)(2,1)} %get-tuple-element.67), calls=%async_computation | async-start | bytes 2621440 | tf_op jit(solution)/shard_map/all_to_all | solution.py:361
  31.9 0.7 collective-permute-start.9
  32.6 0.2 shard_map.77
  32.8 0.1 collective-permute-start.10
  32.9 2.4 %collective-permute-start.11 = (bf16[256,256]{1,0:T(8,128)(2,1)S(1)}, bf16[256,256]{1,0:T(8,128)(2,1)S(1)}, u32[]{:S(2)}, u32[]{:S(2)}) collective-permute-start(bf16[256,256]{1,0:T(8,128)(2,1)S(1)} %get-tuple-element.65.own), channel_id=1, source_target_pairs={{0,2},{1,3},{2,0},{3,1},{4,6},{5,7},{6,4},{7,5},{8,10},{9,11},{10,... | collective-permute-start | bytes 393224 | tf_op jit(solution)/shard_map/ppermute | solution.py:314
  35.3 2.3 %collective-permute-start.12 = (bf16[256,256]{1,0:T(8,128)(2,1)S(1)}, bf16[256,256]{1,0:T(8,128)(2,1)S(1)}, u32[]{:S(2)}, u32[]{:S(2)}) collective-permute-start(bf16[256,256]{1,0:T(8,128)(2,1)S(1)} %get-tuple-element.65.own), channel_id=1, source_target_pairs={{0,3},{1,2},{2,1},{3,0},{4,7},{5,6},{6,5},{7,4},{8,11},{9,10},{10,... | collective-permute-start | bytes 393224 | tf_op jit(solution)/shard_map/ppermute | solution.py:314
  37.6 4.7 %collective-permute-start.13 = (bf16[128,256]{1,0:T(8,128)(2,1)S(1)}, bf16[128,256]{1,0:T(8,128)(2,1)S(1)}, u32[]{:S(2)}, u32[]{:S(2)}) collective-permute-start(bf16[128,256]{1,0:T(8,128)(2,1)S(1)} %get-tuple-element.66), channel_id=1, source_target_pairs={{0,4},{4,0},{8,12},{12,8},{16,20},{20,16},{24,28},{28,24},{32,36},... | collective-permute-start | bytes 196616 | tf_op jit(solution)/shard_map/ppermute | solution.py:302
  42.3 0.7 collective-permute-start.14
  42.9 0.2 collective-permute-done.13.inner
  43.2 0.0 collective-permute-done.10.r1
  43.2 0.0 collective-permute-done.11.r2
  43.2 0.0 collective-permute-done.12.r3
  43.2 0.0 copy-start.4
  43.2 5.6 %all-to-all-done.v.d = bf16[4,640,256]{2,1,0:T(8,128)(2,1)S(1)} async-done(((bf16[4,640,256]{2,1,0:T(8,128)(2,1)}), bf16[4,640,256]{2,1,0:T(8,128)(2,1)S(1)}, u32[]{:S(2)}, u32[]{:S(2)}) %all-to-all-start) | async-done | bytes 1310752 | tf_op jit(solution)/shard_map/all_to_all | solution.py:361
  48.8 2.0 %copy-done.1 = bf16[512,27,128]{2,0,1:T(8,128)(2,1)S(1)} copy-done((bf16[512,27,128]{2,0,1:T(8,128)(2,1)S(1)}, bf16[512,27,128]{2,0,1:T(8,128)(2,1)}, u32[]{:S(2)}) %copy-start.1) | copy-done | bytes 3538968
  50.8 2.2 %shard_map.78 = (bf16[4,256,256]{2,1,0:T(8,128)(2,1)}, bf16[384,256]{1,0:T(8,128)(2,1)S(1)}) custom-call(bf16[256,256]{1,0:T(8,128)(2,1)S(1)} %get-tuple-element.71.own, bf16[128,256]{1,0:T(8,128)(2,1)S(1)} %collective-permute-done.13.inner, bf16[128,256]{1,0:T(8,128)(2,1)S(1)} %collective-permute-done.14.outer, bf16[27,512,128]{2,1,0:T(8,128)(2,1)S(1)} %bitcast.30), custom_call_target="tpu_custom_call" | custom-call | flops 1207959552 | bytes 5242880 | tf_op jit(solution)/shard_map/pallas_call | solution.py:54
  53.0 0.9 copy-done.5
  53.9 1.6 %shard_map.79 = (f32[256,256]{1,0:T(8,128)S(1)}, bf16[128,256]{1,0:T(8,128)(2,1)S(1)}, bf16[128,256]{1,0:T(8,128)(2,1)S(1)}, bf16[640,256]{1,0:T(8,128)(2,1)S(1)...) custom-call(bf16[256,256]{1,0:T(8,128)(2,1)S(1)} %get-tuple-element.65.own, ...), custom_call_target="tpu_custom_call" | custom-call | flops 1207959552 | bytes 5242880 | tf_op jit(solution)/shard_map/pallas_call | solution.py:54
  55.5 6.9 %collective-permute-start.17 = (bf16[640,256]{1,0:T(8,128)(2,1)S(1)}, bf16[640,256]{1,0:T(8,128)(2,1)}, u32[]{:S(2)}, u32[]{:S(2)}) collective-permute-start(bf16[640,256]{1,0:T(8,128)(2,1)S(1)} %get-tuple-element.79), channel_id=1, source_target_pairs={{0,96},{4,100},{8,104},{12,108},{16,112},{20,116},{24,120},{28,124... | collective-permute-start | bytes 983048 | tf_op jit(solution)/shard_map/ppermute | solution.py:331
  62.4 0.9 collective-permute-start.16
  63.3 0.1 collective-permute-start.15
  63.4 1.3 %collective-permute-done.18 = bf16[128,256]{1,0:T(8,128)(2,1)S(1)} collective-permute-done((bf16[128,256]{1,0:T(8,128)(2,1)S(1)}, bf16[128,256]{1,0:T(8,128)(2,1)S(1)}, u32[]{:S(2)}, u32[]{:S(2)}) %collective-permute-start.18) | collective-permute-done | bytes 65568 | tf_op jit(solution)/shard_map/ppermute | solution.py:302
  64.6 4.1 %all-to-all-start.1 = ((bf16[4,256,256]{2,1,0:T(8,128)(2,1)}), bf16[4,256,256]{2,1,0:T(8,128)(2,1)}, u32[]{:S(2)}, u32[]{:S(2)}) async-start(bf16[4,256,256]{2,1,0:T(8,128)(2,1)} %get-tuple-element.82), calls=%async_computation.1 | async-start | bytes 1048576 | tf_op jit(solution)/shard_map/all_to_all | solution.py:373
  68.8 0.7 collective-permute-start.19
  69.5 1.5 %collective-permute-start.20 = (bf16[4,640,256]{2,1,0:T(8,128)(2,1)S(1)}, bf16[4,640,256]{2,1,0:T(8,128)(2,1)}, u32[]{:S(2)}, u32[]{:S(2)}) collective-permute-start(bf16[4,640,256]{2,1,0:T(8,128)(2,1)S(1)} %all-to-all-done.v.d), channel_id=1, source_target_pairs={{0,4},{4,0},{8,12},{12,8},{16,20},{20,16},{24,28},{28,24},{32,36},... | collective-permute-start | bytes 3932168 | tf_op jit(solution)/shard_map/ppermute | solution.py:335
  71.0 4.9 %collective-permute-done.17 = bf16[640,256]{1,0:T(8,128)(2,1)} collective-permute-done((bf16[640,256]{1,0:T(8,128)(2,1)S(1)}, bf16[640,256]{1,0:T(8,128)(2,1)}, u32[]{:S(2)}, u32[]{:S(2)}) %collective-permute-start.17) | collective-permute-done | bytes 327712 | tf_op jit(solution)/shard_map/ppermute | solution.py:331
  75.8 0.7 collective-permute-done.15
  76.5 1.3 %pad_maximum_fusion.d.v = bf16[4,640,256]{2,1,0:T(8,128)(2,1)S(1)} fusion(bf16[1,640,256]{2,1,0:T(8,128)(2,1)} %bitcast.7, bf16[1,640,256]{2,1,0:T(8,128)(2,1)} %bitcast.6, bf16[1,640,256]{2,1,0:T(8,128)(2,1)} %bitcast.5, bf16[1,640,256]{2,1,0:T(8,128)(2,1)S(1)} %bitcast.24), kind=kLoop, calls=%fused_computation | loop fusion | flops 1966080 | bytes 2621440 | tf_op jit(solution)/shard_map/stack | solution.py:370
  77.9 1.0 all-to-all-done.1
  78.9 0.0 collective-permute-start.21
  79.0 3.1 %collective-permute-done.21.d_far.v_far = bf16[4,640,256]{2,1,0:T(8,128)(2,1)} collective-permute-done((bf16[4,640,256]{2,1,0:T(8,128)(2,1)S(1)}, bf16[4,640,256]{2,1,0:T(8,128)(2,1)}, u32[]{:S(2)}, u32[]{:S(2)}) %collective-permute-start.21) | collective-permute-done | bytes 1310752 | tf_op jit(solution)/shard_map/ppermute | solution.py:335
  82.1 4.0 %shard_map.80 = (f32[9,16,384]{2,1,0:T(8,128)S(1)}, bf16[9,16,384]{2,1,0:T(8,128)(2,1)S(1)}, bf16[9,16,384]{2,1,0:T(8,128)(2,1)}, bf16[9,16,384]{2,1,0:T(8,128)(2,1)}) custom-call(bf16[4,640,256]{2,1,0:T(8,128)(2,1)S(1)} %all-to-all-done.v.d, bf16[4,640,256]{2,1,0:T(8,128)(2,1)} %collective-permute-done.20.v_far.d_far, ...), custom_call_target="tpu_custom_call" | custom-call | flops 1207959552 | bytes 4194304 | tf_op jit(solution)/shard_map/pallas_call | solution.py:247
  86.1 0.1 collective-permute-start.22
  86.2 3.9 %collective-permute-start.23 = (bf16[9,16,384]{2,1,0:T(8,128)(2,1)}, bf16[9,16,384]{2,1,0:T(8,128)(2,1)}, u32[]{:S(2)}, u32[]{:S(2)}) collective-permute-start(bf16[9,16,384]{2,1,0:T(8,128)(2,1)} %get-tuple-element.92), channel_id=1, source_target_pairs={{0,16},{4,20},{8,24},{12,28},{16,0},{20,4},{24,8},{28,12},{32,48},... | collective-permute-start | bytes 331784 | tf_op jit(solution)/shard_map/ppermute | solution.py:324
  90.0 0.8 collective-permute-start.24
  90.8 4.0 %shard_map.82 = (f32[9,16,384]{2,1,0:T(8,128)S(1)}, bf16[9,16,384]{2,1,0:T(8,128)(2,1)}, bf16[9,16,384]{2,1,0:T(8,128)(2,1)}, bf16[9,16,384]{2,1,0:T(8,128)(2,1)}) custom-call(bf16[4,640,256]{2,1,0:T(8,128)(2,1)S(1)} %pad_maximum_fusion.d.v, bf16[4,640,256]{2,1,0:T(8,128)(2,1)} %collective-permute-done.21.d_far.v_far, ...), custom_call_target="tpu_custom_call" | custom-call | flops 1207959552 | bytes 4194304 | tf_op jit(solution)/shard_map/pallas_call | solution.py:247
  94.8 0.1 collective-permute-start.25
  94.9 3.9 %collective-permute-start.26 = (bf16[9,16,384]{2,1,0:T(8,128)(2,1)}, bf16[9,16,384]{2,1,0:T(8,128)(2,1)S(1)}, u32[]{:S(2)}, u32[]{:S(2)}) collective-permute-start(bf16[9,16,384]{2,1,0:T(8,128)(2,1)} %get-tuple-element.96), channel_id=1, source_target_pairs={{0,16},{4,20},{8,24},{12,28},{16,0},{20,4},{24,8},{28,12},{32,48},... | collective-permute-start | bytes 331784 | tf_op jit(solution)/shard_map/ppermute | solution.py:324
  98.8 0.8 collective-permute-start.27
  99.7 0.8 copy.13
  100.5 1.1 %reduce_sum.12 = bf16[256,256]{1,0:T(8,128)(2,1)S(1)} reduce(bf16[4,256,256]{2,1,0:T(8,128)(2,1)} %all-to-all-done.1, bf16[]{:T(256)} %constant.29.clone.1), dimensions={0}, to_apply=%region_0.1 | reduce | flops 196608 | bytes 655362 | tf_op jit(solution)/shard_map/reduce_sum | solution.py:378
  101.7 0.8 copy.14
  102.4 1.7 %shard_map.81 = f32[27,16,128]{2,1,0:T(8,128)} custom-call(f32[9,16,384]{2,1,0:T(8,128)S(1)} %get-tuple-element.90.own, bf16[9,16,384]{2,1,0:T(8,128)(2,1)S(1)} %collective-permute-done.22.r1, bf16[9,16,384]{2,1,0:T(8,128)(2,1)} %collective-permute-done.23.r2, bf16[9,16,384]{2,1,0:T(8,128)(2,1)} %collective-permute-done.24.r3), custom_call_target="tpu_custom_call" | custom-call | bytes 774144 | tf_op jit(solution)/shard_map/pallas_call | solution.py:24
  104.1 1.1 %collective-permute-done.27.r3 = bf16[9,16,384]{2,1,0:T(8,128)(2,1)S(1)} collective-permute-done((bf16[9,16,384]{2,1,0:T(8,128)(2,1)}, bf16[9,16,384]{2,1,0:T(8,128)(2,1)S(1)}, u32[]{:S(2)}, u32[]{:S(2)}) %collective-permute-start.27) | collective-permute-done | bytes 110624 | tf_op jit(solution)/shard_map/ppermute | solution.py:324
  105.3 0.7 shard_map.83
  (30 shorter events, 0.2 us)
Async XLA Ops:
  1.8 6.7 %collective-permute-start.3 = (bf16[128,256]{1,0:T(8,128)(2,1)S(1)}, bf16[128,256]{1,0:T(8,128)(2,1)S(1)}, u32[]{:S(2)}, u32[]{:S(2)}) collective-permute-start(bf16[128,256]{1,0:T(8,128)(2,1)S(1)} %get-tuple-element.105), channel_id=1, source_target_pairs={{0,4},{4,0},{8,12},{12,8},{16,20},{20,16},{24,28},{28,24},{32,36},... | collective-permute-start | bytes 196616 | tf_op jit(solution)/shard_map/ppermute | solution.py:302
  1.9 6.6 %collective-permute-start.4 = (bf16[128,256]{1,0:T(8,128)(2,1)S(1)}, bf16[128,256]{1,0:T(8,128)(2,1)S(1)}, u32[]{:S(2)}, u32[]{:S(2)}) collective-permute-start(bf16[128,256]{1,0:T(8,128)(2,1)S(1)} %get-tuple-element.104), channel_id=1, source_target_pairs={{4,8},{8,4},{12,16},{16,12},{20,24},{24,20},{28,32},{32,28},{36,40... | collective-permute-start | bytes 196616 | tf_op jit(solution)/shard_map/ppermute | solution.py:302
  3.7 12.9 %collective-permute-start = (bf16[256,256]{1,0:T(8,128)(2,1)S(1)}, bf16[256,256]{1,0:T(8,128)(2,1)S(1)}, u32[]{:S(2)}, u32[]{:S(2)}) collective-permute-start(bf16[256,256]{1,0:T(8,128)(2,1)S(1)} %bitcast.25), channel_id=1, source_target_pairs={{0,1},{1,0},{2,3},{3,2},{4,5},{5,4},{6,7},{7,6},{8,9},{9,8},{10,11... | collective-permute-start | bytes 393224 | tf_op jit(solution)/shard_map/ppermute | solution.py:314
  5.4 11.3 %collective-permute-start.1 = (bf16[256,256]{1,0:T(8,128)(2,1)S(1)}, bf16[256,256]{1,0:T(8,128)(2,1)S(1)}, u32[]{:S(2)}, u32[]{:S(2)}) collective-permute-start(bf16[256,256]{1,0:T(8,128)(2,1)S(1)} %bitcast.26), channel_id=1, source_target_pairs={{0,2},{1,3},{2,0},{3,1},{4,6},{5,7},{6,4},{7,5},{8,10},{9,11},{10,... | collective-permute-start | bytes 393224 | tf_op jit(solution)/shard_map/ppermute | solution.py:314
  8.3 8.4 %collective-permute-start.2 = (bf16[256,256]{1,0:T(8,128)(2,1)S(1)}, bf16[256,256]{1,0:T(8,128)(2,1)S(1)}, u32[]{:S(2)}, u32[]{:S(2)}) collective-permute-start(bf16[256,256]{1,0:T(8,128)(2,1)S(1)} %bitcast.27), channel_id=1, source_target_pairs={{0,3},{1,2},{2,1},{3,0},{4,7},{5,6},{6,5},{7,4},{8,11},{9,10},{10,... | collective-permute-start | bytes 393224 | tf_op jit(solution)/shard_map/ppermute | solution.py:314
  8.5 2.0 %copy-start.2 = (bf16[512,27,128]{2,0,1:T(8,128)(2,1)S(1)}, bf16[512,27,128]{2,0,1:T(8,128)(2,1)}, u32[]{:S(2)}) copy-start(bf16[512,27,128]{2,0,1:T(8,128)(2,1)} %param.6) | copy-start | bytes 10616836
  10.5 6.2 %copy-start = (bf16[512,27,128]{2,0,1:T(8,128)(2,1)S(1)}, bf16[512,27,128]{2,0,1:T(8,128)(2,1)}, u32[]{:S(2)}) copy-start(bf16[512,27,128]{2,0,1:T(8,128)(2,1)} %param.5) | copy-start | bytes 10616836
  11.9 8.7 %collective-permute-start.5 = (bf16[256,256]{1,0:T(8,128)(2,1)S(1)}, bf16[256,256]{1,0:T(8,128)(2,1)S(1)}, u32[]{:S(2)}, u32[]{:S(2)}) collective-permute-start(bf16[256,256]{1,0:T(8,128)(2,1)S(1)} %get-tuple-element.55), channel_id=1, source_target_pairs={{0,1},{1,0},{2,3},{3,2},{4,5},{5,4},{6,7},{7,6},{8,9},{9,8},{10,11... | collective-permute-start | bytes 393224 | tf_op jit(solution)/shard_map/ppermute | solution.py:319
  12.4 10.3 %collective-permute-start.6 = (bf16[256,256]{1,0:T(8,128)(2,1)S(1)}, bf16[256,256]{1,0:T(8,128)(2,1)S(1)}, u32[]{:S(2)}, u32[]{:S(2)}) collective-permute-start(bf16[256,256]{1,0:T(8,128)(2,1)S(1)} %get-tuple-element.56), channel_id=1, source_target_pairs={{0,2},{1,3},{2,0},{3,1},{4,6},{5,7},{6,4},{7,5},{8,10},{9,11},{10,... | collective-permute-start | bytes 393224 | tf_op jit(solution)/shard_map/ppermute | solution.py:319
  16.5 9.4 %collective-permute-start.7 = (bf16[256,256]{1,0:T(8,128)(2,1)S(1)}, bf16[256,256]{1,0:T(8,128)(2,1)S(1)}, u32[]{:S(2)}, u32[]{:S(2)}) collective-permute-start(bf16[256,256]{1,0:T(8,128)(2,1)S(1)} %get-tuple-element.57), channel_id=1, source_target_pairs={{0,3},{1,2},{2,1},{3,0},{4,7},{5,6},{6,5},{7,4},{8,11},{9,10},{10,... | collective-permute-start | bytes 393224 | tf_op jit(solution)/shard_map/ppermute | solution.py:319
  19.3 6.7 %collective-permute-start.8 = (bf16[128,256]{1,0:T(8,128)(2,1)S(1)}, bf16[128,256]{1,0:T(8,128)(2,1)S(1)}, u32[]{:S(2)}, u32[]{:S(2)}) collective-permute-start(bf16[128,256]{1,0:T(8,128)(2,1)S(1)} %get-tuple-element.58), channel_id=1, source_target_pairs={{0,4},{4,0},{8,12},{12,8},{16,20},{20,16},{24,28},{28,24},{32,36},... | collective-permute-start | bytes 196616 | tf_op jit(solution)/shard_map/ppermute | solution.py:302
  25.9 22.8 %all-to-all-start = ((bf16[4,640,256]{2,1,0:T(8,128)(2,1)}), bf16[4,640,256]{2,1,0:T(8,128)(2,1)S(1)}, u32[]{:S(2)}, u32[]{:S(2)}) async-start(bf16[4,640,256]{2,1,0:T(8,128)(2,1)} %get-tuple-element.67), calls=%async_computation | async-start | bytes 2621440 | tf_op jit(solution)/shard_map/all_to_all | solution.py:361
  31.9 0.7 collective-permute-start.9
  32.8 10.3 %collective-permute-start.10 = (bf16[256,256]{1,0:T(8,128)(2,1)S(1)}, bf16[256,256]{1,0:T(8,128)(2,1)S(1)}, u32[]{:S(2)}, u32[]{:S(2)}) collective-permute-start(bf16[256,256]{1,0:T(8,128)(2,1)S(1)} %get-tuple-element.65.own), channel_id=1, source_target_pairs={{0,1},{1,0},{2,3},{3,2},{4,5},{5,4},{6,7},{7,6},{8,9},{9,8},{10,11... | collective-permute-start | bytes 393224 | tf_op jit(solution)/shard_map/ppermute | solution.py:314
  32.9 10.3 %collective-permute-start.11 = (bf16[256,256]{1,0:T(8,128)(2,1)S(1)}, bf16[256,256]{1,0:T(8,128)(2,1)S(1)}, u32[]{:S(2)}, u32[]{:S(2)}) collective-permute-start(bf16[256,256]{1,0:T(8,128)(2,1)S(1)} %get-tuple-element.65.own), channel_id=1, source_target_pairs={{0,2},{1,3},{2,0},{3,1},{4,6},{5,7},{6,4},{7,5},{8,10},{9,11},{10,... | collective-permute-start | bytes 393224 | tf_op jit(solution)/shard_map/ppermute | solution.py:314
  35.3 7.9 %collective-permute-start.12 = (bf16[256,256]{1,0:T(8,128)(2,1)S(1)}, bf16[256,256]{1,0:T(8,128)(2,1)S(1)}, u32[]{:S(2)}, u32[]{:S(2)}) collective-permute-start(bf16[256,256]{1,0:T(8,128)(2,1)S(1)} %get-tuple-element.65.own), channel_id=1, source_target_pairs={{0,3},{1,2},{2,1},{3,0},{4,7},{5,6},{6,5},{7,4},{8,11},{9,10},{10,... | collective-permute-start | bytes 393224 | tf_op jit(solution)/shard_map/ppermute | solution.py:314
  37.6 5.6 %collective-permute-start.13 = (bf16[128,256]{1,0:T(8,128)(2,1)S(1)}, bf16[128,256]{1,0:T(8,128)(2,1)S(1)}, u32[]{:S(2)}, u32[]{:S(2)}) collective-permute-start(bf16[128,256]{1,0:T(8,128)(2,1)S(1)} %get-tuple-element.66), channel_id=1, source_target_pairs={{0,4},{4,0},{8,12},{12,8},{16,20},{20,16},{24,28},{28,24},{32,36},... | collective-permute-start | bytes 196616 | tf_op jit(solution)/shard_map/ppermute | solution.py:302
  42.3 6.5 %collective-permute-start.14 = (bf16[128,256]{1,0:T(8,128)(2,1)S(1)}, bf16[128,256]{1,0:T(8,128)(2,1)S(1)}, u32[]{:S(2)}, u32[]{:S(2)}) collective-permute-start(bf16[128,256]{1,0:T(8,128)(2,1)S(1)} %get-tuple-element.73), channel_id=1, source_target_pairs={{4,8},{8,4},{12,16},{16,12},{20,24},{24,20},{28,32},{32,28},{36,40... | collective-permute-start | bytes 196616 | tf_op jit(solution)/shard_map/ppermute | solution.py:302
  43.2 9.8 %copy-start.4 = (bf16[256,256]{1,0:T(8,128)(2,1)}, bf16[256,256]{1,0:T(8,128)(2,1)S(1)}, u32[]{:S(2)}) copy-start(bf16[256,256]{1,0:T(8,128)(2,1)S(1)} %collective-permute-done.12.r3) | copy-start | bytes 393220
  48.8 2.0 %copy-start.1 = (bf16[512,27,128]{2,0,1:T(8,128)(2,1)S(1)}, bf16[512,27,128]{2,0,1:T(8,128)(2,1)}, u32[]{:S(2)}) copy-start(bf16[512,27,128]{2,0,1:T(8,128)(2,1)} %param.5) | copy-start | bytes 10616836
  50.8 2.2 %copy-start.3 = (bf16[512,27,128]{2,0,1:T(8,128)(2,1)S(1)}, bf16[512,27,128]{2,0,1:T(8,128)(2,1)}, u32[]{:S(2)}) copy-start(bf16[512,27,128]{2,0,1:T(8,128)(2,1)} %param.6) | copy-start | bytes 10616836
  53.0 0.9 copy-start.5
  55.5 20.3 %collective-permute-start.17 = (bf16[640,256]{1,0:T(8,128)(2,1)S(1)}, bf16[640,256]{1,0:T(8,128)(2,1)}, u32[]{:S(2)}, u32[]{:S(2)}) collective-permute-start(bf16[640,256]{1,0:T(8,128)(2,1)S(1)} %get-tuple-element.79), channel_id=1, source_target_pairs={{0,96},{4,100},{8,104},{12,108},{16,112},{20,116},{24,120},{28,124... | collective-permute-start | bytes 983048 | tf_op jit(solution)/shard_map/ppermute | solution.py:331
  62.4 13.4 %collective-permute-start.16 = (bf16[640,256]{1,0:T(8,128)(2,1)S(1)}, bf16[640,256]{1,0:T(8,128)(2,1)}, u32[]{:S(2)}, u32[]{:S(2)}) collective-permute-start(bf16[640,256]{1,0:T(8,128)(2,1)S(1)} %get-tuple-element.78), channel_id=1, source_target_pairs={{0,64},{4,68},{8,72},{12,76},{16,80},{20,84},{24,88},{28,92},{32,9... | collective-permute-start | bytes 983048 | tf_op jit(solution)/shard_map/ppermute | solution.py:331
  63.3 13.3 %collective-permute-start.15 = (bf16[640,256]{1,0:T(8,128)(2,1)S(1)}, bf16[640,256]{1,0:T(8,128)(2,1)}, u32[]{:S(2)}, u32[]{:S(2)}) collective-permute-start(bf16[640,256]{1,0:T(8,128)(2,1)S(1)} %get-tuple-element.77), channel_id=1, source_target_pairs={{0,32},{4,36},{8,40},{12,44},{16,48},{20,52},{24,56},{28,60},{32,0... | collective-permute-start | bytes 983048 | tf_op jit(solution)/shard_map/ppermute | solution.py:331
  63.4 1.3 %collective-permute-start.18 = (bf16[128,256]{1,0:T(8,128)(2,1)S(1)}, bf16[128,256]{1,0:T(8,128)(2,1)S(1)}, u32[]{:S(2)}, u32[]{:S(2)}) collective-permute-start(bf16[128,256]{1,0:T(8,128)(2,1)S(1)} %get-tuple-element.81), channel_id=1, source_target_pairs={{0,4},{4,0},{8,12},{12,8},{16,20},{20,16},{24,28},{28,24},{32,36},... | collective-permute-start | bytes 196616 | tf_op jit(solution)/shard_map/ppermute | solution.py:302
  64.6 14.3 %all-to-all-start.1 = ((bf16[4,256,256]{2,1,0:T(8,128)(2,1)}), bf16[4,256,256]{2,1,0:T(8,128)(2,1)}, u32[]{:S(2)}, u32[]{:S(2)}) async-start(bf16[4,256,256]{2,1,0:T(8,128)(2,1)} %get-tuple-element.82), calls=%async_computation.1 | async-start | bytes 1048576 | tf_op jit(solution)/shard_map/all_to_all | solution.py:373
  68.8 9.1 %collective-permute-start.19 = (bf16[128,256]{1,0:T(8,128)(2,1)S(1)}, bf16[128,256]{1,0:T(8,128)(2,1)S(1)}, u32[]{:S(2)}, u32[]{:S(2)}) collective-permute-start(bf16[128,256]{1,0:T(8,128)(2,1)S(1)} %get-tuple-element.84), channel_id=1, source_target_pairs={{4,8},{8,4},{12,16},{16,12},{20,24},{24,20},{28,32},{32,28},{36,40... | collective-permute-start | bytes 196616 | tf_op jit(solution)/shard_map/ppermute | solution.py:302
  69.5 9.5 %collective-permute-start.20 = (bf16[4,640,256]{2,1,0:T(8,128)(2,1)S(1)}, bf16[4,640,256]{2,1,0:T(8,128)(2,1)}, u32[]{:S(2)}, u32[]{:S(2)}) collective-permute-start(bf16[4,640,256]{2,1,0:T(8,128)(2,1)S(1)} %all-to-all-done.v.d), channel_id=1, source_target_pairs={{0,4},{4,0},{8,12},{12,8},{16,20},{20,16},{24,28},{28,24},{32,36},... | collective-permute-start | bytes 3932168 | tf_op jit(solution)/shard_map/ppermute | solution.py:335
  78.9 3.2 %collective-permute-start.21 = (bf16[4,640,256]{2,1,0:T(8,128)(2,1)S(1)}, bf16[4,640,256]{2,1,0:T(8,128)(2,1)}, u32[]{:S(2)}, u32[]{:S(2)}) collective-permute-start(bf16[4,640,256]{2,1,0:T(8,128)(2,1)S(1)} %pad_maximum_fusion.d.v), channel_id=1, source_target_pairs={{0,4},{4,0},{8,12},{12,8},{16,20},{20,16},{24,28},{28,24},{32,36},... | collective-permute-start | bytes 3932168 | tf_op jit(solution)/shard_map/ppermute | solution.py:335
  86.1 12.7 %collective-permute-start.22 = (bf16[9,16,384]{2,1,0:T(8,128)(2,1)S(1)}, bf16[9,16,384]{2,1,0:T(8,128)(2,1)S(1)}, u32[]{:S(2)}, u32[]{:S(2)}) collective-permute-start(bf16[9,16,384]{2,1,0:T(8,128)(2,1)S(1)} %get-tuple-element.91), channel_id=1, source_target_pairs={{0,8},{4,12},{8,0},{12,4},{16,24},{20,28},{24,16},{28,20},{32,40},... | collective-permute-start | bytes 331784 | tf_op jit(solution)/shard_map/ppermute | solution.py:324
  86.2 16.3 %collective-permute-start.23 = (bf16[9,16,384]{2,1,0:T(8,128)(2,1)}, bf16[9,16,384]{2,1,0:T(8,128)(2,1)}, u32[]{:S(2)}, u32[]{:S(2)}) collective-permute-start(bf16[9,16,384]{2,1,0:T(8,128)(2,1)} %get-tuple-element.92), channel_id=1, source_target_pairs={{0,16},{4,20},{8,24},{12,28},{16,0},{20,4},{24,8},{28,12},{32,48},... | collective-permute-start | bytes 331784 | tf_op jit(solution)/shard_map/ppermute | solution.py:324
  90.0 12.4 %collective-permute-start.24 = (bf16[9,16,384]{2,1,0:T(8,128)(2,1)}, bf16[9,16,384]{2,1,0:T(8,128)(2,1)}, u32[]{:S(2)}, u32[]{:S(2)}) collective-permute-start(bf16[9,16,384]{2,1,0:T(8,128)(2,1)} %get-tuple-element.93), channel_id=1, source_target_pairs={{0,24},{4,28},{8,16},{12,20},{16,8},{20,12},{24,0},{28,4},{32,56},... | collective-permute-start | bytes 331784 | tf_op jit(solution)/shard_map/ppermute | solution.py:324
  94.8 9.3 %collective-permute-start.25 = (bf16[9,16,384]{2,1,0:T(8,128)(2,1)}, bf16[9,16,384]{2,1,0:T(8,128)(2,1)S(1)}, u32[]{:S(2)}, u32[]{:S(2)}) collective-permute-start(bf16[9,16,384]{2,1,0:T(8,128)(2,1)} %get-tuple-element.95), channel_id=1, source_target_pairs={{0,8},{4,12},{8,0},{12,4},{16,24},{20,28},{24,16},{28,20},{32,40},... | collective-permute-start | bytes 331784 | tf_op jit(solution)/shard_map/ppermute | solution.py:324
  94.9 9.2 %collective-permute-start.26 = (bf16[9,16,384]{2,1,0:T(8,128)(2,1)}, bf16[9,16,384]{2,1,0:T(8,128)(2,1)S(1)}, u32[]{:S(2)}, u32[]{:S(2)}) collective-permute-start(bf16[9,16,384]{2,1,0:T(8,128)(2,1)} %get-tuple-element.96), channel_id=1, source_target_pairs={{0,16},{4,20},{8,24},{12,28},{16,0},{20,4},{24,8},{28,12},{32,48},... | collective-permute-start | bytes 331784 | tf_op jit(solution)/shard_map/ppermute | solution.py:324
  98.8 6.5 %collective-permute-start.27 = (bf16[9,16,384]{2,1,0:T(8,128)(2,1)}, bf16[9,16,384]{2,1,0:T(8,128)(2,1)S(1)}, u32[]{:S(2)}, u32[]{:S(2)}) collective-permute-start(bf16[9,16,384]{2,1,0:T(8,128)(2,1)} %get-tuple-element.97), channel_id=1, source_target_pairs={{0,24},{4,28},{8,16},{12,20},{16,8},{20,12},{24,0},{28,4},{32,56},... | collective-permute-start | bytes 331784 | tf_op jit(solution)/shard_map/ppermute | solution.py:324

commit v3 on v2

--- a/solution.py
+++ b/solution.py
@@ -62,25 +62,49 @@
     )(*operands, weight)
 
 
-def conv_kernel(own, r1, r2, r3, three, weight, core_out, inner_out, outer_out, *rest):
-    *payload, field, turned = rest
+def pack_kernel(own, r1, r2, r3, grad, outer, *rest):
+    *payload, turned = rest
     y = lax.axis_index("chan")
     space = lax.axis_index("space")
-    first = space % 2 == 0
-    z = space // 8
+    first, z = space % 2 == 0, space // 8
+    mine, far = grad[...], outer[...]
+    three = jnp.where(
+        first, jnp.concatenate([far, mine], axis=0), jnp.concatenate([mine, far], axis=0)
+    )
     for step, part in enumerate((own, r1, r2, r3)):
-        place = y ^ step
+        turn(part[...], turned.at[y ^ step])
+    for step, out in enumerate(payload):
+        out[:256, :] = turned[z ^ step]
+        out[256:, :] = three
+
+
+def pack(own, others, grad, outer):
+    return call(
+        pack_kernel,
+        [shape((640, 256), BF16)] * 4,
+        (own, *others, grad, outer),
+        [pltpu.VMEM((4, 256, 256), BF16)],
+        flops=10**9,
+        vmem=8,
+    )
+
+
+def conv_kernel(own, r1, r2, r3, *rest):
+    y = lax.axis_index("chan")
+    first = lax.axis_index("space") % 2 == 0
+    if len(rest) == 5:
+        weight, core_out, inner_out, outer_out, field = rest
+    else:
+        three, weight, core_out, inner_out, outer_out, payload, field, turned = rest
+        for step, part in enumerate((own, r1, r2, r3)):
+            turn(part[...], turned.at[y ^ step])
+        for z in range(4):
+            payload[z, :256, :] = turned[z]
+            payload[z, 256:, :] = three[...]
+    for step, part in enumerate((own, r1, r2, r3)):
         for b in range(2):
-            at = pl.multiple_of(b * 512 + place * 128, 128)
+            at = pl.multiple_of(b * 512 + (y ^ step) * 128, 128)
             field[:, pl.ds(at, 128)] = part[:, b * 128 : b * 128 + 128]
-        turn(part[...], turned.at[place])
-    for step in range(4):
-        if len(payload) == 1:
-            out, at = payload[0].at[step], step
-        else:
-            out, at = payload[step], z ^ step
-        out[:256, :] = turned[at]
-        out[256:, :] = three[...]
     values = field[...]
     sums = None
     for k in range(3):
@@ -109,17 +133,14 @@
     outer_out[...] = jnp.where(first, low, high)
 
 
-def conv(own, others, weight, three, whole):
+def conv(own, others, weight, three=()):
     outs = [shape((256, 256), F32), shape((128, 256), BF16), shape((128, 256), BF16)]
-    outs += [shape((4, 640, 256), BF16)] if whole else [shape((640, 256), BF16)] * 4
-    scratch = [
-        pltpu.VMEM((256, 1024), BF16),
-        pltpu.VMEM((4, 256, 256), BF16),
-    ]
-    core_out, inner, outer, *payload = layer_call(
-        conv_kernel, outs, (own, *others, three), weight, scratch, 16, 2 * 9 * 256 * 1024 * 256
-    )
-    return core_out, inner, outer, payload
+    outs += [shape((4, 640, 256), BF16)] * len(three)
+    scratch = [pltpu.VMEM((256, 1024), BF16)]
+    scratch += [pltpu.VMEM((4, 256, 256), BF16)] * len(three)
+    return layer_call(
+        conv_kernel, outs, (own, *others, *three), weight, scratch, 16, 2 * 9 * 256 * 1024 * 256
+    )
 
 
 def conv_t_kernel(own, inner, outer, weight, *rest):
@@ -197,22 +218,25 @@
     total[tap, :, 256:384] = product[:64, 128:]
 
 
-def wprod_kernel(late_v, v, v_far, d, d_far, o0, o1, o2, o3, d_all, v_all, sums, total, sems):
+def wprod_kernel(early, early_far, late, late_far, o0, o1, o2, o3, d_all, v_all, sums, total, sems):
     space = lax.axis_index("space")
     core, z = space % 2, space // 8
     rows = pl.ds(pl.multiple_of(core * 128, 128), 128)
+    planes = pl.ds(256, 384)
     started = []
     for step in range(4):
-        v_from, d_from = (step, z ^ step) if late_v else (z ^ step, step)
         pieces = []
-        for far, (v_slots, d_slots) in enumerate(((v, d), (v_far, d_far))):
-            pieces += [
-                (v_slots.at[v_from, rows], v_all.at[step, core ^ far]),
-                (d_slots.at[d_from, pl.ds(256, 384)], d_all.at[step, core ^ far]),
-            ]
+        for far in range(2):
+            soon = (early, early_far)[far].at[z ^ step]
+            last = (late, late_far)[far].at[step]
+            for layer, (v, d) in enumerate(((soon, last), (last, soon))):
+                pieces += [
+                    (v.at[rows], v_all.at[layer, step, core ^ far]),
+                    (d.at[planes], d_all.at[layer, step, core ^ far]),
+                ]
         started.append(
             [
-                pltpu.make_async_copy(source, target, sems.at[4 * step + at])
+                pltpu.make_async_copy(source, target, sems.at[8 * step + at])
                 for at, (source, target) in enumerate(pieces)
             ]
         )
@@ -222,16 +246,18 @@
     for step, copies in enumerate(started):
         for copy in copies:
             copy.wait()
-        lhs = jnp.concatenate([v_all[step, 0], v_all[step, 1]], axis=1)
-        moved = three_shifts(d_all[step].reshape(768, 256))
-        for i, k in TAPS:
-            at = (2 - i) * 128
-            product = jnp.dot(lhs, moved[k][at : at + 512], preferred_element_type=F32)
-            if step == 0:
-                sums[3 * i + k] = product
-            else:
-                sums[3 * i + k] += product
-    for tap in range(9):
+        for layer in range(2):
+            lhs = jnp.concatenate([v_all[layer, step, 0], v_all[layer, step, 1]], axis=1)
+            moved = three_shifts(d_all[layer, step].reshape(768, 256))
+            for i, k in TAPS:
+                at = (2 - i) * 128
+                tap = 9 * layer + 3 * i + k
+                product = jnp.dot(lhs, moved[k][at : at + 512], preferred_element_type=F32)
+                if step == 0:
+                    sums[tap] = product
+                else:
+                    sums[tap] += product
+    for tap in range(18):
         total[tap, :, 0:128] = sums[tap, 64:, :128]
         total[tap, :, 128:256] = sums[tap, 64:, 128:] + sums[tap, :64, :128]
         total[tap, :, 256:384] = sums[tap, :64, 128:]
@@ -241,38 +267,40 @@
         out[...] = total[:, chosen, :].astype(out.dtype)
 
 
-def wprod(late_v, v_slots, d_slots):
+def wprod(early, late):
     hbm_spec = pl.BlockSpec(memory_space=pltpu.HBM)
     vmem_spec = pl.BlockSpec(memory_space=pltpu.VMEM)
     return pl.pallas_call(
-        functools.partial(wprod_kernel, late_v),
-        out_shape=(shape((9, 16, 384), F32),) + (shape((9, 16, 384), BF16),) * 3,
+        wprod_kernel,
+        out_shape=(shape((18, 16, 384), F32),) + (shape((18, 16, 384), BF16),) * 3,
         in_specs=[hbm_spec] * 4,
         out_specs=(vmem_spec,) * 4,
         scratch_shapes=[
-            pltpu.VMEM((4, 2, 384, 256), BF16),
-            pltpu.VMEM((4, 2, 128, 256), BF16),
-            pltpu.VMEM((9, 128, 256), F32),
-            pltpu.VMEM((9, 64, 384), F32),
-            pltpu.SemaphoreType.DMA((16,)),
+            pltpu.VMEM((2, 4, 2, 384, 256), BF16),
+            pltpu.VMEM((2, 4, 2, 128, 256), BF16),
+            pltpu.VMEM((18, 128, 256), F32),
+            pltpu.VMEM((18, 64, 384), F32),
+            pltpu.SemaphoreType.DMA((32,)),
         ],
         compiler_params=pltpu.CompilerParams(vmem_limit_bytes=24 * MIB),
         cost_estimate=pl.CostEstimate(
-            flops=2 * 9 * 128 * 2048 * 256, bytes_accessed=4 * MIB, transcendentals=0
+            flops=4 * 9 * 128 * 2048 * 256, bytes_accessed=8 * MIB, transcendentals=0
         ),
-    )(*v_slots, *d_slots)
-
-
-def last_kernel(own, r1, r2, r3, out):
-    for i, k in TAPS:
-        tap = 3 * i + k
-        total = own[tap] + r1[tap].astype(F32) + r2[tap].astype(F32) + r3[tap].astype(F32)
-        for j in range(3):
-            out[9 * i + 3 * j + k] = total[:, (2 - j) * 128 : (2 - j) * 128 + 128]
+    )(*early, *late)
+
+
+def last_kernel(own, r1, r2, r3, one_out, two_out):
+    for layer, out in enumerate((one_out, two_out)):
+        for i, k in TAPS:
+            tap = 9 * layer + 3 * i + k
+            total = own[tap] + r1[tap].astype(F32) + r2[tap].astype(F32) + r3[tap].astype(F32)
+            for j in range(3):
+                out[9 * i + 3 * j + k] = total[:, (2 - j) * 128 : (2 - j) * 128 + 128]
 
 
 def last(parts):
-    return call(last_kernel, [shape((27, 16, 128), F32)], parts, vmem=4)[0].transpose(1, 0, 2)
+    outs = call(last_kernel, [shape((27, 16, 128), F32)] * 2, parts, vmem=4)
+    return [out.transpose(1, 0, 2) for out in outs]
 
 
 def chip(z, x, core):
@@ -355,27 +383,30 @@
     x_others = gather_chan(x_own)
     hidden_parts, c_three = conv_t(c_own, c_inner, c_outer, w_two, False)
     hidden_parts = scatter_chan(hidden_parts)
-    pre, low, high, payload = conv(x_own, x_others, w_one, c_three, True)
+    pre, low, high, payload = conv(x_own, x_others, w_one, [c_three])
     low, high = swap_halo(low, high)
     payload, hidden_parts, low = lax.optimization_barrier((payload, hidden_parts, low))
-    early = lax.all_to_all(payload[0], "space", 0, 0, tiled=True, axis_index_groups=ALONG_Z)
+    early = lax.all_to_all(payload, "space", 0, 0, tiled=True, axis_index_groups=ALONG_Z)
     hidden, grad, g_inner, g_outer = middle(pre, low, high, hidden_parts)
 
     h_others = gather_chan(hidden)
     g_inner, g_outer = swap_halo(g_inner, g_outer)
     h_others, g_inner, early = lax.optimization_barrier((h_others, g_inner, early))
     early = with_far(early)
-    input_parts, g_three = conv_t(grad, g_inner, g_outer, w_one, True)
-    result, low, high, payload = conv(hidden, h_others, w_two, g_three, False)
-    late = jnp.stack(exchange_z(payload))
+    payload = pack(hidden, h_others, grad, g_outer)
+    payload, grad, hidden = lax.optimization_barrier((payload, grad, hidden))
+    late = exchange_z(payload)
+    input_parts, _ = conv_t(grad, g_inner, g_outer, w_one, False)
+    input_parts = scatter_chan(input_parts)
+    result, low, high = conv(hidden, h_others, w_two)
+    late, input_parts, low = lax.optimization_barrier((late, input_parts, low))
+    late = with_far(jnp.stack(late))
+    shares = wprod(early, late)
+    shares = scatter_x(shares)
+    shares[1], low, high = lax.optimization_barrier((shares[1], low, high))
+    grad_one, grad_two = last(shares)
     low, high = swap_halo(low, high)
-    input_parts, low = lax.optimization_barrier((input_parts, low))
-    input_parts = lax.all_to_all(input_parts[0], "chan", 0, 0, tiled=True)
-    late, input_parts, low, high = lax.optimization_barrier((late, input_parts, low, high))
-    late = with_far(late)
-    grad_one = last(scatter_x(wprod(False, early, late)))
-    grad_two = last(scatter_x(wprod(True, late, early)))
-    input_grad = jnp.sum(input_parts.astype(F32), axis=0)
+    input_grad = sum(part.astype(F32) for part in input_parts)
     return (
         channels_major(add_halo(result, low, high)),
         channels_major(input_grad),

time: 107 us -> 103 us (0.963)
  waiting for transfers between devices: 23.3 us -> 33 us
  starting transfers between devices: 52.1 us -> 45.4 us
  local copies, waits for them, and re-layouts: 8.77 us -> 5.86 us
  other arithmetic: 2.5 us -> 0.28 us
    ppermute x6 -> x3, waiting for transfers between devices: 1.12 us -> 7.63 us  [scatter_x(): lax.ppermute(parts[step], 'space', over_x(step))]
    ppermute x3 -> x6, waiting for transfers between devices: 5.34 us -> 10.8 us  [scatter_chan(): lax.ppermute(parts[step], 'chan', over_chan(step))]
    ppermute x6 -> x3, starting transfers between devices: 9.54 us -> 4.77 us  [scatter_x(): lax.ppermute(parts[step], 'space', over_x(step))]
    unnamed x15 -> x10, local copies, waits for them, and re-layouts: 5.75 us -> 2.05 us
    all_to_all x2 -> x1, starting transfers between devices: 10.1 us -> 6.46 us  [body(): lax.all_to_all(payload, 'space', 0, 0, tiled=True, axis_index_groups=ALON...]
    ppermute x3 -> x6, starting transfers between devices: 4.78 us -> 8.44 us  [scatter_chan(): lax.ppermute(parts[step], 'chan', over_chan(step))]
    ppermute x3, waiting for transfers between devices: 5.59 us -> 2.54 us  [exchange_z(): lax.ppermute(parts[step], 'space', over_z(step))]
    all_to_all x2 -> x1, waiting for transfers between devices: 6.6 us -> 8.55 us  [body(): lax.all_to_all(payload, 'space', 0, 0, tiled=True, axis_index_groups=ALON...]
  transfers between devices with their start and end apart: 30 -> 29, of which waited for: 10 -> 12; matrix products, arithmetic and copies ran while one was open for 5% -> 2% of each run, Pallas kernels for 9% -> 8%
where the time goes in v3:
time: 103 us
  starting transfers between devices  45.4 us (44%)
  waiting for transfers between devices  33 us (32%)
  Pallas kernels  17.5 us (17%)
  local copies, waits for them, and re-layouts  5.86 us (6%)
    ppermute x6, waiting for transfers between devices, scatter_chan(): lax.ppermute(parts[step], 'chan', over_chan(step))  10.8 us
    pallas_call x1, Pallas kernels, wprod(): pl.pallas_call(wprod_kernel, out_shape=(shape((18, 16, 384), F32),) + (sh...  8.83 us
    all_to_all x1, waiting for transfers between devices, body(): lax.all_to_all(payload, 'space', 0, 0, tiled=True, axis_index_groups=ALON...  8.55 us
    ppermute x6, starting transfers between devices, scatter_chan(): lax.ppermute(parts[step], 'chan', over_chan(step))  8.44 us
    ppermute x6, starting transfers between devices, gather_chan(): return [lax.ppermute(block, 'chan', over_chan(step)) for step in (1, 2, 3)]  8.35 us
    ppermute x4, starting transfers between devices, swap_halo(): lax.ppermute(inner, 'space', CORES)  7.66 us
    ppermute x3, waiting for transfers between devices, scatter_x(): lax.ppermute(parts[step], 'space', over_x(step))  7.63 us
    pallas_call x4, Pallas kernels, layer_call(): pl.pallas_call(kernel, out_shape=tuple(outs), in_specs=[vmem_spec] * (len...  7.45 us
  transfers between devices with their start and end apart: 29, of which 12 were waited for; matrix products, arithmetic and copies ran while one was open for 2% of the time, Pallas kernels for 8%

profile of v3, /device:TPU:0, one launch (start us, length us, event | category | flops | bytes accessed | tf_op | source)
XLA Modules:
  0.0 103.0 jit_solution(4888994711403670774)
XLA Ops:
  0.6 1.1 %copy.9 = bf16[2,128,2,128]{3,2,1,0:T(2,128)(2,1)S(1)} copy(bf16[2,128,2,128]{1,2,0,3:T(2,128)(2,1)} %bitcast.38) | data formatting | bytes 262144 | tf_op jit(solution)/shard_map/transpose | solution.py:334
  1.8 0.7 collective-permute-start.4
  2.5 3.0 %collective-permute-start.3 = (bf16[128,256]{1,0:T(8,128)(2,1)S(1)}, bf16[128,256]{1,0:T(8,128)(2,1)S(1)}, u32[]{:S(2)}, u32[]{:S(2)}) collective-permute-start(bf16[128,256]{1,0:T(8,128)(2,1)S(1)} %get-tuple-element.125), channel_id=1, source_target_pairs={{0,4},{4,0},{8,12},{12,8},{16,20},{20,16},{24,28},{28,24},{32,36},... | collective-permute-start | bytes 196616 | tf_op jit(solution)/shard_map/ppermute | solution.py:330
  5.5 1.1 %copy.8 = bf16[2,128,2,128]{3,2,1,0:T(2,128)(2,1)S(1)} copy(bf16[2,128,2,128]{1,2,0,3:T(2,128)(2,1)} %bitcast.39) | data formatting | bytes 262144 | tf_op jit(solution)/shard_map/transpose | solution.py:334
  6.6 3.1 %collective-permute-start.2 = (bf16[256,256]{1,0:T(8,128)(2,1)S(1)}, bf16[256,256]{1,0:T(8,128)(2,1)S(1)}, u32[]{:S(2)}, u32[]{:S(2)}) collective-permute-start(bf16[256,256]{1,0:T(8,128)(2,1)S(1)} %bitcast.25), channel_id=1, source_target_pairs={{0,3},{1,2},{2,1},{3,0},{4,7},{5,6},{6,5},{7,4},{8,11},{9,10},{10,... | collective-permute-start | bytes 393224 | tf_op jit(solution)/shard_map/ppermute | solution.py:342
  9.7 0.6 collective-permute-start.1
  10.3 0.5 collective-permute-start
  10.8 0.0 collective-permute-done.4.outer
  10.8 0.0 collective-permute-done.3.inner
  10.8 2.0 %copy-done.2 = bf16[512,27,128]{2,0,1:T(8,128)(2,1)S(1)} copy-done((bf16[512,27,128]{2,0,1:T(8,128)(2,1)S(1)}, bf16[512,27,128]{2,0,1:T(8,128)(2,1)}, u32[]{:S(2)}) %copy-start.2) | copy-done | bytes 3538968
  12.8 1.4 %shard_map.75 = (f32[256,256]{1,0:T(8,128)S(1)}, bf16[256,256]{1,0:T(8,128)(2,1)S(1)}, bf16[256,256]{1,0:T(8,128)(2,1)S(1)}, bf16[256,256]{1,0:T(8,128)(2,1)S(1)}, bf16[384,256]{1,0:T(8,128)(2,1)S(1)}) custom-call(bf16[256,256]{1,0:T(8,128)(2,1)S(1)} %bitcast.23, bf16[128,256]{1,0:T(8,128)(2,1)S(1)} %collective-permute-done.3.inner, ...), custom_call_target="tpu_custom_call" | custom-call | flops 1207959552 | bytes 5242880 | tf_op jit(solution)/shard_map/pallas_call | solution.py:54
  14.2 1.7 %collective-permute-start.5 = (bf16[256,256]{1,0:T(8,128)(2,1)S(1)}, bf16[256,256]{1,0:T(8,128)(2,1)S(1)}, u32[]{:S(2)}, u32[]{:S(2)}) collective-permute-start(bf16[256,256]{1,0:T(8,128)(2,1)S(1)} %get-tuple-element.67), channel_id=1, source_target_pairs={{0,1},{1,0},{2,3},{3,2},{4,5},{5,4},{6,7},{7,6},{8,9},{9,8},{10,11... | collective-permute-start | bytes 393224 | tf_op jit(solution)/shard_map/ppermute | solution.py:347
  15.9 2.9 %collective-permute-start.6 = (bf16[256,256]{1,0:T(8,128)(2,1)S(1)}, bf16[256,256]{1,0:T(8,128)(2,1)S(1)}, u32[]{:S(2)}, u32[]{:S(2)}) collective-permute-start(bf16[256,256]{1,0:T(8,128)(2,1)S(1)} %get-tuple-element.68), channel_id=1, source_target_pairs={{0,2},{1,3},{2,0},{3,1},{4,6},{5,7},{6,4},{7,5},{8,10},{9,11},{10,... | collective-permute-start | bytes 393224 | tf_op jit(solution)/shard_map/ppermute | solution.py:347
  18.8 0.0 collective-permute-done.2.r3
  18.8 0.4 collective-permute-start.7
  19.1 2.6 %shard_map.76 = (f32[256,256]{1,0:T(8,128)S(1)}, bf16[128,256]{1,0:T(8,128)(2,1)S(1)}, bf16[128,256]{1,0:T(8,128)(2,1)S(1)}, bf16[4,640,256]{2,1,0:T(8,128)(2,1)}) custom-call(bf16[256,256]{1,0:T(8,128)(2,1)S(1)} %bitcast.28, bf16[256,256]{1,0:T(8,128)(2,1)S(1)} %collective-permute-done.r1, bf16[256,256]{1,0:T(8,128)(2,1)S(1)} %collective-permute-done.1.r2, ...), custom_call_target="tpu_custom_call" | custom-call | flops 1207959552 | bytes 5242880 | tf_op jit(solution)/shard_map/pallas_call | solution.py:54
  21.7 3.1 %collective-permute-done.6.g2 = bf16[256,256]{1,0:T(8,128)(2,1)S(1)} collective-permute-done((bf16[256,256]{1,0:T(8,128)(2,1)S(1)}, bf16[256,256]{1,0:T(8,128)(2,1)S(1)}, u32[]{:S(2)}, u32[]{:S(2)}) %collective-permute-start.6) | collective-permute-done | bytes 131104 | tf_op jit(solution)/shard_map/ppermute | solution.py:347
  24.9 1.7 %collective-permute-done.7.g3 = bf16[256,256]{1,0:T(8,128)(2,1)S(1)} collective-permute-done((bf16[256,256]{1,0:T(8,128)(2,1)S(1)}, bf16[256,256]{1,0:T(8,128)(2,1)S(1)}, u32[]{:S(2)}, u32[]{:S(2)}) %collective-permute-start.7) | collective-permute-done | bytes 131104 | tf_op jit(solution)/shard_map/ppermute | solution.py:347
  26.6 6.5 %all-to-all-start = ((bf16[4,640,256]{2,1,0:T(8,128)(2,1)}), bf16[4,640,256]{2,1,0:T(8,128)(2,1)S(1)}, u32[]{:S(2)}, u32[]{:S(2)}) async-start(bf16[4,640,256]{2,1,0:T(8,128)(2,1)} %get-tuple-element.79), calls=%async_computation | async-start | bytes 2621440 | tf_op jit(solution)/shard_map/all_to_all | solution.py:389
  33.0 0.7 collective-permute-start.9
  33.7 0.2 shard_map.77
  33.9 1.1 %collective-permute-start.12 = (bf16[256,256]{1,0:T(8,128)(2,1)S(1)}, bf16[256,256]{1,0:T(8,128)(2,1)S(1)}, u32[]{:S(2)}, u32[]{:S(2)}) collective-permute-start(bf16[256,256]{1,0:T(8,128)(2,1)S(1)} %get-tuple-element.89.own), channel_id=1, source_target_pairs={{0,3},{1,2},{2,1},{3,0},{4,7},{5,6},{6,5},{7,4},{8,11},{9,10},{10,... | collective-permute-start | bytes 393224 | tf_op jit(solution)/shard_map/ppermute | solution.py:342
  35.0 0.1 collective-permute-start.11
  35.1 2.9 %collective-permute-start.10 = (bf16[256,256]{1,0:T(8,128)(2,1)S(1)}, bf16[256,256]{1,0:T(8,128)(2,1)S(1)}, u32[]{:S(2)}, u32[]{:S(2)}) collective-permute-start(bf16[256,256]{1,0:T(8,128)(2,1)S(1)} %get-tuple-element.89.own), channel_id=1, source_target_pairs={{0,1},{1,0},{2,3},{3,2},{4,5},{5,4},{6,7},{7,6},{8,9},{9,8},{10,11... | collective-permute-start | bytes 393224 | tf_op jit(solution)/shard_map/ppermute | solution.py:342
  38.1 3.2 %collective-permute-start.13 = (bf16[128,256]{1,0:T(8,128)(2,1)S(1)}, bf16[128,256]{1,0:T(8,128)(2,1)S(1)}, u32[]{:S(2)}, u32[]{:S(2)}) collective-permute-start(bf16[128,256]{1,0:T(8,128)(2,1)S(1)} %get-tuple-element.78), channel_id=1, source_target_pairs={{0,4},{4,0},{8,12},{12,8},{16,20},{20,16},{24,28},{28,24},{32,36},... | collective-permute-start | bytes 196616 | tf_op jit(solution)/shard_map/ppermute | solution.py:330
  41.3 0.7 collective-permute-start.14
  42.0 0.2 collective-permute-done.13.inner
  42.2 0.0 collective-permute-done.12.r3
  42.2 0.0 collective-permute-done.11.r2
  42.2 0.2 collective-permute-done.10.r1
  42.4 8.6 %all-to-all-done.early = bf16[4,640,256]{2,1,0:T(8,128)(2,1)S(1)} async-done(((bf16[4,640,256]{2,1,0:T(8,128)(2,1)}), bf16[4,640,256]{2,1,0:T(8,128)(2,1)S(1)}, u32[]{:S(2)}, u32[]{:S(2)}) %all-to-all-start) | async-done | bytes 1310752 | tf_op jit(solution)/shard_map/all_to_all | solution.py:389
  51.0 0.2 shard_map.78
  51.2 0.0 copy-start.3
  51.2 4.0 %collective-permute-start.16 = (bf16[640,256]{1,0:T(8,128)(2,1)S(1)}, bf16[640,256]{1,0:T(8,128)(2,1)S(1)}, u32[]{:S(2)}, u32[]{:S(2)}) collective-permute-start(bf16[640,256]{1,0:T(8,128)(2,1)S(1)} %get-tuple-element.93), channel_id=1, source_target_pairs={{0,32},{4,36},{8,40},{12,44},{16,48},{20,52},{24,56},{28,60},{32,0... | collective-permute-start | bytes 983048 | tf_op jit(solution)/shard_map/ppermute | solution.py:359
  55.2 2.7 %collective-permute-start.17 = (bf16[640,256]{1,0:T(8,128)(2,1)S(1)}, bf16[640,256]{1,0:T(8,128)(2,1)S(1)}, u32[]{:S(2)}, u32[]{:S(2)}) collective-permute-start(bf16[640,256]{1,0:T(8,128)(2,1)S(1)} %get-tuple-element.94), channel_id=1, source_target_pairs={{0,64},{4,68},{8,72},{12,76},{16,80},{20,84},{24,88},{28,92},{32,9... | collective-permute-start | bytes 983048 | tf_op jit(solution)/shard_map/ppermute | solution.py:359
  57.9 0.1 collective-permute-start.18
  58.0 1.9 %shard_map.80 = (f32[256,256]{1,0:T(8,128)S(1)}, bf16[256,256]{1,0:T(8,128)(2,1)S(1)}, bf16[256,256]{1,0:T(8,128)(2,1)S(1)}, bf16[256,256]{1,0:T(8,128)(2,1)S(1)}, bf16[384,256]{1,0:T(8,128)(2,1)}) custom-call(bf16[256,256]{1,0:T(8,128)(2,1)S(1)} %get-tuple-element.96.grad.own, bf16[128,256]{1,0:T(8,128)(2,1)S(1)} %collective-permute-done.13.inner, ...), custom_call_target="tpu_custom_call" | custom-call | flops 1207959552 | bytes 5242880 | tf_op jit(solution)/shard_map/pallas_call | solution.py:54
  59.9 0.0 collective-permute-start.19
  59.9 2.5 %collective-permute-start.20 = (bf16[256,256]{1,0:T(8,128)(2,1)S(1)}, bf16[256,256]{1,0:T(8,128)(2,1)S(1)}, u32[]{:S(2)}, u32[]{:S(2)}) collective-permute-start(bf16[256,256]{1,0:T(8,128)(2,1)S(1)} %get-tuple-element.100), channel_id=1, source_target_pairs={{0,2},{1,3},{2,0},{3,1},{4,6},{5,7},{6,4},{7,5},{8,10},{9,11},{10,... | collective-permute-start | bytes 393224 | tf_op jit(solution)/shard_map/ppermute | solution.py:347
  62.4 2.5 %collective-permute-done.19 = bf16[256,256]{1,0:T(8,128)(2,1)S(1)} collective-permute-done((bf16[256,256]{1,0:T(8,128)(2,1)S(1)}, bf16[256,256]{1,0:T(8,128)(2,1)S(1)}, u32[]{:S(2)}, u32[]{:S(2)}) %collective-permute-start.19) | collective-permute-done | bytes 131104 | tf_op jit(solution)/shard_map/ppermute | solution.py:347
  64.9 1.0 %collective-permute-start.21 = (bf16[256,256]{1,0:T(8,128)(2,1)S(1)}, bf16[256,256]{1,0:T(8,128)(2,1)S(1)}, u32[]{:S(2)}, u32[]{:S(2)}) collective-permute-start(bf16[256,256]{1,0:T(8,128)(2,1)S(1)} %get-tuple-element.101), channel_id=1, source_target_pairs={{0,3},{1,2},{2,1},{3,0},{4,7},{5,6},{6,5},{7,4},{8,11},{9,10},{10,... | collective-permute-start | bytes 393224 | tf_op jit(solution)/shard_map/ppermute | solution.py:347
  65.9 1.5 %shard_map.79 = (f32[256,256]{1,0:T(8,128)S(1)}, bf16[128,256]{1,0:T(8,128)(2,1)S(1)}, bf16[128,256]{1,0:T(8,128)(2,1)S(1)}) custom-call(bf16[256,256]{1,0:T(8,128)(2,1)S(1)} %get-tuple-element.89.own, bf16[256,256]{1,0:T(8,128)(2,1)S(1)} %collective-permute-done.10.r1, bf16[256,256]{1,0:T(8,128)(2,1)S(1)} %collective-permute-done.11.r2, ...), custom_call_target="tpu_custom_call" | custom-call | flops 1207959552 | bytes 5242880 | tf_op jit(solution)/shard_map/pallas_call | solution.py:54
  67.4 0.0 collective-permute-done.20
  67.5 0.1 collective-permute-start.15
  67.5 3.5 %collective-permute-done.21 = bf16[256,256]{1,0:T(8,128)(2,1)S(1)} collective-permute-done((bf16[256,256]{1,0:T(8,128)(2,1)S(1)}, bf16[256,256]{1,0:T(8,128)(2,1)S(1)}, u32[]{:S(2)}, u32[]{:S(2)}) %collective-permute-start.21) | collective-permute-done | bytes 131104 | tf_op jit(solution)/shard_map/ppermute | solution.py:347
  71.0 0.0 collective-permute-done.16
  71.0 0.0 collective-permute-done.17
  71.1 2.5 %collective-permute-done.18 = bf16[640,256]{1,0:T(8,128)(2,1)S(1)} collective-permute-done((bf16[640,256]{1,0:T(8,128)(2,1)S(1)}, bf16[640,256]{1,0:T(8,128)(2,1)S(1)}, u32[]{:S(2)}, u32[]{:S(2)}) %collective-permute-start.18) | collective-permute-done | bytes 327712 | tf_op jit(solution)/shard_map/ppermute | solution.py:359
  73.6 0.2 pad_maximum_fusion.late
  73.8 0.3 collective-permute-start.22
  74.0 3.0 %collective-permute-done.22.late_far = bf16[4,640,256]{2,1,0:T(8,128)(2,1)S(1)} collective-permute-done((bf16[4,640,256]{2,1,0:T(8,128)(2,1)S(1)}, bf16[4,640,256]{2,1,0:T(8,128)(2,1)S(1)}, u32[]{:S(2)}, u32[]{:S(2)}) %collective-permute-start.22) | collective-permute-done | bytes 1310752 | tf_op jit(solution)/shard_map/ppermute | solution.py:363
  77.0 8.8 %shard_map.81 = (f32[18,16,384]{2,1,0:T(8,128)S(1)}, bf16[18,16,384]{2,1,0:T(8,128)(2,1)S(1)}, bf16[18,16,384]{2,1,0:T(8,128)(2,1)S(1)}, bf16[18,16,384]{2,1,0:T(8,128)(2,1)S(1)}) custom-call(bf16[4,640,256]{2,1,0:T(8,128)(2,1)S(1)} %all-to-all-done.early, bf16[4,640,256]{2,1,0:T(8,128)(2,1)S(1)} %collective-permute-done.15.early_far, ...), custom_call_target="tpu_custom_call" | custom-call | flops 2415919104 | bytes 8388608 | tf_op jit(solution)/shard_map/pallas_call | solution.py:273
  85.9 0.1 collective-permute-start.23
  86.0 1.5 %collective-permute-start.26 = (bf16[18,16,384]{2,1,0:T(8,128)(2,1)S(1)}, bf16[18,16,384]{2,1,0:T(8,128)(2,1)S(1)}, u32[]{:S(2)}, u32[]{:S(2)}) collective-permute-start(bf16[18,16,384]{2,1,0:T(8,128)(2,1)S(1)} %get-tuple-element.118), channel_id=1, source_target_pairs={{0,16},{4,20},{8,24},{12,28},{16,0},{20,4},{24,8},{28,12},{32,48},... | collective-permute-start | bytes 663560 | tf_op jit(solution)/shard_map/ppermute | solution.py:352
  87.5 3.2 %collective-permute-start.27 = (bf16[18,16,384]{2,1,0:T(8,128)(2,1)S(1)}, bf16[18,16,384]{2,1,0:T(8,128)(2,1)S(1)}, u32[]{:S(2)}, u32[]{:S(2)}) collective-permute-start(bf16[18,16,384]{2,1,0:T(8,128)(2,1)S(1)} %get-tuple-element.119), channel_id=1, source_target_pairs={{0,24},{4,28},{8,16},{12,20},{16,8},{20,12},{24,0},{28,4},{32,56},... | collective-permute-start | bytes 663560 | tf_op jit(solution)/shard_map/ppermute | solution.py:352
  90.7 3.6 %collective-permute-done.23.r1 = bf16[18,16,384]{2,1,0:T(8,128)(2,1)S(1)} collective-permute-done((bf16[18,16,384]{2,1,0:T(8,128)(2,1)S(1)}, bf16[18,16,384]{2,1,0:T(8,128)(2,1)S(1)}, u32[]{:S(2)}, u32[]{:S(2)}) %collective-permute-start.23) | collective-permute-done | bytes 221216 | tf_op jit(solution)/shard_map/ppermute | solution.py:352
  94.2 0.7 collective-permute-start.24
  94.9 1.4 %collective-permute-start.25 = (bf16[128,256]{1,0:T(8,128)(2,1)S(1)}, bf16[128,256]{1,0:T(8,128)(2,1)S(1)}, u32[]{:S(2)}, u32[]{:S(2)}) collective-permute-start(bf16[128,256]{1,0:T(8,128)(2,1)S(1)} %get-tuple-element.111), channel_id=1, source_target_pairs={{0,4},{4,0},{8,12},{12,8},{16,20},{20,16},{24,28},{28,24},{32,36},... | collective-permute-start | bytes 196616 | tf_op jit(solution)/shard_map/ppermute | solution.py:330
  96.3 0.1 add_convert_fusion
  96.4 0.8 copy.11
  97.2 0.6 collective-permute-done.26.r2
  97.9 3.4 %collective-permute-done.27.r3 = bf16[18,16,384]{2,1,0:T(8,128)(2,1)S(1)} collective-permute-done((bf16[18,16,384]{2,1,0:T(8,128)(2,1)S(1)}, bf16[18,16,384]{2,1,0:T(8,128)(2,1)S(1)}, u32[]{:S(2)}, u32[]{:S(2)}) %collective-permute-start.27) | collective-permute-done | bytes 221216 | tf_op jit(solution)/shard_map/ppermute | solution.py:352
  101.3 0.8 shard_map.82
  102.2 0.8 copy.10
  (23 shorter events, 0.2 us)
Async XLA Ops:
  1.8 9.0 %collective-permute-start.4 = (bf16[128,256]{1,0:T(8,128)(2,1)S(1)}, bf16[128,256]{1,0:T(8,128)(2,1)S(1)}, u32[]{:S(2)}, u32[]{:S(2)}) collective-permute-start(bf16[128,256]{1,0:T(8,128)(2,1)S(1)} %get-tuple-element.124), channel_id=1, source_target_pairs={{4,8},{8,4},{12,16},{16,12},{20,24},{24,20},{28,32},{32,28},{36,40... | collective-permute-start | bytes 196616 | tf_op jit(solution)/shard_map/ppermute | solution.py:330
  2.5 8.3 %collective-permute-start.3 = (bf16[128,256]{1,0:T(8,128)(2,1)S(1)}, bf16[128,256]{1,0:T(8,128)(2,1)S(1)}, u32[]{:S(2)}, u32[]{:S(2)}) collective-permute-start(bf16[128,256]{1,0:T(8,128)(2,1)S(1)} %get-tuple-element.125), channel_id=1, source_target_pairs={{0,4},{4,0},{8,12},{12,8},{16,20},{20,16},{24,28},{28,24},{32,36},... | collective-permute-start | bytes 196616 | tf_op jit(solution)/shard_map/ppermute | solution.py:330
  6.6 12.2 %collective-permute-start.2 = (bf16[256,256]{1,0:T(8,128)(2,1)S(1)}, bf16[256,256]{1,0:T(8,128)(2,1)S(1)}, u32[]{:S(2)}, u32[]{:S(2)}) collective-permute-start(bf16[256,256]{1,0:T(8,128)(2,1)S(1)} %bitcast.25), channel_id=1, source_target_pairs={{0,3},{1,2},{2,1},{3,0},{4,7},{5,6},{6,5},{7,4},{8,11},{9,10},{10,... | collective-permute-start | bytes 393224 | tf_op jit(solution)/shard_map/ppermute | solution.py:342
  9.7 9.4 %collective-permute-start.1 = (bf16[256,256]{1,0:T(8,128)(2,1)S(1)}, bf16[256,256]{1,0:T(8,128)(2,1)S(1)}, u32[]{:S(2)}, u32[]{:S(2)}) collective-permute-start(bf16[256,256]{1,0:T(8,128)(2,1)S(1)} %bitcast.26), channel_id=1, source_target_pairs={{0,2},{1,3},{2,0},{3,1},{4,6},{5,7},{6,4},{7,5},{8,10},{9,11},{10,... | collective-permute-start | bytes 393224 | tf_op jit(solution)/shard_map/ppermute | solution.py:342
  10.3 8.8 %collective-permute-start = (bf16[256,256]{1,0:T(8,128)(2,1)S(1)}, bf16[256,256]{1,0:T(8,128)(2,1)S(1)}, u32[]{:S(2)}, u32[]{:S(2)}) collective-permute-start(bf16[256,256]{1,0:T(8,128)(2,1)S(1)} %bitcast.27), channel_id=1, source_target_pairs={{0,1},{1,0},{2,3},{3,2},{4,5},{5,4},{6,7},{7,6},{8,9},{9,8},{10,11... | collective-permute-start | bytes 393224 | tf_op jit(solution)/shard_map/ppermute | solution.py:342
  10.8 2.0 %copy-start.2 = (bf16[512,27,128]{2,0,1:T(8,128)(2,1)S(1)}, bf16[512,27,128]{2,0,1:T(8,128)(2,1)}, u32[]{:S(2)}) copy-start(bf16[512,27,128]{2,0,1:T(8,128)(2,1)} %param.6) | copy-start | bytes 10616836
  12.8 6.4 %copy-start = (bf16[512,27,128]{2,0,1:T(8,128)(2,1)S(1)}, bf16[512,27,128]{2,0,1:T(8,128)(2,1)}, u32[]{:S(2)}) copy-start(bf16[512,27,128]{2,0,1:T(8,128)(2,1)} %param.5) | copy-start | bytes 10616836
  14.2 7.5 %collective-permute-start.5 = (bf16[256,256]{1,0:T(8,128)(2,1)S(1)}, bf16[256,256]{1,0:T(8,128)(2,1)S(1)}, u32[]{:S(2)}, u32[]{:S(2)}) collective-permute-start(bf16[256,256]{1,0:T(8,128)(2,1)S(1)} %get-tuple-element.67), channel_id=1, source_target_pairs={{0,1},{1,0},{2,3},{3,2},{4,5},{5,4},{6,7},{7,6},{8,9},{9,8},{10,11... | collective-permute-start | bytes 393224 | tf_op jit(solution)/shard_map/ppermute | solution.py:347
  15.9 9.0 %collective-permute-start.6 = (bf16[256,256]{1,0:T(8,128)(2,1)S(1)}, bf16[256,256]{1,0:T(8,128)(2,1)S(1)}, u32[]{:S(2)}, u32[]{:S(2)}) collective-permute-start(bf16[256,256]{1,0:T(8,128)(2,1)S(1)} %get-tuple-element.68), channel_id=1, source_target_pairs={{0,2},{1,3},{2,0},{3,1},{4,6},{5,7},{6,4},{7,5},{8,10},{9,11},{10,... | collective-permute-start | bytes 393224 | tf_op jit(solution)/shard_map/ppermute | solution.py:347
  18.8 7.8 %collective-permute-start.7 = (bf16[256,256]{1,0:T(8,128)(2,1)S(1)}, bf16[256,256]{1,0:T(8,128)(2,1)S(1)}, u32[]{:S(2)}, u32[]{:S(2)}) collective-permute-start(bf16[256,256]{1,0:T(8,128)(2,1)S(1)} %get-tuple-element.69), channel_id=1, source_target_pairs={{0,3},{1,2},{2,1},{3,0},{4,7},{5,6},{6,5},{7,4},{8,11},{9,10},{10,... | collective-permute-start | bytes 393224 | tf_op jit(solution)/shard_map/ppermute | solution.py:347
  21.7 4.8 %collective-permute-start.8 = (bf16[128,256]{1,0:T(8,128)(2,1)S(1)}, bf16[128,256]{1,0:T(8,128)(2,1)S(1)}, u32[]{:S(2)}, u32[]{:S(2)}) collective-permute-start(bf16[128,256]{1,0:T(8,128)(2,1)S(1)} %get-tuple-element.70), channel_id=1, source_target_pairs={{0,4},{4,0},{8,12},{12,8},{16,20},{20,16},{24,28},{28,24},{32,36},... | collective-permute-start | bytes 196616 | tf_op jit(solution)/shard_map/ppermute | solution.py:330
  26.6 24.4 %all-to-all-start = ((bf16[4,640,256]{2,1,0:T(8,128)(2,1)}), bf16[4,640,256]{2,1,0:T(8,128)(2,1)S(1)}, u32[]{:S(2)}, u32[]{:S(2)}) async-start(bf16[4,640,256]{2,1,0:T(8,128)(2,1)} %get-tuple-element.79), calls=%async_computation | async-start | bytes 2621440 | tf_op jit(solution)/shard_map/all_to_all | solution.py:389
  33.0 0.7 collective-permute-start.9
  33.9 8.3 %collective-permute-start.12 = (bf16[256,256]{1,0:T(8,128)(2,1)S(1)}, bf16[256,256]{1,0:T(8,128)(2,1)S(1)}, u32[]{:S(2)}, u32[]{:S(2)}) collective-permute-start(bf16[256,256]{1,0:T(8,128)(2,1)S(1)} %get-tuple-element.89.own), channel_id=1, source_target_pairs={{0,3},{1,2},{2,1},{3,0},{4,7},{5,6},{6,5},{7,4},{8,11},{9,10},{10,... | collective-permute-start | bytes 393224 | tf_op jit(solution)/shard_map/ppermute | solution.py:342
  35.0 7.2 %collective-permute-start.11 = (bf16[256,256]{1,0:T(8,128)(2,1)S(1)}, bf16[256,256]{1,0:T(8,128)(2,1)S(1)}, u32[]{:S(2)}, u32[]{:S(2)}) collective-permute-start(bf16[256,256]{1,0:T(8,128)(2,1)S(1)} %get-tuple-element.89.own), channel_id=1, source_target_pairs={{0,2},{1,3},{2,0},{3,1},{4,6},{5,7},{6,4},{7,5},{8,10},{9,11},{10,... | collective-permute-start | bytes 393224 | tf_op jit(solution)/shard_map/ppermute | solution.py:342
  35.1 7.3 %collective-permute-start.10 = (bf16[256,256]{1,0:T(8,128)(2,1)S(1)}, bf16[256,256]{1,0:T(8,128)(2,1)S(1)}, u32[]{:S(2)}, u32[]{:S(2)}) collective-permute-start(bf16[256,256]{1,0:T(8,128)(2,1)S(1)} %get-tuple-element.89.own), channel_id=1, source_target_pairs={{0,1},{1,0},{2,3},{3,2},{4,5},{5,4},{6,7},{7,6},{8,9},{9,8},{10,11... | collective-permute-start | bytes 393224 | tf_op jit(solution)/shard_map/ppermute | solution.py:342
  38.1 4.1 %collective-permute-start.13 = (bf16[128,256]{1,0:T(8,128)(2,1)S(1)}, bf16[128,256]{1,0:T(8,128)(2,1)S(1)}, u32[]{:S(2)}, u32[]{:S(2)}) collective-permute-start(bf16[128,256]{1,0:T(8,128)(2,1)S(1)} %get-tuple-element.78), channel_id=1, source_target_pairs={{0,4},{4,0},{8,12},{12,8},{16,20},{20,16},{24,28},{28,24},{32,36},... | collective-permute-start | bytes 196616 | tf_op jit(solution)/shard_map/ppermute | solution.py:330
  41.3 9.7 %collective-permute-start.14 = (bf16[128,256]{1,0:T(8,128)(2,1)S(1)}, bf16[128,256]{1,0:T(8,128)(2,1)S(1)}, u32[]{:S(2)}, u32[]{:S(2)}) collective-permute-start(bf16[128,256]{1,0:T(8,128)(2,1)S(1)} %get-tuple-element.84), channel_id=1, source_target_pairs={{4,8},{8,4},{12,16},{16,12},{20,24},{24,20},{28,32},{32,28},{36,40... | collective-permute-start | bytes 196616 | tf_op jit(solution)/shard_map/ppermute | solution.py:330
  51.0 7.0 %copy-start.1 = (bf16[512,27,128]{2,0,1:T(8,128)(2,1)S(1)}, bf16[512,27,128]{2,0,1:T(8,128)(2,1)}, u32[]{:S(2)}) copy-start(bf16[512,27,128]{2,0,1:T(8,128)(2,1)} %param.5) | copy-start | bytes 10616836
  51.2 14.7 %copy-start.3 = (bf16[512,27,128]{2,0,1:T(8,128)(2,1)S(1)}, bf16[512,27,128]{2,0,1:T(8,128)(2,1)}, u32[]{:S(2)}) copy-start(bf16[512,27,128]{2,0,1:T(8,128)(2,1)} %param.6) | copy-start | bytes 10616836
  51.2 19.8 %collective-permute-start.16 = (bf16[640,256]{1,0:T(8,128)(2,1)S(1)}, bf16[640,256]{1,0:T(8,128)(2,1)S(1)}, u32[]{:S(2)}, u32[]{:S(2)}) collective-permute-start(bf16[640,256]{1,0:T(8,128)(2,1)S(1)} %get-tuple-element.93), channel_id=1, source_target_pairs={{0,32},{4,36},{8,40},{12,44},{16,48},{20,52},{24,56},{28,60},{32,0... | collective-permute-start | bytes 983048 | tf_op jit(solution)/shard_map/ppermute | solution.py:359
  55.2 15.8 %collective-permute-start.17 = (bf16[640,256]{1,0:T(8,128)(2,1)S(1)}, bf16[640,256]{1,0:T(8,128)(2,1)S(1)}, u32[]{:S(2)}, u32[]{:S(2)}) collective-permute-start(bf16[640,256]{1,0:T(8,128)(2,1)S(1)} %get-tuple-element.94), channel_id=1, source_target_pairs={{0,64},{4,68},{8,72},{12,76},{16,80},{20,84},{24,88},{28,92},{32,9... | collective-permute-start | bytes 983048 | tf_op jit(solution)/shard_map/ppermute | solution.py:359
  57.9 15.7 %collective-permute-start.18 = (bf16[640,256]{1,0:T(8,128)(2,1)S(1)}, bf16[640,256]{1,0:T(8,128)(2,1)S(1)}, u32[]{:S(2)}, u32[]{:S(2)}) collective-permute-start(bf16[640,256]{1,0:T(8,128)(2,1)S(1)} %get-tuple-element.95), channel_id=1, source_target_pairs={{0,96},{4,100},{8,104},{12,108},{16,112},{20,116},{24,120},{28,124... | collective-permute-start | bytes 983048 | tf_op jit(solution)/shard_map/ppermute | solution.py:359
  59.9 5.0 %collective-permute-start.19 = (bf16[256,256]{1,0:T(8,128)(2,1)S(1)}, bf16[256,256]{1,0:T(8,128)(2,1)S(1)}, u32[]{:S(2)}, u32[]{:S(2)}) collective-permute-start(bf16[256,256]{1,0:T(8,128)(2,1)S(1)} %get-tuple-element.99), channel_id=1, source_target_pairs={{0,1},{1,0},{2,3},{3,2},{4,5},{5,4},{6,7},{7,6},{8,9},{9,8},{10,11... | collective-permute-start | bytes 393224 | tf_op jit(solution)/shard_map/ppermute | solution.py:347
  59.9 7.5 %collective-permute-start.20 = (bf16[256,256]{1,0:T(8,128)(2,1)S(1)}, bf16[256,256]{1,0:T(8,128)(2,1)S(1)}, u32[]{:S(2)}, u32[]{:S(2)}) collective-permute-start(bf16[256,256]{1,0:T(8,128)(2,1)S(1)} %get-tuple-element.100), channel_id=1, source_target_pairs={{0,2},{1,3},{2,0},{3,1},{4,6},{5,7},{6,4},{7,5},{8,10},{9,11},{10,... | collective-permute-start | bytes 393224 | tf_op jit(solution)/shard_map/ppermute | solution.py:347
  64.9 6.2 %collective-permute-start.21 = (bf16[256,256]{1,0:T(8,128)(2,1)S(1)}, bf16[256,256]{1,0:T(8,128)(2,1)S(1)}, u32[]{:S(2)}, u32[]{:S(2)}) collective-permute-start(bf16[256,256]{1,0:T(8,128)(2,1)S(1)} %get-tuple-element.101), channel_id=1, source_target_pairs={{0,3},{1,2},{2,1},{3,0},{4,7},{5,6},{6,5},{7,4},{8,11},{9,10},{10,... | collective-permute-start | bytes 393224 | tf_op jit(solution)/shard_map/ppermute | solution.py:347
  67.5 6.6 %collective-permute-start.15 = (bf16[4,640,256]{2,1,0:T(8,128)(2,1)S(1)}, bf16[4,640,256]{2,1,0:T(8,128)(2,1)S(1)}, u32[]{:S(2)}, u32[]{:S(2)}) collective-permute-start(bf16[4,640,256]{2,1,0:T(8,128)(2,1)S(1)} %all-to-all-done.early), channel_id=1, source_target_pairs={{0,4},{4,0},{8,12},{12,8},{16,20},{20,16},{24,28},{28,24},{32,36},... | collective-permute-start | bytes 3932168 | tf_op jit(solution)/shard_map/ppermute | solution.py:363
  73.8 3.3 %collective-permute-start.22 = (bf16[4,640,256]{2,1,0:T(8,128)(2,1)S(1)}, bf16[4,640,256]{2,1,0:T(8,128)(2,1)S(1)}, u32[]{:S(2)}, u32[]{:S(2)}) collective-permute-start(bf16[4,640,256]{2,1,0:T(8,128)(2,1)S(1)} %pad_maximum_fusion.late), channel_id=1, source_target_pairs={{0,4},{4,0},{8,12},{12,8},{16,20},{20,16},{24,28},{28,24},{32,36},... | collective-permute-start | bytes 3932168 | tf_op jit(solution)/shard_map/ppermute | solution.py:363
  85.9 8.4 %collective-permute-start.23 = (bf16[18,16,384]{2,1,0:T(8,128)(2,1)S(1)}, bf16[18,16,384]{2,1,0:T(8,128)(2,1)S(1)}, u32[]{:S(2)}, u32[]{:S(2)}) collective-permute-start(bf16[18,16,384]{2,1,0:T(8,128)(2,1)S(1)} %get-tuple-element.107), channel_id=1, source_target_pairs={{0,8},{4,12},{8,0},{12,4},{16,24},{20,28},{24,16},{28,20},{32,40},... | collective-permute-start | bytes 663560 | tf_op jit(solution)/shard_map/ppermute | solution.py:352
  86.0 11.9 %collective-permute-start.26 = (bf16[18,16,384]{2,1,0:T(8,128)(2,1)S(1)}, bf16[18,16,384]{2,1,0:T(8,128)(2,1)S(1)}, u32[]{:S(2)}, u32[]{:S(2)}) collective-permute-start(bf16[18,16,384]{2,1,0:T(8,128)(2,1)S(1)} %get-tuple-element.118), channel_id=1, source_target_pairs={{0,16},{4,20},{8,24},{12,28},{16,0},{20,4},{24,8},{28,12},{32,48},... | collective-permute-start | bytes 663560 | tf_op jit(solution)/shard_map/ppermute | solution.py:352
  87.5 13.8 %collective-permute-start.27 = (bf16[18,16,384]{2,1,0:T(8,128)(2,1)S(1)}, bf16[18,16,384]{2,1,0:T(8,128)(2,1)S(1)}, u32[]{:S(2)}, u32[]{:S(2)}) collective-permute-start(bf16[18,16,384]{2,1,0:T(8,128)(2,1)S(1)} %get-tuple-element.119), channel_id=1, source_target_pairs={{0,24},{4,28},{8,16},{12,20},{16,8},{20,12},{24,0},{28,4},{32,56},... | collective-permute-start | bytes 663560 | tf_op jit(solution)/shard_map/ppermute | solution.py:352
  94.2 7.8 %collective-permute-start.24 = (bf16[128,256]{1,0:T(8,128)(2,1)S(1)}, bf16[128,256]{1,0:T(8,128)(2,1)S(1)}, u32[]{:S(2)}, u32[]{:S(2)}) collective-permute-start(bf16[128,256]{1,0:T(8,128)(2,1)S(1)} %get-tuple-element.110), channel_id=1, source_target_pairs={{4,8},{8,4},{12,16},{16,12},{20,24},{24,20},{28,32},{32,28},{36,40... | collective-permute-start | bytes 196616 | tf_op jit(solution)/shard_map/ppermute | solution.py:330
  94.9 7.2 %collective-permute-start.25 = (bf16[128,256]{1,0:T(8,128)(2,1)S(1)}, bf16[128,256]{1,0:T(8,128)(2,1)S(1)}, u32[]{:S(2)}, u32[]{:S(2)}) collective-permute-start(bf16[128,256]{1,0:T(8,128)(2,1)S(1)} %get-tuple-element.111), channel_id=1, source_target_pairs={{0,4},{4,0},{8,12},{12,8},{16,20},{20,16},{24,28},{28,24},{32,36},... | collective-permute-start | bytes 196616 | tf_op jit(solution)/shard_map/ppermute | solution.py:330

commit v4 on v3

--- a/solution.py
+++ b/solution.py
@@ -218,37 +218,26 @@
     total[tap, :, 256:384] = product[:64, 128:]
 
 
-def wprod_kernel(early, early_far, late, late_far, o0, o1, o2, o3, d_all, v_all, sums, total, sems):
+def wprod_kernel(early, early_far, late, late_far, o0, o1, o2, o3, sums, total):
     space = lax.axis_index("space")
     core, z = space % 2, space // 8
+    first = core == 0
     rows = pl.ds(pl.multiple_of(core * 128, 128), 128)
-    planes = pl.ds(256, 384)
-    started = []
+
+    def in_order(near, far, axis):
+        return jnp.concatenate(
+            [jnp.where(first, near, far), jnp.where(first, far, near)], axis=axis
+        )
+
     for step in range(4):
-        pieces = []
-        for far in range(2):
-            soon = (early, early_far)[far].at[z ^ step]
-            last = (late, late_far)[far].at[step]
-            for layer, (v, d) in enumerate(((soon, last), (last, soon))):
-                pieces += [
-                    (v.at[rows], v_all.at[layer, step, core ^ far]),
-                    (d.at[planes], d_all.at[layer, step, core ^ far]),
-                ]
-        started.append(
-            [
-                pltpu.make_async_copy(source, target, sems.at[8 * step + at])
-                for at, (source, target) in enumerate(pieces)
-            ]
-        )
-    for copies in started:
-        for copy in copies:
-            copy.start()
-    for step, copies in enumerate(started):
-        for copy in copies:
-            copy.wait()
+        soon, soon_far = early.at[z ^ step], early_far.at[z ^ step]
+        last, last_far = late.at[step], late_far.at[step]
         for layer in range(2):
-            lhs = jnp.concatenate([v_all[layer, step, 0], v_all[layer, step, 1]], axis=1)
-            moved = three_shifts(d_all[layer, step].reshape(768, 256))
+            v, v_far, d, d_far = (
+                (soon, soon_far, last, last_far) if layer == 0 else (last, last_far, soon, soon_far)
+            )
+            lhs = in_order(v[rows, :], v_far[rows, :], 1)
+            moved = three_shifts(in_order(d[256:640, :], d_far[256:640, :], 0))
             for i, k in TAPS:
                 at = (2 - i) * 128
                 tap = 9 * layer + 3 * i + k
@@ -268,25 +257,13 @@
 
 
 def wprod(early, late):
-    hbm_spec = pl.BlockSpec(memory_space=pltpu.HBM)
-    vmem_spec = pl.BlockSpec(memory_space=pltpu.VMEM)
-    return pl.pallas_call(
+    return call(
         wprod_kernel,
-        out_shape=(shape((18, 16, 384), F32),) + (shape((18, 16, 384), BF16),) * 3,
-        in_specs=[hbm_spec] * 4,
-        out_specs=(vmem_spec,) * 4,
-        scratch_shapes=[
-            pltpu.VMEM((2, 4, 2, 384, 256), BF16),
-            pltpu.VMEM((2, 4, 2, 128, 256), BF16),
-            pltpu.VMEM((18, 128, 256), F32),
-            pltpu.VMEM((18, 64, 384), F32),
-            pltpu.SemaphoreType.DMA((32,)),
-        ],
-        compiler_params=pltpu.CompilerParams(vmem_limit_bytes=24 * MIB),
-        cost_estimate=pl.CostEstimate(
-            flops=4 * 9 * 128 * 2048 * 256, bytes_accessed=8 * MIB, transcendentals=0
-        ),
-    )(*early, *late)
+        [shape((18, 16, 384), F32)] + [shape((18, 16, 384), BF16)] * 3,
+        (*early, *late),
+        [pltpu.VMEM((18, 128, 256), F32), pltpu.VMEM((18, 64, 384), F32)],
+        flops=4 * 9 * 128 * 2048 * 256,
+    )
 
 
 def last_kernel(own, r1, r2, r3, one_out, two_out):

time: 103 us -> 97.4 us (0.946)
  Pallas kernels: 17.5 us -> 11.6 us
    pallas_call x1 -> x0, Pallas kernels: 8.83 us -> none  [wprod(): pl.pallas_call(wprod_kernel, out_shape=(shape((18, 16, 384), F32),) + (sh...]
    pallas_call x3 -> x4, Pallas kernels: 1.25 us -> 4.15 us  [call(): pl.pallas_call(kernel, out_shape=tuple(out_shapes), in_specs=[pl.BlockSpe...]
  transfers between devices with their start and end apart: 29 -> 29, of which waited for: 12 -> 12; matrix products, arithmetic and copies ran while one was open for 2% -> 2% of each run, Pallas kernels for 8% -> 9%
where the time goes in v4:
time: 97.4 us; the launch traced here: 97.1 us
  starting transfers between devices  45.4 us (47%)
  waiting for transfers between devices  33 us (34%)
  Pallas kernels  11.6 us (12%)
  local copies, waits for them, and re-layouts  5.86 us (6%)
    ppermute x6, waiting for transfers between devices, scatter_chan(): lax.ppermute(parts[step], 'chan', over_chan(step))  10.8 us
    all_to_all x1, waiting for transfers between devices, body(): lax.all_to_all(payload, 'space', 0, 0, tiled=True, axis_index_groups=ALON...  8.55 us
    ppermute x6, starting transfers between devices, scatter_chan(): lax.ppermute(parts[step], 'chan', over_chan(step))  8.44 us
    ppermute x6, starting transfers between devices, gather_chan(): return [lax.ppermute(block, 'chan', over_chan(step)) for step in (1, 2, 3)]  8.35 us
    ppermute x4, starting transfers between devices, swap_halo(): lax.ppermute(inner, 'space', CORES)  7.66 us
    ppermute x3, waiting for transfers between devices, scatter_x(): lax.ppermute(parts[step], 'space', over_x(step))  7.63 us
    pallas_call x4, Pallas kernels, layer_call(): pl.pallas_call(kernel, out_shape=tuple(outs), in_specs=[vmem_spec] * (len...  7.45 us
    ppermute x3, starting transfers between devices, exchange_z(): lax.ppermute(parts[step], 'space', over_z(step))  6.75 us
  transfers between devices with their start and end apart: 29, of which 12 were waited for; matrix products, arithmetic and copies ran while one was open for 2% of the time, Pallas kernels for 9%

profile of v4, /device:TPU:0, one launch (start us, length us, event | category | flops | bytes accessed | tf_op | source)
XLA Modules:
  0.0 97.1 jit_solution(33426624413869182)
XLA Ops:
  0.6 1.1 %copy.9 = bf16[2,128,2,128]{3,2,1,0:T(2,128)(2,1)S(1)} copy(bf16[2,128,2,128]{1,2,0,3:T(2,128)(2,1)} %bitcast.38) | data formatting | bytes 262144 | tf_op jit(solution)/shard_map/transpose | solution.py:311
  1.8 0.7 collective-permute-start.4
  2.5 3.0 %collective-permute-start.3 = (bf16[128,256]{1,0:T(8,128)(2,1)S(1)}, bf16[128,256]{1,0:T(8,128)(2,1)S(1)}, u32[]{:S(2)}, u32[]{:S(2)}) collective-permute-start(bf16[128,256]{1,0:T(8,128)(2,1)S(1)} %get-tuple-element.125), channel_id=1, source_target_pairs={{0,4},{4,0},{8,12},{12,8},{16,20},{20,16},{24,28},{28,24},{32,36},... | collective-permute-start | bytes 196616 | tf_op jit(solution)/shard_map/ppermute | solution.py:307
  5.5 1.1 %copy.8 = bf16[2,128,2,128]{3,2,1,0:T(2,128)(2,1)S(1)} copy(bf16[2,128,2,128]{1,2,0,3:T(2,128)(2,1)} %bitcast.39) | data formatting | bytes 262144 | tf_op jit(solution)/shard_map/transpose | solution.py:311
  6.6 3.1 %collective-permute-start.2 = (bf16[256,256]{1,0:T(8,128)(2,1)S(1)}, bf16[256,256]{1,0:T(8,128)(2,1)S(1)}, u32[]{:S(2)}, u32[]{:S(2)}) collective-permute-start(bf16[256,256]{1,0:T(8,128)(2,1)S(1)} %bitcast.25), channel_id=1, source_target_pairs={{0,3},{1,2},{2,1},{3,0},{4,7},{5,6},{6,5},{7,4},{8,11},{9,10},{10,... | collective-permute-start | bytes 393224 | tf_op jit(solution)/shard_map/ppermute | solution.py:319
  9.7 0.6 collective-permute-start.1
  10.3 0.5 collective-permute-start
  10.8 0.0 collective-permute-done.4.outer
  10.8 0.0 collective-permute-done.3.inner
  10.8 2.0 %copy-done.2 = bf16[512,27,128]{2,0,1:T(8,128)(2,1)S(1)} copy-done((bf16[512,27,128]{2,0,1:T(8,128)(2,1)S(1)}, bf16[512,27,128]{2,0,1:T(8,128)(2,1)}, u32[]{:S(2)}) %copy-start.2) | copy-done | bytes 3538968
  12.8 1.4 %shard_map.75 = (f32[256,256]{1,0:T(8,128)S(1)}, bf16[256,256]{1,0:T(8,128)(2,1)S(1)}, bf16[256,256]{1,0:T(8,128)(2,1)S(1)}, bf16[256,256]{1,0:T(8,128)(2,1)S(1)}, bf16[384,256]{1,0:T(8,128)(2,1)S(1)}) custom-call(bf16[256,256]{1,0:T(8,128)(2,1)S(1)} %bitcast.23, bf16[128,256]{1,0:T(8,128)(2,1)S(1)} %collective-permute-done.3.inner, ...), custom_call_target="tpu_custom_call" | custom-call | flops 1207959552 | bytes 5242880 | tf_op jit(solution)/shard_map/pallas_call | solution.py:54
  14.2 1.7 %collective-permute-start.5 = (bf16[256,256]{1,0:T(8,128)(2,1)S(1)}, bf16[256,256]{1,0:T(8,128)(2,1)S(1)}, u32[]{:S(2)}, u32[]{:S(2)}) collective-permute-start(bf16[256,256]{1,0:T(8,128)(2,1)S(1)} %get-tuple-element.67), channel_id=1, source_target_pairs={{0,1},{1,0},{2,3},{3,2},{4,5},{5,4},{6,7},{7,6},{8,9},{9,8},{10,11... | collective-permute-start | bytes 393224 | tf_op jit(solution)/shard_map/ppermute | solution.py:324
  15.9 2.9 %collective-permute-start.6 = (bf16[256,256]{1,0:T(8,128)(2,1)S(1)}, bf16[256,256]{1,0:T(8,128)(2,1)S(1)}, u32[]{:S(2)}, u32[]{:S(2)}) collective-permute-start(bf16[256,256]{1,0:T(8,128)(2,1)S(1)} %get-tuple-element.68), channel_id=1, source_target_pairs={{0,2},{1,3},{2,0},{3,1},{4,6},{5,7},{6,4},{7,5},{8,10},{9,11},{10,... | collective-permute-start | bytes 393224 | tf_op jit(solution)/shard_map/ppermute | solution.py:324
  18.8 0.0 collective-permute-done.2.r3
  18.8 0.4 collective-permute-start.7
  19.1 2.6 %shard_map.76 = (f32[256,256]{1,0:T(8,128)S(1)}, bf16[128,256]{1,0:T(8,128)(2,1)S(1)}, bf16[128,256]{1,0:T(8,128)(2,1)S(1)}, bf16[4,640,256]{2,1,0:T(8,128)(2,1)}) custom-call(bf16[256,256]{1,0:T(8,128)(2,1)S(1)} %bitcast.28, bf16[256,256]{1,0:T(8,128)(2,1)S(1)} %collective-permute-done.r1, bf16[256,256]{1,0:T(8,128)(2,1)S(1)} %collective-permute-done.1.r2, ...), custom_call_target="tpu_custom_call" | custom-call | flops 1207959552 | bytes 5242880 | tf_op jit(solution)/shard_map/pallas_call | solution.py:54
  21.7 3.1 %collective-permute-done.6.g2 = bf16[256,256]{1,0:T(8,128)(2,1)S(1)} collective-permute-done((bf16[256,256]{1,0:T(8,128)(2,1)S(1)}, bf16[256,256]{1,0:T(8,128)(2,1)S(1)}, u32[]{:S(2)}, u32[]{:S(2)}) %collective-permute-start.6) | collective-permute-done | bytes 131104 | tf_op jit(solution)/shard_map/ppermute | solution.py:324
  24.9 1.7 %collective-permute-done.7.g3 = bf16[256,256]{1,0:T(8,128)(2,1)S(1)} collective-permute-done((bf16[256,256]{1,0:T(8,128)(2,1)S(1)}, bf16[256,256]{1,0:T(8,128)(2,1)S(1)}, u32[]{:S(2)}, u32[]{:S(2)}) %collective-permute-start.7) | collective-permute-done | bytes 131104 | tf_op jit(solution)/shard_map/ppermute | solution.py:324
  26.6 6.5 %all-to-all-start = ((bf16[4,640,256]{2,1,0:T(8,128)(2,1)}), bf16[4,640,256]{2,1,0:T(8,128)(2,1)S(1)}, u32[]{:S(2)}, u32[]{:S(2)}) async-start(bf16[4,640,256]{2,1,0:T(8,128)(2,1)} %get-tuple-element.79), calls=%async_computation | async-start | bytes 2621440 | tf_op jit(solution)/shard_map/all_to_all | solution.py:366
  33.0 0.7 collective-permute-start.9
  33.7 0.2 shard_map.77
  33.9 1.1 %collective-permute-start.12 = (bf16[256,256]{1,0:T(8,128)(2,1)S(1)}, bf16[256,256]{1,0:T(8,128)(2,1)S(1)}, u32[]{:S(2)}, u32[]{:S(2)}) collective-permute-start(bf16[256,256]{1,0:T(8,128)(2,1)S(1)} %get-tuple-element.89.own), channel_id=1, source_target_pairs={{0,3},{1,2},{2,1},{3,0},{4,7},{5,6},{6,5},{7,4},{8,11},{9,10},{10,... | collective-permute-start | bytes 393224 | tf_op jit(solution)/shard_map/ppermute | solution.py:319
  35.0 0.1 collective-permute-start.11
  35.1 2.9 %collective-permute-start.10 = (bf16[256,256]{1,0:T(8,128)(2,1)S(1)}, bf16[256,256]{1,0:T(8,128)(2,1)S(1)}, u32[]{:S(2)}, u32[]{:S(2)}) collective-permute-start(bf16[256,256]{1,0:T(8,128)(2,1)S(1)} %get-tuple-element.89.own), channel_id=1, source_target_pairs={{0,1},{1,0},{2,3},{3,2},{4,5},{5,4},{6,7},{7,6},{8,9},{9,8},{10,11... | collective-permute-start | bytes 393224 | tf_op jit(solution)/shard_map/ppermute | solution.py:319
  38.1 3.2 %collective-permute-start.13 = (bf16[128,256]{1,0:T(8,128)(2,1)S(1)}, bf16[128,256]{1,0:T(8,128)(2,1)S(1)}, u32[]{:S(2)}, u32[]{:S(2)}) collective-permute-start(bf16[128,256]{1,0:T(8,128)(2,1)S(1)} %get-tuple-element.78), channel_id=1, source_target_pairs={{0,4},{4,0},{8,12},{12,8},{16,20},{20,16},{24,28},{28,24},{32,36},... | collective-permute-start | bytes 196616 | tf_op jit(solution)/shard_map/ppermute | solution.py:307
  41.3 0.7 collective-permute-start.14
  42.0 0.2 collective-permute-done.13.inner
  42.2 0.0 collective-permute-done.12.r3
  42.2 0.0 collective-permute-done.11.r2
  42.2 0.2 collective-permute-done.10.r1
  42.4 8.6 %all-to-all-done.early = bf16[4,640,256]{2,1,0:T(8,128)(2,1)S(1)} async-done(((bf16[4,640,256]{2,1,0:T(8,128)(2,1)}), bf16[4,640,256]{2,1,0:T(8,128)(2,1)S(1)}, u32[]{:S(2)}, u32[]{:S(2)}) %all-to-all-start) | async-done | bytes 1310752 | tf_op jit(solution)/shard_map/all_to_all | solution.py:366
  51.0 0.2 shard_map.78
  51.2 0.0 copy-start.3
  51.2 4.0 %collective-permute-start.16 = (bf16[640,256]{1,0:T(8,128)(2,1)S(1)}, bf16[640,256]{1,0:T(8,128)(2,1)S(1)}, u32[]{:S(2)}, u32[]{:S(2)}) collective-permute-start(bf16[640,256]{1,0:T(8,128)(2,1)S(1)} %get-tuple-element.93), channel_id=1, source_target_pairs={{0,32},{4,36},{8,40},{12,44},{16,48},{20,52},{24,56},{28,60},{32,0... | collective-permute-start | bytes 983048 | tf_op jit(solution)/shard_map/ppermute | solution.py:336
  55.2 2.7 %collective-permute-start.17 = (bf16[640,256]{1,0:T(8,128)(2,1)S(1)}, bf16[640,256]{1,0:T(8,128)(2,1)S(1)}, u32[]{:S(2)}, u32[]{:S(2)}) collective-permute-start(bf16[640,256]{1,0:T(8,128)(2,1)S(1)} %get-tuple-element.94), channel_id=1, source_target_pairs={{0,64},{4,68},{8,72},{12,76},{16,80},{20,84},{24,88},{28,92},{32,9... | collective-permute-start | bytes 983048 | tf_op jit(solution)/shard_map/ppermute | solution.py:336
  57.9 0.1 collective-permute-start.18
  58.0 1.9 %shard_map.80 = (f32[256,256]{1,0:T(8,128)S(1)}, bf16[256,256]{1,0:T(8,128)(2,1)S(1)}, bf16[256,256]{1,0:T(8,128)(2,1)S(1)}, bf16[256,256]{1,0:T(8,128)(2,1)S(1)}, bf16[384,256]{1,0:T(8,128)(2,1)}) custom-call(bf16[256,256]{1,0:T(8,128)(2,1)S(1)} %get-tuple-element.96.grad.own, bf16[128,256]{1,0:T(8,128)(2,1)S(1)} %collective-permute-done.13.inner, ...), custom_call_target="tpu_custom_call" | custom-call | flops 1207959552 | bytes 5242880 | tf_op jit(solution)/shard_map/pallas_call | solution.py:54
  59.9 0.0 collective-permute-start.19
  59.9 2.5 %collective-permute-start.20 = (bf16[256,256]{1,0:T(8,128)(2,1)S(1)}, bf16[256,256]{1,0:T(8,128)(2,1)S(1)}, u32[]{:S(2)}, u32[]{:S(2)}) collective-permute-start(bf16[256,256]{1,0:T(8,128)(2,1)S(1)} %get-tuple-element.100), channel_id=1, source_target_pairs={{0,2},{1,3},{2,0},{3,1},{4,6},{5,7},{6,4},{7,5},{8,10},{9,11},{10,... | collective-permute-start | bytes 393224 | tf_op jit(solution)/shard_map/ppermute | solution.py:324
  62.4 2.5 %collective-permute-done.19 = bf16[256,256]{1,0:T(8,128)(2,1)S(1)} collective-permute-done((bf16[256,256]{1,0:T(8,128)(2,1)S(1)}, bf16[256,256]{1,0:T(8,128)(2,1)S(1)}, u32[]{:S(2)}, u32[]{:S(2)}) %collective-permute-start.19) | collective-permute-done | bytes 131104 | tf_op jit(solution)/shard_map/ppermute | solution.py:324
  64.9 1.0 %collective-permute-start.21 = (bf16[256,256]{1,0:T(8,128)(2,1)S(1)}, bf16[256,256]{1,0:T(8,128)(2,1)S(1)}, u32[]{:S(2)}, u32[]{:S(2)}) collective-permute-start(bf16[256,256]{1,0:T(8,128)(2,1)S(1)} %get-tuple-element.101), channel_id=1, source_target_pairs={{0,3},{1,2},{2,1},{3,0},{4,7},{5,6},{6,5},{7,4},{8,11},{9,10},{10,... | collective-permute-start | bytes 393224 | tf_op jit(solution)/shard_map/ppermute | solution.py:324
  65.9 1.5 %shard_map.79 = (f32[256,256]{1,0:T(8,128)S(1)}, bf16[128,256]{1,0:T(8,128)(2,1)S(1)}, bf16[128,256]{1,0:T(8,128)(2,1)S(1)}) custom-call(bf16[256,256]{1,0:T(8,128)(2,1)S(1)} %get-tuple-element.89.own, bf16[256,256]{1,0:T(8,128)(2,1)S(1)} %collective-permute-done.10.r1, bf16[256,256]{1,0:T(8,128)(2,1)S(1)} %collective-permute-done.11.r2, ...), custom_call_target="tpu_custom_call" | custom-call | flops 1207959552 | bytes 5242880 | tf_op jit(solution)/shard_map/pallas_call | solution.py:54
  67.4 0.0 collective-permute-done.20
  67.5 0.1 collective-permute-start.15
  67.5 3.5 %collective-permute-done.21 = bf16[256,256]{1,0:T(8,128)(2,1)S(1)} collective-permute-done((bf16[256,256]{1,0:T(8,128)(2,1)S(1)}, bf16[256,256]{1,0:T(8,128)(2,1)S(1)}, u32[]{:S(2)}, u32[]{:S(2)}) %collective-permute-start.21) | collective-permute-done | bytes 131104 | tf_op jit(solution)/shard_map/ppermute | solution.py:324
  71.0 0.0 collective-permute-done.16
  71.0 0.0 collective-permute-done.17
  71.1 2.5 %collective-permute-done.18 = bf16[640,256]{1,0:T(8,128)(2,1)S(1)} collective-permute-done((bf16[640,256]{1,0:T(8,128)(2,1)S(1)}, bf16[640,256]{1,0:T(8,128)(2,1)S(1)}, u32[]{:S(2)}, u32[]{:S(2)}) %collective-permute-start.18) | collective-permute-done | bytes 327712 | tf_op jit(solution)/shard_map/ppermute | solution.py:336
  73.6 0.2 pad_maximum_fusion.late
  73.8 0.3 collective-permute-start.22
  74.0 3.0 %collective-permute-done.22.late_far = bf16[4,640,256]{2,1,0:T(8,128)(2,1)S(1)} collective-permute-done((bf16[4,640,256]{2,1,0:T(8,128)(2,1)S(1)}, bf16[4,640,256]{2,1,0:T(8,128)(2,1)S(1)}, u32[]{:S(2)}, u32[]{:S(2)}) %collective-permute-start.22) | collective-permute-done | bytes 1310752 | tf_op jit(solution)/shard_map/ppermute | solution.py:340
  77.0 2.9 %shard_map.81 = (f32[18,16,384]{2,1,0:T(8,128)S(1)}, bf16[18,16,384]{2,1,0:T(8,128)(2,1)S(1)}, bf16[18,16,384]{2,1,0:T(8,128)(2,1)S(1)}, bf16[18,16,384]{2,1,0:T(8,128)(2,1)S(1)}) custom-call(bf16[4,640,256]{2,1,0:T(8,128)(2,1)S(1)} %all-to-all-done.early, bf16[4,640,256]{2,1,0:T(8,128)(2,1)S(1)} %collective-permute-done.15.early_far, ...), custom_call_target="tpu_custom_call" | custom-call | flops 2415919104 | bytes 6348800 | tf_op jit(solution)/shard_map/pallas_call | solution.py:24
  80.0 0.1 collective-permute-start.23
  80.1 1.5 %collective-permute-start.26 = (bf16[18,16,384]{2,1,0:T(8,128)(2,1)S(1)}, bf16[18,16,384]{2,1,0:T(8,128)(2,1)S(1)}, u32[]{:S(2)}, u32[]{:S(2)}) collective-permute-start(bf16[18,16,384]{2,1,0:T(8,128)(2,1)S(1)} %get-tuple-element.118), channel_id=1, source_target_pairs={{0,16},{4,20},{8,24},{12,28},{16,0},{20,4},{24,8},{28,12},{32,48},... | collective-permute-start | bytes 663560 | tf_op jit(solution)/shard_map/ppermute | solution.py:329
  81.6 3.2 %collective-permute-start.27 = (bf16[18,16,384]{2,1,0:T(8,128)(2,1)S(1)}, bf16[18,16,384]{2,1,0:T(8,128)(2,1)S(1)}, u32[]{:S(2)}, u32[]{:S(2)}) collective-permute-start(bf16[18,16,384]{2,1,0:T(8,128)(2,1)S(1)} %get-tuple-element.119), channel_id=1, source_target_pairs={{0,24},{4,28},{8,16},{12,20},{16,8},{20,12},{24,0},{28,4},{32,56},... | collective-permute-start | bytes 663560 | tf_op jit(solution)/shard_map/ppermute | solution.py:329
  84.7 3.6 %collective-permute-done.23.r1 = bf16[18,16,384]{2,1,0:T(8,128)(2,1)S(1)} collective-permute-done((bf16[18,16,384]{2,1,0:T(8,128)(2,1)S(1)}, bf16[18,16,384]{2,1,0:T(8,128)(2,1)S(1)}, u32[]{:S(2)}, u32[]{:S(2)}) %collective-permute-start.23) | collective-permute-done | bytes 221216 | tf_op jit(solution)/shard_map/ppermute | solution.py:329
  88.3 0.7 collective-permute-start.24
  89.0 1.4 %collective-permute-start.25 = (bf16[128,256]{1,0:T(8,128)(2,1)S(1)}, bf16[128,256]{1,0:T(8,128)(2,1)S(1)}, u32[]{:S(2)}, u32[]{:S(2)}) collective-permute-start(bf16[128,256]{1,0:T(8,128)(2,1)S(1)} %get-tuple-element.111), channel_id=1, source_target_pairs={{0,4},{4,0},{8,12},{12,8},{16,20},{20,16},{24,28},{28,24},{32,36},... | collective-permute-start | bytes 196616 | tf_op jit(solution)/shard_map/ppermute | solution.py:307
  90.4 0.1 add_convert_fusion
  90.5 0.8 copy.11
  91.3 0.7 collective-permute-done.26.r2
  91.9 3.4 %collective-permute-done.27.r3 = bf16[18,16,384]{2,1,0:T(8,128)(2,1)S(1)} collective-permute-done((bf16[18,16,384]{2,1,0:T(8,128)(2,1)S(1)}, bf16[18,16,384]{2,1,0:T(8,128)(2,1)S(1)}, u32[]{:S(2)}, u32[]{:S(2)}) %collective-permute-start.27) | collective-permute-done | bytes 221216 | tf_op jit(solution)/shard_map/ppermute | solution.py:329
  95.4 0.8 shard_map.82
  96.3 0.8 copy.10
  (23 shorter events, 0.2 us)
Async XLA Ops:
  1.8 9.0 %collective-permute-start.4 = (bf16[128,256]{1,0:T(8,128)(2,1)S(1)}, bf16[128,256]{1,0:T(8,128)(2,1)S(1)}, u32[]{:S(2)}, u32[]{:S(2)}) collective-permute-start(bf16[128,256]{1,0:T(8,128)(2,1)S(1)} %get-tuple-element.124), channel_id=1, source_target_pairs={{4,8},{8,4},{12,16},{16,12},{20,24},{24,20},{28,32},{32,28},{36,40... | collective-permute-start | bytes 196616 | tf_op jit(solution)/shard_map/ppermute | solution.py:307
  2.5 8.3 %collective-permute-start.3 = (bf16[128,256]{1,0:T(8,128)(2,1)S(1)}, bf16[128,256]{1,0:T(8,128)(2,1)S(1)}, u32[]{:S(2)}, u32[]{:S(2)}) collective-permute-start(bf16[128,256]{1,0:T(8,128)(2,1)S(1)} %get-tuple-element.125), channel_id=1, source_target_pairs={{0,4},{4,0},{8,12},{12,8},{16,20},{20,16},{24,28},{28,24},{32,36},... | collective-permute-start | bytes 196616 | tf_op jit(solution)/shard_map/ppermute | solution.py:307
  6.6 12.2 %collective-permute-start.2 = (bf16[256,256]{1,0:T(8,128)(2,1)S(1)}, bf16[256,256]{1,0:T(8,128)(2,1)S(1)}, u32[]{:S(2)}, u32[]{:S(2)}) collective-permute-start(bf16[256,256]{1,0:T(8,128)(2,1)S(1)} %bitcast.25), channel_id=1, source_target_pairs={{0,3},{1,2},{2,1},{3,0},{4,7},{5,6},{6,5},{7,4},{8,11},{9,10},{10,... | collective-permute-start | bytes 393224 | tf_op jit(solution)/shard_map/ppermute | solution.py:319
  9.7 9.4 %collective-permute-start.1 = (bf16[256,256]{1,0:T(8,128)(2,1)S(1)}, bf16[256,256]{1,0:T(8,128)(2,1)S(1)}, u32[]{:S(2)}, u32[]{:S(2)}) collective-permute-start(bf16[256,256]{1,0:T(8,128)(2,1)S(1)} %bitcast.26), channel_id=1, source_target_pairs={{0,2},{1,3},{2,0},{3,1},{4,6},{5,7},{6,4},{7,5},{8,10},{9,11},{10,... | collective-permute-start | bytes 393224 | tf_op jit(solution)/shard_map/ppermute | solution.py:319
  10.3 8.8 %collective-permute-start = (bf16[256,256]{1,0:T(8,128)(2,1)S(1)}, bf16[256,256]{1,0:T(8,128)(2,1)S(1)}, u32[]{:S(2)}, u32[]{:S(2)}) collective-permute-start(bf16[256,256]{1,0:T(8,128)(2,1)S(1)} %bitcast.27), channel_id=1, source_target_pairs={{0,1},{1,0},{2,3},{3,2},{4,5},{5,4},{6,7},{7,6},{8,9},{9,8},{10,11... | collective-permute-start | bytes 393224 | tf_op jit(solution)/shard_map/ppermute | solution.py:319
  10.8 2.0 %copy-start.2 = (bf16[512,27,128]{2,0,1:T(8,128)(2,1)S(1)}, bf16[512,27,128]{2,0,1:T(8,128)(2,1)}, u32[]{:S(2)}) copy-start(bf16[512,27,128]{2,0,1:T(8,128)(2,1)} %param.6) | copy-start | bytes 10616836
  12.8 6.4 %copy-start = (bf16[512,27,128]{2,0,1:T(8,128)(2,1)S(1)}, bf16[512,27,128]{2,0,1:T(8,128)(2,1)}, u32[]{:S(2)}) copy-start(bf16[512,27,128]{2,0,1:T(8,128)(2,1)} %param.5) | copy-start | bytes 10616836
  14.2 7.5 %collective-permute-start.5 = (bf16[256,256]{1,0:T(8,128)(2,1)S(1)}, bf16[256,256]{1,0:T(8,128)(2,1)S(1)}, u32[]{:S(2)}, u32[]{:S(2)}) collective-permute-start(bf16[256,256]{1,0:T(8,128)(2,1)S(1)} %get-tuple-element.67), channel_id=1, source_target_pairs={{0,1},{1,0},{2,3},{3,2},{4,5},{5,4},{6,7},{7,6},{8,9},{9,8},{10,11... | collective-permute-start | bytes 393224 | tf_op jit(solution)/shard_map/ppermute | solution.py:324
  15.9 9.0 %collective-permute-start.6 = (bf16[256,256]{1,0:T(8,128)(2,1)S(1)}, bf16[256,256]{1,0:T(8,128)(2,1)S(1)}, u32[]{:S(2)}, u32[]{:S(2)}) collective-permute-start(bf16[256,256]{1,0:T(8,128)(2,1)S(1)} %get-tuple-element.68), channel_id=1, source_target_pairs={{0,2},{1,3},{2,0},{3,1},{4,6},{5,7},{6,4},{7,5},{8,10},{9,11},{10,... | collective-permute-start | bytes 393224 | tf_op jit(solution)/shard_map/ppermute | solution.py:324
  18.8 7.8 %collective-permute-start.7 = (bf16[256,256]{1,0:T(8,128)(2,1)S(1)}, bf16[256,256]{1,0:T(8,128)(2,1)S(1)}, u32[]{:S(2)}, u32[]{:S(2)}) collective-permute-start(bf16[256,256]{1,0:T(8,128)(2,1)S(1)} %get-tuple-element.69), channel_id=1, source_target_pairs={{0,3},{1,2},{2,1},{3,0},{4,7},{5,6},{6,5},{7,4},{8,11},{9,10},{10,... | collective-permute-start | bytes 393224 | tf_op jit(solution)/shard_map/ppermute | solution.py:324
  21.7 4.8 %collective-permute-start.8 = (bf16[128,256]{1,0:T(8,128)(2,1)S(1)}, bf16[128,256]{1,0:T(8,128)(2,1)S(1)}, u32[]{:S(2)}, u32[]{:S(2)}) collective-permute-start(bf16[128,256]{1,0:T(8,128)(2,1)S(1)} %get-tuple-element.70), channel_id=1, source_target_pairs={{0,4},{4,0},{8,12},{12,8},{16,20},{20,16},{24,28},{28,24},{32,36},... | collective-permute-start | bytes 196616 | tf_op jit(solution)/shard_map/ppermute | solution.py:307
  26.6 24.4 %all-to-all-start = ((bf16[4,640,256]{2,1,0:T(8,128)(2,1)}), bf16[4,640,256]{2,1,0:T(8,128)(2,1)S(1)}, u32[]{:S(2)}, u32[]{:S(2)}) async-start(bf16[4,640,256]{2,1,0:T(8,128)(2,1)} %get-tuple-element.79), calls=%async_computation | async-start | bytes 2621440 | tf_op jit(solution)/shard_map/all_to_all | solution.py:366
  33.0 0.7 collective-permute-start.9
  33.9 8.3 %collective-permute-start.12 = (bf16[256,256]{1,0:T(8,128)(2,1)S(1)}, bf16[256,256]{1,0:T(8,128)(2,1)S(1)}, u32[]{:S(2)}, u32[]{:S(2)}) collective-permute-start(bf16[256,256]{1,0:T(8,128)(2,1)S(1)} %get-tuple-element.89.own), channel_id=1, source_target_pairs={{0,3},{1,2},{2,1},{3,0},{4,7},{5,6},{6,5},{7,4},{8,11},{9,10},{10,... | collective-permute-start | bytes 393224 | tf_op jit(solution)/shard_map/ppermute | solution.py:319
  35.0 7.2 %collective-permute-start.11 = (bf16[256,256]{1,0:T(8,128)(2,1)S(1)}, bf16[256,256]{1,0:T(8,128)(2,1)S(1)}, u32[]{:S(2)}, u32[]{:S(2)}) collective-permute-start(bf16[256,256]{1,0:T(8,128)(2,1)S(1)} %get-tuple-element.89.own), channel_id=1, source_target_pairs={{0,2},{1,3},{2,0},{3,1},{4,6},{5,7},{6,4},{7,5},{8,10},{9,11},{10,... | collective-permute-start | bytes 393224 | tf_op jit(solution)/shard_map/ppermute | solution.py:319
  35.1 7.3 %collective-permute-start.10 = (bf16[256,256]{1,0:T(8,128)(2,1)S(1)}, bf16[256,256]{1,0:T(8,128)(2,1)S(1)}, u32[]{:S(2)}, u32[]{:S(2)}) collective-permute-start(bf16[256,256]{1,0:T(8,128)(2,1)S(1)} %get-tuple-element.89.own), channel_id=1, source_target_pairs={{0,1},{1,0},{2,3},{3,2},{4,5},{5,4},{6,7},{7,6},{8,9},{9,8},{10,11... | collective-permute-start | bytes 393224 | tf_op jit(solution)/shard_map/ppermute | solution.py:319
  38.1 4.1 %collective-permute-start.13 = (bf16[128,256]{1,0:T(8,128)(2,1)S(1)}, bf16[128,256]{1,0:T(8,128)(2,1)S(1)}, u32[]{:S(2)}, u32[]{:S(2)}) collective-permute-start(bf16[128,256]{1,0:T(8,128)(2,1)S(1)} %get-tuple-element.78), channel_id=1, source_target_pairs={{0,4},{4,0},{8,12},{12,8},{16,20},{20,16},{24,28},{28,24},{32,36},... | collective-permute-start | bytes 196616 | tf_op jit(solution)/shard_map/ppermute | solution.py:307
  41.3 9.7 %collective-permute-start.14 = (bf16[128,256]{1,0:T(8,128)(2,1)S(1)}, bf16[128,256]{1,0:T(8,128)(2,1)S(1)}, u32[]{:S(2)}, u32[]{:S(2)}) collective-permute-start(bf16[128,256]{1,0:T(8,128)(2,1)S(1)} %get-tuple-element.84), channel_id=1, source_target_pairs={{4,8},{8,4},{12,16},{16,12},{20,24},{24,20},{28,32},{32,28},{36,40... | collective-permute-start | bytes 196616 | tf_op jit(solution)/shard_map/ppermute | solution.py:307
  51.0 7.0 %copy-start.1 = (bf16[512,27,128]{2,0,1:T(8,128)(2,1)S(1)}, bf16[512,27,128]{2,0,1:T(8,128)(2,1)}, u32[]{:S(2)}) copy-start(bf16[512,27,128]{2,0,1:T(8,128)(2,1)} %param.5) | copy-start | bytes 10616836
  51.2 14.7 %copy-start.3 = (bf16[512,27,128]{2,0,1:T(8,128)(2,1)S(1)}, bf16[512,27,128]{2,0,1:T(8,128)(2,1)}, u32[]{:S(2)}) copy-start(bf16[512,27,128]{2,0,1:T(8,128)(2,1)} %param.6) | copy-start | bytes 10616836
  51.2 19.8 %collective-permute-start.16 = (bf16[640,256]{1,0:T(8,128)(2,1)S(1)}, bf16[640,256]{1,0:T(8,128)(2,1)S(1)}, u32[]{:S(2)}, u32[]{:S(2)}) collective-permute-start(bf16[640,256]{1,0:T(8,128)(2,1)S(1)} %get-tuple-element.93), channel_id=1, source_target_pairs={{0,32},{4,36},{8,40},{12,44},{16,48},{20,52},{24,56},{28,60},{32,0... | collective-permute-start | bytes 983048 | tf_op jit(solution)/shard_map/ppermute | solution.py:336
  55.2 15.8 %collective-permute-start.17 = (bf16[640,256]{1,0:T(8,128)(2,1)S(1)}, bf16[640,256]{1,0:T(8,128)(2,1)S(1)}, u32[]{:S(2)}, u32[]{:S(2)}) collective-permute-start(bf16[640,256]{1,0:T(8,128)(2,1)S(1)} %get-tuple-element.94), channel_id=1, source_target_pairs={{0,64},{4,68},{8,72},{12,76},{16,80},{20,84},{24,88},{28,92},{32,9... | collective-permute-start | bytes 983048 | tf_op jit(solution)/shard_map/ppermute | solution.py:336
  57.9 15.7 %collective-permute-start.18 = (bf16[640,256]{1,0:T(8,128)(2,1)S(1)}, bf16[640,256]{1,0:T(8,128)(2,1)S(1)}, u32[]{:S(2)}, u32[]{:S(2)}) collective-permute-start(bf16[640,256]{1,0:T(8,128)(2,1)S(1)} %get-tuple-element.95), channel_id=1, source_target_pairs={{0,96},{4,100},{8,104},{12,108},{16,112},{20,116},{24,120},{28,124... | collective-permute-start | bytes 983048 | tf_op jit(solution)/shard_map/ppermute | solution.py:336
  59.9 5.0 %collective-permute-start.19 = (bf16[256,256]{1,0:T(8,128)(2,1)S(1)}, bf16[256,256]{1,0:T(8,128)(2,1)S(1)}, u32[]{:S(2)}, u32[]{:S(2)}) collective-permute-start(bf16[256,256]{1,0:T(8,128)(2,1)S(1)} %get-tuple-element.99), channel_id=1, source_target_pairs={{0,1},{1,0},{2,3},{3,2},{4,5},{5,4},{6,7},{7,6},{8,9},{9,8},{10,11... | collective-permute-start | bytes 393224 | tf_op jit(solution)/shard_map/ppermute | solution.py:324
  59.9 7.5 %collective-permute-start.20 = (bf16[256,256]{1,0:T(8,128)(2,1)S(1)}, bf16[256,256]{1,0:T(8,128)(2,1)S(1)}, u32[]{:S(2)}, u32[]{:S(2)}) collective-permute-start(bf16[256,256]{1,0:T(8,128)(2,1)S(1)} %get-tuple-element.100), channel_id=1, source_target_pairs={{0,2},{1,3},{2,0},{3,1},{4,6},{5,7},{6,4},{7,5},{8,10},{9,11},{10,... | collective-permute-start | bytes 393224 | tf_op jit(solution)/shard_map/ppermute | solution.py:324
  64.9 6.2 %collective-permute-start.21 = (bf16[256,256]{1,0:T(8,128)(2,1)S(1)}, bf16[256,256]{1,0:T(8,128)(2,1)S(1)}, u32[]{:S(2)}, u32[]{:S(2)}) collective-permute-start(bf16[256,256]{1,0:T(8,128)(2,1)S(1)} %get-tuple-element.101), channel_id=1, source_target_pairs={{0,3},{1,2},{2,1},{3,0},{4,7},{5,6},{6,5},{7,4},{8,11},{9,10},{10,... | collective-permute-start | bytes 393224 | tf_op jit(solution)/shard_map/ppermute | solution.py:324
  67.5 6.6 %collective-permute-start.15 = (bf16[4,640,256]{2,1,0:T(8,128)(2,1)S(1)}, bf16[4,640,256]{2,1,0:T(8,128)(2,1)S(1)}, u32[]{:S(2)}, u32[]{:S(2)}) collective-permute-start(bf16[4,640,256]{2,1,0:T(8,128)(2,1)S(1)} %all-to-all-done.early), channel_id=1, source_target_pairs={{0,4},{4,0},{8,12},{12,8},{16,20},{20,16},{24,28},{28,24},{32,36},... | collective-permute-start | bytes 3932168 | tf_op jit(solution)/shard_map/ppermute | solution.py:340
  73.8 3.3 %collective-permute-start.22 = (bf16[4,640,256]{2,1,0:T(8,128)(2,1)S(1)}, bf16[4,640,256]{2,1,0:T(8,128)(2,1)S(1)}, u32[]{:S(2)}, u32[]{:S(2)}) collective-permute-start(bf16[4,640,256]{2,1,0:T(8,128)(2,1)S(1)} %pad_maximum_fusion.late), channel_id=1, source_target_pairs={{0,4},{4,0},{8,12},{12,8},{16,20},{20,16},{24,28},{28,24},{32,36},... | collective-permute-start | bytes 3932168 | tf_op jit(solution)/shard_map/ppermute | solution.py:340
  80.0 8.4 %collective-permute-start.23 = (bf16[18,16,384]{2,1,0:T(8,128)(2,1)S(1)}, bf16[18,16,384]{2,1,0:T(8,128)(2,1)S(1)}, u32[]{:S(2)}, u32[]{:S(2)}) collective-permute-start(bf16[18,16,384]{2,1,0:T(8,128)(2,1)S(1)} %get-tuple-element.107), channel_id=1, source_target_pairs={{0,8},{4,12},{8,0},{12,4},{16,24},{20,28},{24,16},{28,20},{32,40},... | collective-permute-start | bytes 663560 | tf_op jit(solution)/shard_map/ppermute | solution.py:329
  80.1 11.9 %collective-permute-start.26 = (bf16[18,16,384]{2,1,0:T(8,128)(2,1)S(1)}, bf16[18,16,384]{2,1,0:T(8,128)(2,1)S(1)}, u32[]{:S(2)}, u32[]{:S(2)}) collective-permute-start(bf16[18,16,384]{2,1,0:T(8,128)(2,1)S(1)} %get-tuple-element.118), channel_id=1, source_target_pairs={{0,16},{4,20},{8,24},{12,28},{16,0},{20,4},{24,8},{28,12},{32,48},... | collective-permute-start | bytes 663560 | tf_op jit(solution)/shard_map/ppermute | solution.py:329
  81.6 13.8 %collective-permute-start.27 = (bf16[18,16,384]{2,1,0:T(8,128)(2,1)S(1)}, bf16[18,16,384]{2,1,0:T(8,128)(2,1)S(1)}, u32[]{:S(2)}, u32[]{:S(2)}) collective-permute-start(bf16[18,16,384]{2,1,0:T(8,128)(2,1)S(1)} %get-tuple-element.119), channel_id=1, source_target_pairs={{0,24},{4,28},{8,16},{12,20},{16,8},{20,12},{24,0},{28,4},{32,56},... | collective-permute-start | bytes 663560 | tf_op jit(solution)/shard_map/ppermute | solution.py:329
  88.3 7.9 %collective-permute-start.24 = (bf16[128,256]{1,0:T(8,128)(2,1)S(1)}, bf16[128,256]{1,0:T(8,128)(2,1)S(1)}, u32[]{:S(2)}, u32[]{:S(2)}) collective-permute-start(bf16[128,256]{1,0:T(8,128)(2,1)S(1)} %get-tuple-element.110), channel_id=1, source_target_pairs={{4,8},{8,4},{12,16},{16,12},{20,24},{24,20},{28,32},{32,28},{36,40... | collective-permute-start | bytes 196616 | tf_op jit(solution)/shard_map/ppermute | solution.py:307
  89.0 7.2 %collective-permute-start.25 = (bf16[128,256]{1,0:T(8,128)(2,1)S(1)}, bf16[128,256]{1,0:T(8,128)(2,1)S(1)}, u32[]{:S(2)}, u32[]{:S(2)}) collective-permute-start(bf16[128,256]{1,0:T(8,128)(2,1)S(1)} %get-tuple-element.111), channel_id=1, source_target_pairs={{0,4},{4,0},{8,12},{12,8},{16,20},{20,16},{24,28},{28,24},{32,36},... | collective-permute-start | bytes 196616 | tf_op jit(solution)/shard_map/ppermute | solution.py:307

commit v5 on v4

--- a/solution.py
+++ b/solution.py
@@ -362,21 +362,22 @@
     hidden_parts = scatter_chan(hidden_parts)
     pre, low, high, payload = conv(x_own, x_others, w_one, [c_three])
     low, high = swap_halo(low, high)
-    payload, hidden_parts, low = lax.optimization_barrier((payload, hidden_parts, low))
+    payload, hidden_parts, low, high = lax.optimization_barrier(
+        (payload, hidden_parts, low, high)
+    )
     early = lax.all_to_all(payload, "space", 0, 0, tiled=True, axis_index_groups=ALONG_Z)
     hidden, grad, g_inner, g_outer = middle(pre, low, high, hidden_parts)
 
     h_others = gather_chan(hidden)
     g_inner, g_outer = swap_halo(g_inner, g_outer)
-    h_others, g_inner, early = lax.optimization_barrier((h_others, g_inner, early))
-    early = with_far(early)
     payload = pack(hidden, h_others, grad, g_outer)
     payload, grad, hidden = lax.optimization_barrier((payload, grad, hidden))
     late = exchange_z(payload)
     input_parts, _ = conv_t(grad, g_inner, g_outer, w_one, False)
     input_parts = scatter_chan(input_parts)
     result, low, high = conv(hidden, h_others, w_two)
-    late, input_parts, low = lax.optimization_barrier((late, input_parts, low))
+    late, input_parts, low, early = lax.optimization_barrier((late, input_parts, low, early))
+    early = with_far(early)
     late = with_far(jnp.stack(late))
     shares = wprod(early, late)
     shares = scatter_x(shares)

time: 97.4 us -> 95 us (0.975)
  waiting for transfers between devices: 33 us -> 27 us
  starting transfers between devices: 45.4 us -> 49 us
    all_to_all x1, waiting for transfers between devices: 8.55 us -> 0.01 us  [body(): lax.all_to_all(payload, 'space', 0, 0, tiled=True, axis_index_groups=ALON...]
    ppermute x6, waiting for transfers between devices: 0.21 us -> 4.02 us  [gather_chan(): return [lax.ppermute(block, 'chan', over_chan(step)) for step in (1, 2, 3)]]
    ppermute x6, waiting for transfers between devices: 10.8 us -> 7.47 us  [scatter_chan(): lax.ppermute(parts[step], 'chan', over_chan(step))]
    ppermute x4, starting transfers between devices: 7.66 us -> 4.51 us  [swap_halo(): lax.ppermute(inner, 'space', CORES)]
    ppermute x6, starting transfers between devices: 8.44 us -> 11.2 us  [scatter_chan(): lax.ppermute(parts[step], 'chan', over_chan(step))]
    all_to_all x1, starting transfers between devices: 6.46 us -> 9.08 us  [body(): lax.all_to_all(payload, 'space', 0, 0, tiled=True, axis_index_groups=ALON...]
    ppermute x3, waiting for transfers between devices: 7.63 us -> 9.29 us  [scatter_x(): lax.ppermute(parts[step], 'space', over_x(step))]
    ppermute x2, waiting for transfers between devices: 3.01 us -> 4.4 us  [with_far(): return [near, lax.ppermute(near, 'space', CORES)]]
  transfers between devices with their start and end apart: 29 -> 29, of which waited for: 12 -> 13; matrix products, arithmetic and copies ran while one was open for 2% -> 2% of each run, Pallas kernels for 9% -> 9%
where the time goes in v5:
time: 95 us; the launch traced here: 94.7 us
  starting transfers between devices  49 us (52%)
  waiting for transfers between devices  27 us (28%)
  Pallas kernels  11.6 us (12%)
  local copies, waits for them, and re-layouts  5.88 us (6%)
    ppermute x6, starting transfers between devices, scatter_chan(): lax.ppermute(parts[step], 'chan', over_chan(step))  11.2 us
    ppermute x3, waiting for transfers between devices, scatter_x(): lax.ppermute(parts[step], 'space', over_x(step))  9.29 us
    all_to_all x1, starting transfers between devices, body(): lax.all_to_all(payload, 'space', 0, 0, tiled=True, axis_index_groups=ALON...  9.08 us
    ppermute x6, starting transfers between devices, gather_chan(): return [lax.ppermute(block, 'chan', over_chan(step)) for step in (1, 2, 3)]  8.35 us
    ppermute x3, starting transfers between devices, exchange_z(): lax.ppermute(parts[step], 'space', over_z(step))  7.89 us
    pallas_call x4, Pallas kernels, layer_call(): pl.pallas_call(kernel, out_shape=tuple(outs), in_specs=[vmem_spec] * (len...  7.47 us
    ppermute x6, waiting for transfers between devices, scatter_chan(): lax.ppermute(parts[step], 'chan', over_chan(step))  7.47 us
    ppermute x3, starting transfers between devices, scatter_x(): lax.ppermute(parts[step], 'space', over_x(step))  4.77 us
  transfers between devices with their start and end apart: 29, of which 13 were waited for; matrix products, arithmetic and copies ran while one was open for 2% of the time, Pallas kernels for 9%

profile of v5, /device:TPU:0, one launch (start us, length us, event | category | flops | bytes accessed | tf_op | source)
XLA Modules:
  0.0 94.7 jit_solution(17177575738479610087)
XLA Ops:
  0.6 1.1 %copy.9 = bf16[2,128,2,128]{3,2,1,0:T(2,128)(2,1)S(1)} copy(bf16[2,128,2,128]{1,2,0,3:T(2,128)(2,1)} %bitcast.38) | data formatting | bytes 262144 | tf_op jit(solution)/shard_map/transpose | solution.py:311
  1.8 0.7 collective-permute-start.4
  2.5 3.0 %collective-permute-start.3 = (bf16[128,256]{1,0:T(8,128)(2,1)S(1)}, bf16[128,256]{1,0:T(8,128)(2,1)S(1)}, u32[]{:S(2)}, u32[]{:S(2)}) collective-permute-start(bf16[128,256]{1,0:T(8,128)(2,1)S(1)} %get-tuple-element.119), channel_id=1, source_target_pairs={{0,4},{4,0},{8,12},{12,8},{16,20},{20,16},{24,28},{28,24},{32,36},... | collective-permute-start | bytes 196616 | tf_op jit(solution)/shard_map/ppermute | solution.py:307
  5.5 1.1 %copy.8 = bf16[2,128,2,128]{3,2,1,0:T(2,128)(2,1)S(1)} copy(bf16[2,128,2,128]{1,2,0,3:T(2,128)(2,1)} %bitcast.39) | data formatting | bytes 262144 | tf_op jit(solution)/shard_map/transpose | solution.py:311
  6.6 3.1 %collective-permute-start.2 = (bf16[256,256]{1,0:T(8,128)(2,1)S(1)}, bf16[256,256]{1,0:T(8,128)(2,1)S(1)}, u32[]{:S(2)}, u32[]{:S(2)}) collective-permute-start(bf16[256,256]{1,0:T(8,128)(2,1)S(1)} %bitcast.25), channel_id=1, source_target_pairs={{0,3},{1,2},{2,1},{3,0},{4,7},{5,6},{6,5},{7,4},{8,11},{9,10},{10,... | collective-permute-start | bytes 393224 | tf_op jit(solution)/shard_map/ppermute | solution.py:319
  9.7 0.6 collective-permute-start.1
  10.3 0.5 collective-permute-start
  10.8 0.0 collective-permute-done.4.outer
  10.8 2.0 %copy-done.2 = bf16[512,27,128]{2,0,1:T(8,128)(2,1)S(1)} copy-done((bf16[512,27,128]{2,0,1:T(8,128)(2,1)S(1)}, bf16[512,27,128]{2,0,1:T(8,128)(2,1)}, u32[]{:S(2)}) %copy-start.2) | copy-done | bytes 3538968
  12.8 1.4 %shard_map.75 = (f32[256,256]{1,0:T(8,128)S(1)}, bf16[256,256]{1,0:T(8,128)(2,1)S(1)}, bf16[256,256]{1,0:T(8,128)(2,1)S(1)}, bf16[256,256]{1,0:T(8,128)(2,1)S(1)}, bf16[384,256]{1,0:T(8,128)(2,1)S(1)}) custom-call(bf16[256,256]{1,0:T(8,128)(2,1)S(1)} %bitcast.23, bf16[128,256]{1,0:T(8,128)(2,1)S(1)} %collective-permute-done.3.inner, ...), custom_call_target="tpu_custom_call" | custom-call | flops 1207959552 | bytes 5242880 | tf_op jit(solution)/shard_map/pallas_call | solution.py:54
  14.2 1.7 %collective-permute-start.5 = (bf16[256,256]{1,0:T(8,128)(2,1)S(1)}, bf16[256,256]{1,0:T(8,128)(2,1)S(1)}, u32[]{:S(2)}, u32[]{:S(2)}) collective-permute-start(bf16[256,256]{1,0:T(8,128)(2,1)S(1)} %get-tuple-element.64), channel_id=1, source_target_pairs={{0,1},{1,0},{2,3},{3,2},{4,5},{5,4},{6,7},{7,6},{8,9},{9,8},{10,11... | collective-permute-start | bytes 393224 | tf_op jit(solution)/shard_map/ppermute | solution.py:324
  15.9 2.9 %collective-permute-start.6 = (bf16[256,256]{1,0:T(8,128)(2,1)S(1)}, bf16[256,256]{1,0:T(8,128)(2,1)S(1)}, u32[]{:S(2)}, u32[]{:S(2)}) collective-permute-start(bf16[256,256]{1,0:T(8,128)(2,1)S(1)} %get-tuple-element.65), channel_id=1, source_target_pairs={{0,2},{1,3},{2,0},{3,1},{4,6},{5,7},{6,4},{7,5},{8,10},{9,11},{10,... | collective-permute-start | bytes 393224 | tf_op jit(solution)/shard_map/ppermute | solution.py:324
  18.8 0.0 collective-permute-done.2.r3
  18.8 0.4 collective-permute-start.7
  19.1 2.6 %shard_map.76 = (f32[256,256]{1,0:T(8,128)S(1)}, bf16[128,256]{1,0:T(8,128)(2,1)S(1)}, bf16[128,256]{1,0:T(8,128)(2,1)S(1)}, bf16[4,640,256]{2,1,0:T(8,128)(2,1)}) custom-call(bf16[256,256]{1,0:T(8,128)(2,1)S(1)} %bitcast.28, bf16[256,256]{1,0:T(8,128)(2,1)S(1)} %collective-permute-done.r1, bf16[256,256]{1,0:T(8,128)(2,1)S(1)} %collective-permute-done.1.r2, ...), custom_call_target="tpu_custom_call" | custom-call | flops 1207959552 | bytes 5242880 | tf_op jit(solution)/shard_map/pallas_call | solution.py:54
  21.7 0.7 collective-permute-start.9
  22.4 0.0 collective-permute-done.5.g1
  22.4 2.4 %collective-permute-done.6.g2 = bf16[256,256]{1,0:T(8,128)(2,1)S(1)} collective-permute-done((bf16[256,256]{1,0:T(8,128)(2,1)S(1)}, bf16[256,256]{1,0:T(8,128)(2,1)S(1)}, u32[]{:S(2)}, u32[]{:S(2)}) %collective-permute-start.6) | collective-permute-done | bytes 131104 | tf_op jit(solution)/shard_map/ppermute | solution.py:324
  24.9 1.7 %collective-permute-done.7.g3 = bf16[256,256]{1,0:T(8,128)(2,1)S(1)} collective-permute-done((bf16[256,256]{1,0:T(8,128)(2,1)S(1)}, bf16[256,256]{1,0:T(8,128)(2,1)S(1)}, u32[]{:S(2)}, u32[]{:S(2)}) %collective-permute-start.7) | collective-permute-done | bytes 131104 | tf_op jit(solution)/shard_map/ppermute | solution.py:324
  26.6 9.1 %all-to-all-start = ((bf16[4,640,256]{2,1,0:T(8,128)(2,1)}), bf16[4,640,256]{2,1,0:T(8,128)(2,1)S(1)}, u32[]{:S(2)}, u32[]{:S(2)}) async-start(bf16[4,640,256]{2,1,0:T(8,128)(2,1)} %get-tuple-element.95), calls=%async_computation | async-start | bytes 2621440 | tf_op jit(solution)/shard_map/all_to_all | solution.py:368
  35.6 0.2 shard_map.77
  35.8 2.5 %collective-permute-start.12 = (bf16[256,256]{1,0:T(8,128)(2,1)S(1)}, bf16[256,256]{1,0:T(8,128)(2,1)S(1)}, u32[]{:S(2)}, u32[]{:S(2)}) collective-permute-start(bf16[256,256]{1,0:T(8,128)(2,1)S(1)} %get-tuple-element.82.own), channel_id=1, source_target_pairs={{0,3},{1,2},{2,1},{3,0},{4,7},{5,6},{6,5},{7,4},{8,11},{9,10},{10,... | collective-permute-start | bytes 393224 | tf_op jit(solution)/shard_map/ppermute | solution.py:319
  38.3 1.7 %collective-permute-start.10 = (bf16[256,256]{1,0:T(8,128)(2,1)S(1)}, bf16[256,256]{1,0:T(8,128)(2,1)S(1)}, u32[]{:S(2)}, u32[]{:S(2)}) collective-permute-start(bf16[256,256]{1,0:T(8,128)(2,1)S(1)} %get-tuple-element.82.own), channel_id=1, source_target_pairs={{0,1},{1,0},{2,3},{3,2},{4,5},{5,4},{6,7},{7,6},{8,9},{9,8},{10,11... | collective-permute-start | bytes 393224 | tf_op jit(solution)/shard_map/ppermute | solution.py:319
  40.0 0.7 collective-permute-start.13
  40.7 0.1 collective-permute-start.17
  40.8 2.3 %collective-permute-done.12.r3 = bf16[256,256]{1,0:T(8,128)(2,1)S(1)} collective-permute-done((bf16[256,256]{1,0:T(8,128)(2,1)S(1)}, bf16[256,256]{1,0:T(8,128)(2,1)S(1)}, u32[]{:S(2)}, u32[]{:S(2)}) %collective-permute-start.12) | collective-permute-done | bytes 131104 | tf_op jit(solution)/shard_map/ppermute | solution.py:319
  43.1 1.7 %collective-permute-done.11.r2 = bf16[256,256]{1,0:T(8,128)(2,1)S(1)} collective-permute-done((bf16[256,256]{1,0:T(8,128)(2,1)S(1)}, bf16[256,256]{1,0:T(8,128)(2,1)S(1)}, u32[]{:S(2)}, u32[]{:S(2)}) %collective-permute-start.11) | collective-permute-done | bytes 131104 | tf_op jit(solution)/shard_map/ppermute | solution.py:319
  44.8 0.0 collective-permute-done.10.r1
  44.8 0.2 shard_map.78
  45.0 0.0 copy-start.3
  45.1 5.1 %collective-permute-start.14 = (bf16[640,256]{1,0:T(8,128)(2,1)S(1)}, bf16[640,256]{1,0:T(8,128)(2,1)S(1)}, u32[]{:S(2)}, u32[]{:S(2)}) collective-permute-start(bf16[640,256]{1,0:T(8,128)(2,1)S(1)} %get-tuple-element.85), channel_id=1, source_target_pairs={{0,32},{4,36},{8,40},{12,44},{16,48},{20,52},{24,56},{28,60},{32,0... | collective-permute-start | bytes 983048 | tf_op jit(solution)/shard_map/ppermute | solution.py:336
  50.2 2.7 %collective-permute-start.15 = (bf16[640,256]{1,0:T(8,128)(2,1)S(1)}, bf16[640,256]{1,0:T(8,128)(2,1)S(1)}, u32[]{:S(2)}, u32[]{:S(2)}) collective-permute-start(bf16[640,256]{1,0:T(8,128)(2,1)S(1)} %get-tuple-element.86), channel_id=1, source_target_pairs={{0,64},{4,68},{8,72},{12,76},{16,80},{20,84},{24,88},{28,92},{32,9... | collective-permute-start | bytes 983048 | tf_op jit(solution)/shard_map/ppermute | solution.py:336
  52.9 0.1 collective-permute-start.16
  53.0 1.9 %shard_map.80 = (f32[256,256]{1,0:T(8,128)S(1)}, bf16[256,256]{1,0:T(8,128)(2,1)S(1)}, bf16[256,256]{1,0:T(8,128)(2,1)S(1)}, bf16[256,256]{1,0:T(8,128)(2,1)S(1)}, bf16[384,256]{1,0:T(8,128)(2,1)}) custom-call(bf16[256,256]{1,0:T(8,128)(2,1)S(1)} %get-tuple-element.88.grad.own, bf16[128,256]{1,0:T(8,128)(2,1)S(1)} %collective-permute-done.17.inner, ...), custom_call_target="tpu_custom_call" | custom-call | flops 1207959552 | bytes 5242880 | tf_op jit(solution)/shard_map/pallas_call | solution.py:54
  54.9 0.3 collective-permute-start.18
  55.2 3.5 %collective-permute-start.19 = (bf16[256,256]{1,0:T(8,128)(2,1)S(1)}, bf16[256,256]{1,0:T(8,128)(2,1)S(1)}, u32[]{:S(2)}, u32[]{:S(2)}) collective-permute-start(bf16[256,256]{1,0:T(8,128)(2,1)S(1)} %get-tuple-element.92), channel_id=1, source_target_pairs={{0,2},{1,3},{2,0},{3,1},{4,6},{5,7},{6,4},{7,5},{8,10},{9,11},{10,... | collective-permute-start | bytes 393224 | tf_op jit(solution)/shard_map/ppermute | solution.py:324
  58.7 1.1 %collective-permute-done.18 = bf16[256,256]{1,0:T(8,128)(2,1)S(1)} collective-permute-done((bf16[256,256]{1,0:T(8,128)(2,1)S(1)}, bf16[256,256]{1,0:T(8,128)(2,1)S(1)}, u32[]{:S(2)}, u32[]{:S(2)}) %collective-permute-start.18) | collective-permute-done | bytes 131104 | tf_op jit(solution)/shard_map/ppermute | solution.py:324
  59.8 2.4 %collective-permute-start.20 = (bf16[256,256]{1,0:T(8,128)(2,1)S(1)}, bf16[256,256]{1,0:T(8,128)(2,1)S(1)}, u32[]{:S(2)}, u32[]{:S(2)}) collective-permute-start(bf16[256,256]{1,0:T(8,128)(2,1)S(1)} %get-tuple-element.93), channel_id=1, source_target_pairs={{0,3},{1,2},{2,1},{3,0},{4,7},{5,6},{6,5},{7,4},{8,11},{9,10},{10,... | collective-permute-start | bytes 393224 | tf_op jit(solution)/shard_map/ppermute | solution.py:324
  62.2 1.5 %shard_map.79 = (f32[256,256]{1,0:T(8,128)S(1)}, bf16[128,256]{1,0:T(8,128)(2,1)S(1)}, bf16[128,256]{1,0:T(8,128)(2,1)S(1)}) custom-call(bf16[256,256]{1,0:T(8,128)(2,1)S(1)} %get-tuple-element.82.own, bf16[256,256]{1,0:T(8,128)(2,1)S(1)} %collective-permute-done.10.r1, bf16[256,256]{1,0:T(8,128)(2,1)S(1)} %collective-permute-done.11.r2, ...), custom_call_target="tpu_custom_call" | custom-call | flops 1207959552 | bytes 5242880 | tf_op jit(solution)/shard_map/pallas_call | solution.py:54
  63.8 0.0 collective-permute-done.19
  63.8 0.0 copy-start.4
  63.8 2.2 %collective-permute-done.20 = bf16[256,256]{1,0:T(8,128)(2,1)S(1)} collective-permute-done((bf16[256,256]{1,0:T(8,128)(2,1)S(1)}, bf16[256,256]{1,0:T(8,128)(2,1)S(1)}, u32[]{:S(2)}, u32[]{:S(2)}) %collective-permute-start.20) | collective-permute-done | bytes 131104 | tf_op jit(solution)/shard_map/ppermute | solution.py:324
  66.0 1.0 %collective-permute-done.15 = bf16[640,256]{1,0:T(8,128)(2,1)S(1)} collective-permute-done((bf16[640,256]{1,0:T(8,128)(2,1)S(1)}, bf16[640,256]{1,0:T(8,128)(2,1)S(1)}, u32[]{:S(2)}, u32[]{:S(2)}) %collective-permute-start.15) | collective-permute-done | bytes 327712 | tf_op jit(solution)/shard_map/ppermute | solution.py:336
  67.0 0.8 collective-permute-done.16
  67.8 0.2 pad_maximum_fusion.late
  68.0 0.0 copy-start.5
  68.0 0.0 copy-start.7
  68.0 0.1 collective-permute-start.22
  68.1 0.5 collective-permute-start.21
  68.6 2.5 %collective-permute-done.22.late_far = bf16[4,640,256]{2,1,0:T(8,128)(2,1)S(1)} collective-permute-done((bf16[4,640,256]{2,1,0:T(8,128)(2,1)S(1)}, bf16[4,640,256]{2,1,0:T(8,128)(2,1)S(1)}, u32[]{:S(2)}, u32[]{:S(2)}) %collective-permute-start.22) | collective-permute-done | bytes 1310752 | tf_op jit(solution)/shard_map/ppermute | solution.py:340
  71.1 1.9 %collective-permute-done.21.early_far = bf16[4,640,256]{2,1,0:T(8,128)(2,1)S(1)} collective-permute-done((bf16[4,640,256]{2,1,0:T(8,128)(2,1)S(1)}, bf16[4,640,256]{2,1,0:T(8,128)(2,1)S(1)}, u32[]{:S(2)}, u32[]{:S(2)}) %collective-permute-start.21) | collective-permute-done | bytes 1310752 | tf_op jit(solution)/shard_map/ppermute | solution.py:340
  73.0 2.9 %shard_map.81 = (f32[18,16,384]{2,1,0:T(8,128)S(1)}, bf16[18,16,384]{2,1,0:T(8,128)(2,1)S(1)}, bf16[18,16,384]{2,1,0:T(8,128)(2,1)S(1)}, bf16[18,16,384]{2,1,0:T(8,128)(2,1)S(1)}) custom-call(bf16[4,640,256]{2,1,0:T(8,128)(2,1)S(1)} %all-to-all-done.early, bf16[4,640,256]{2,1,0:T(8,128)(2,1)S(1)} %collective-permute-done.21.early_far, ...), custom_call_target="tpu_custom_call" | custom-call | flops 2415919104 | bytes 6348800 | tf_op jit(solution)/shard_map/pallas_call | solution.py:24
  75.9 0.1 collective-permute-start.23
  76.0 3.4 %collective-permute-start.26 = (bf16[18,16,384]{2,1,0:T(8,128)(2,1)S(1)}, bf16[18,16,384]{2,1,0:T(8,128)(2,1)S(1)}, u32[]{:S(2)}, u32[]{:S(2)}) collective-permute-start(bf16[18,16,384]{2,1,0:T(8,128)(2,1)S(1)} %get-tuple-element.112), channel_id=1, source_target_pairs={{0,16},{4,20},{8,24},{12,28},{16,0},{20,4},{24,8},{28,12},{32,48},... | collective-permute-start | bytes 663560 | tf_op jit(solution)/shard_map/ppermute | solution.py:329
  79.4 1.3 %collective-permute-start.27 = (bf16[18,16,384]{2,1,0:T(8,128)(2,1)S(1)}, bf16[18,16,384]{2,1,0:T(8,128)(2,1)S(1)}, u32[]{:S(2)}, u32[]{:S(2)}) collective-permute-start(bf16[18,16,384]{2,1,0:T(8,128)(2,1)S(1)} %get-tuple-element.113), channel_id=1, source_target_pairs={{0,24},{4,28},{8,16},{12,20},{16,8},{20,12},{24,0},{28,4},{32,56},... | collective-permute-start | bytes 663560 | tf_op jit(solution)/shard_map/ppermute | solution.py:329
  80.7 3.6 %collective-permute-done.23.r1 = bf16[18,16,384]{2,1,0:T(8,128)(2,1)S(1)} collective-permute-done((bf16[18,16,384]{2,1,0:T(8,128)(2,1)S(1)}, bf16[18,16,384]{2,1,0:T(8,128)(2,1)S(1)}, u32[]{:S(2)}, u32[]{:S(2)}) %collective-permute-start.23) | collective-permute-done | bytes 221216 | tf_op jit(solution)/shard_map/ppermute | solution.py:329
  84.3 0.7 collective-permute-start.24
  84.9 1.4 %collective-permute-start.25 = (bf16[128,256]{1,0:T(8,128)(2,1)S(1)}, bf16[128,256]{1,0:T(8,128)(2,1)S(1)}, u32[]{:S(2)}, u32[]{:S(2)}) collective-permute-start(bf16[128,256]{1,0:T(8,128)(2,1)S(1)} %get-tuple-element.105), channel_id=1, source_target_pairs={{0,4},{4,0},{8,12},{12,8},{16,20},{20,16},{24,28},{28,24},{32,36},... | collective-permute-start | bytes 196616 | tf_op jit(solution)/shard_map/ppermute | solution.py:307
  86.3 0.1 add_convert_fusion
  86.5 0.8 copy.11
  87.2 2.4 %collective-permute-done.26.r2 = bf16[18,16,384]{2,1,0:T(8,128)(2,1)S(1)} collective-permute-done((bf16[18,16,384]{2,1,0:T(8,128)(2,1)S(1)}, bf16[18,16,384]{2,1,0:T(8,128)(2,1)S(1)}, u32[]{:S(2)}, u32[]{:S(2)}) %collective-permute-start.26) | collective-permute-done | bytes 221216 | tf_op jit(solution)/shard_map/ppermute | solution.py:329
  89.7 3.3 %collective-permute-done.27.r3 = bf16[18,16,384]{2,1,0:T(8,128)(2,1)S(1)} collective-permute-done((bf16[18,16,384]{2,1,0:T(8,128)(2,1)S(1)}, bf16[18,16,384]{2,1,0:T(8,128)(2,1)S(1)}, u32[]{:S(2)}, u32[]{:S(2)}) %collective-permute-start.27) | collective-permute-done | bytes 221216 | tf_op jit(solution)/shard_map/ppermute | solution.py:329
  93.0 0.8 shard_map.82
  93.9 0.8 copy.10
  (31 shorter events, 0.2 us)
Async XLA Ops:
  1.8 9.0 %collective-permute-start.4 = (bf16[128,256]{1,0:T(8,128)(2,1)S(1)}, bf16[128,256]{1,0:T(8,128)(2,1)S(1)}, u32[]{:S(2)}, u32[]{:S(2)}) collective-permute-start(bf16[128,256]{1,0:T(8,128)(2,1)S(1)} %get-tuple-element.118), channel_id=1, source_target_pairs={{4,8},{8,4},{12,16},{16,12},{20,24},{24,20},{28,32},{32,28},{36,40... | collective-permute-start | bytes 196616 | tf_op jit(solution)/shard_map/ppermute | solution.py:307
  2.5 8.3 %collective-permute-start.3 = (bf16[128,256]{1,0:T(8,128)(2,1)S(1)}, bf16[128,256]{1,0:T(8,128)(2,1)S(1)}, u32[]{:S(2)}, u32[]{:S(2)}) collective-permute-start(bf16[128,256]{1,0:T(8,128)(2,1)S(1)} %get-tuple-element.119), channel_id=1, source_target_pairs={{0,4},{4,0},{8,12},{12,8},{16,20},{20,16},{24,28},{28,24},{32,36},... | collective-permute-start | bytes 196616 | tf_op jit(solution)/shard_map/ppermute | solution.py:307
  6.6 12.2 %collective-permute-start.2 = (bf16[256,256]{1,0:T(8,128)(2,1)S(1)}, bf16[256,256]{1,0:T(8,128)(2,1)S(1)}, u32[]{:S(2)}, u32[]{:S(2)}) collective-permute-start(bf16[256,256]{1,0:T(8,128)(2,1)S(1)} %bitcast.25), channel_id=1, source_target_pairs={{0,3},{1,2},{2,1},{3,0},{4,7},{5,6},{6,5},{7,4},{8,11},{9,10},{10,... | collective-permute-start | bytes 393224 | tf_op jit(solution)/shard_map/ppermute | solution.py:319
  9.7 9.4 %collective-permute-start.1 = (bf16[256,256]{1,0:T(8,128)(2,1)S(1)}, bf16[256,256]{1,0:T(8,128)(2,1)S(1)}, u32[]{:S(2)}, u32[]{:S(2)}) collective-permute-start(bf16[256,256]{1,0:T(8,128)(2,1)S(1)} %bitcast.26), channel_id=1, source_target_pairs={{0,2},{1,3},{2,0},{3,1},{4,6},{5,7},{6,4},{7,5},{8,10},{9,11},{10,... | collective-permute-start | bytes 393224 | tf_op jit(solution)/shard_map/ppermute | solution.py:319
  10.3 8.8 %collective-permute-start = (bf16[256,256]{1,0:T(8,128)(2,1)S(1)}, bf16[256,256]{1,0:T(8,128)(2,1)S(1)}, u32[]{:S(2)}, u32[]{:S(2)}) collective-permute-start(bf16[256,256]{1,0:T(8,128)(2,1)S(1)} %bitcast.27), channel_id=1, source_target_pairs={{0,1},{1,0},{2,3},{3,2},{4,5},{5,4},{6,7},{7,6},{8,9},{9,8},{10,11... | collective-permute-start | bytes 393224 | tf_op jit(solution)/shard_map/ppermute | solution.py:319
  10.8 2.0 %copy-start.2 = (bf16[512,27,128]{2,0,1:T(8,128)(2,1)S(1)}, bf16[512,27,128]{2,0,1:T(8,128)(2,1)}, u32[]{:S(2)}) copy-start(bf16[512,27,128]{2,0,1:T(8,128)(2,1)} %param.6) | copy-start | bytes 10616836
  12.8 6.4 %copy-start = (bf16[512,27,128]{2,0,1:T(8,128)(2,1)S(1)}, bf16[512,27,128]{2,0,1:T(8,128)(2,1)}, u32[]{:S(2)}) copy-start(bf16[512,27,128]{2,0,1:T(8,128)(2,1)} %param.5) | copy-start | bytes 10616836
  14.2 8.2 %collective-permute-start.5 = (bf16[256,256]{1,0:T(8,128)(2,1)S(1)}, bf16[256,256]{1,0:T(8,128)(2,1)S(1)}, u32[]{:S(2)}, u32[]{:S(2)}) collective-permute-start(bf16[256,256]{1,0:T(8,128)(2,1)S(1)} %get-tuple-element.64), channel_id=1, source_target_pairs={{0,1},{1,0},{2,3},{3,2},{4,5},{5,4},{6,7},{7,6},{8,9},{9,8},{10,11... | collective-permute-start | bytes 393224 | tf_op jit(solution)/shard_map/ppermute | solution.py:324
  15.9 9.0 %collective-permute-start.6 = (bf16[256,256]{1,0:T(8,128)(2,1)S(1)}, bf16[256,256]{1,0:T(8,128)(2,1)S(1)}, u32[]{:S(2)}, u32[]{:S(2)}) collective-permute-start(bf16[256,256]{1,0:T(8,128)(2,1)S(1)} %get-tuple-element.65), channel_id=1, source_target_pairs={{0,2},{1,3},{2,0},{3,1},{4,6},{5,7},{6,4},{7,5},{8,10},{9,11},{10,... | collective-permute-start | bytes 393224 | tf_op jit(solution)/shard_map/ppermute | solution.py:324
  18.8 7.8 %collective-permute-start.7 = (bf16[256,256]{1,0:T(8,128)(2,1)S(1)}, bf16[256,256]{1,0:T(8,128)(2,1)S(1)}, u32[]{:S(2)}, u32[]{:S(2)}) collective-permute-start(bf16[256,256]{1,0:T(8,128)(2,1)S(1)} %get-tuple-element.66), channel_id=1, source_target_pairs={{0,3},{1,2},{2,1},{3,0},{4,7},{5,6},{6,5},{7,4},{8,11},{9,10},{10,... | collective-permute-start | bytes 393224 | tf_op jit(solution)/shard_map/ppermute | solution.py:324
  21.7 4.8 %collective-permute-start.8 = (bf16[128,256]{1,0:T(8,128)(2,1)S(1)}, bf16[128,256]{1,0:T(8,128)(2,1)S(1)}, u32[]{:S(2)}, u32[]{:S(2)}) collective-permute-start(bf16[128,256]{1,0:T(8,128)(2,1)S(1)} %get-tuple-element.67), channel_id=1, source_target_pairs={{0,4},{4,0},{8,12},{12,8},{16,20},{20,16},{24,28},{28,24},{32,36},... | collective-permute-start | bytes 196616 | tf_op jit(solution)/shard_map/ppermute | solution.py:307
  21.7 4.8 %collective-permute-start.9 = (bf16[128,256]{1,0:T(8,128)(2,1)S(1)}, bf16[128,256]{1,0:T(8,128)(2,1)S(1)}, u32[]{:S(2)}, u32[]{:S(2)}) collective-permute-start(bf16[128,256]{1,0:T(8,128)(2,1)S(1)} %get-tuple-element.68), channel_id=1, source_target_pairs={{4,8},{8,4},{12,16},{16,12},{20,24},{24,20},{28,32},{32,28},{36,40... | collective-permute-start | bytes 196616 | tf_op jit(solution)/shard_map/ppermute | solution.py:307
  26.6 41.2 %all-to-all-start = ((bf16[4,640,256]{2,1,0:T(8,128)(2,1)}), bf16[4,640,256]{2,1,0:T(8,128)(2,1)S(1)}, u32[]{:S(2)}, u32[]{:S(2)}) async-start(bf16[4,640,256]{2,1,0:T(8,128)(2,1)} %get-tuple-element.95), calls=%async_computation | async-start | bytes 2621440 | tf_op jit(solution)/shard_map/all_to_all | solution.py:368
  35.8 7.2 %collective-permute-start.12 = (bf16[256,256]{1,0:T(8,128)(2,1)S(1)}, bf16[256,256]{1,0:T(8,128)(2,1)S(1)}, u32[]{:S(2)}, u32[]{:S(2)}) collective-permute-start(bf16[256,256]{1,0:T(8,128)(2,1)S(1)} %get-tuple-element.82.own), channel_id=1, source_target_pairs={{0,3},{1,2},{2,1},{3,0},{4,7},{5,6},{6,5},{7,4},{8,11},{9,10},{10,... | collective-permute-start | bytes 393224 | tf_op jit(solution)/shard_map/ppermute | solution.py:319
  38.3 6.5 %collective-permute-start.11 = (bf16[256,256]{1,0:T(8,128)(2,1)S(1)}, bf16[256,256]{1,0:T(8,128)(2,1)S(1)}, u32[]{:S(2)}, u32[]{:S(2)}) collective-permute-start(bf16[256,256]{1,0:T(8,128)(2,1)S(1)} %get-tuple-element.82.own), channel_id=1, source_target_pairs={{0,2},{1,3},{2,0},{3,1},{4,6},{5,7},{6,4},{7,5},{8,10},{9,11},{10,... | collective-permute-start | bytes 393224 | tf_op jit(solution)/shard_map/ppermute | solution.py:319
  38.3 6.5 %collective-permute-start.10 = (bf16[256,256]{1,0:T(8,128)(2,1)S(1)}, bf16[256,256]{1,0:T(8,128)(2,1)S(1)}, u32[]{:S(2)}, u32[]{:S(2)}) collective-permute-start(bf16[256,256]{1,0:T(8,128)(2,1)S(1)} %get-tuple-element.82.own), channel_id=1, source_target_pairs={{0,1},{1,0},{2,3},{3,2},{4,5},{5,4},{6,7},{7,6},{8,9},{9,8},{10,11... | collective-permute-start | bytes 393224 | tf_op jit(solution)/shard_map/ppermute | solution.py:319
  40.0 0.8 collective-permute-start.13
  40.7 12.3 %collective-permute-start.17 = (bf16[128,256]{1,0:T(8,128)(2,1)S(1)}, bf16[128,256]{1,0:T(8,128)(2,1)S(1)}, u32[]{:S(2)}, u32[]{:S(2)}) collective-permute-start(bf16[128,256]{1,0:T(8,128)(2,1)S(1)} %get-tuple-element.89), channel_id=1, source_target_pairs={{0,4},{4,0},{8,12},{12,8},{16,20},{20,16},{24,28},{28,24},{32,36},... | collective-permute-start | bytes 196616 | tf_op jit(solution)/shard_map/ppermute | solution.py:307
  44.8 8.1 %copy-start.1 = (bf16[512,27,128]{2,0,1:T(8,128)(2,1)S(1)}, bf16[512,27,128]{2,0,1:T(8,128)(2,1)}, u32[]{:S(2)}) copy-start(bf16[512,27,128]{2,0,1:T(8,128)(2,1)} %param.5) | copy-start | bytes 10616836
  45.0 17.2 %copy-start.3 = (bf16[512,27,128]{2,0,1:T(8,128)(2,1)S(1)}, bf16[512,27,128]{2,0,1:T(8,128)(2,1)}, u32[]{:S(2)}) copy-start(bf16[512,27,128]{2,0,1:T(8,128)(2,1)} %param.6) | copy-start | bytes 10616836
  45.1 21.0 %collective-permute-start.14 = (bf16[640,256]{1,0:T(8,128)(2,1)S(1)}, bf16[640,256]{1,0:T(8,128)(2,1)S(1)}, u32[]{:S(2)}, u32[]{:S(2)}) collective-permute-start(bf16[640,256]{1,0:T(8,128)(2,1)S(1)} %get-tuple-element.85), channel_id=1, source_target_pairs={{0,32},{4,36},{8,40},{12,44},{16,48},{20,52},{24,56},{28,60},{32,0... | collective-permute-start | bytes 983048 | tf_op jit(solution)/shard_map/ppermute | solution.py:336
  50.2 16.8 %collective-permute-start.15 = (bf16[640,256]{1,0:T(8,128)(2,1)S(1)}, bf16[640,256]{1,0:T(8,128)(2,1)S(1)}, u32[]{:S(2)}, u32[]{:S(2)}) collective-permute-start(bf16[640,256]{1,0:T(8,128)(2,1)S(1)} %get-tuple-element.86), channel_id=1, source_target_pairs={{0,64},{4,68},{8,72},{12,76},{16,80},{20,84},{24,88},{28,92},{32,9... | collective-permute-start | bytes 983048 | tf_op jit(solution)/shard_map/ppermute | solution.py:336
  52.9 15.0 %collective-permute-start.16 = (bf16[640,256]{1,0:T(8,128)(2,1)S(1)}, bf16[640,256]{1,0:T(8,128)(2,1)S(1)}, u32[]{:S(2)}, u32[]{:S(2)}) collective-permute-start(bf16[640,256]{1,0:T(8,128)(2,1)S(1)} %get-tuple-element.87), channel_id=1, source_target_pairs={{0,96},{4,100},{8,104},{12,108},{16,112},{20,116},{24,120},{28,124... | collective-permute-start | bytes 983048 | tf_op jit(solution)/shard_map/ppermute | solution.py:336
  54.9 5.0 %collective-permute-start.18 = (bf16[256,256]{1,0:T(8,128)(2,1)S(1)}, bf16[256,256]{1,0:T(8,128)(2,1)S(1)}, u32[]{:S(2)}, u32[]{:S(2)}) collective-permute-start(bf16[256,256]{1,0:T(8,128)(2,1)S(1)} %get-tuple-element.91), channel_id=1, source_target_pairs={{0,1},{1,0},{2,3},{3,2},{4,5},{5,4},{6,7},{7,6},{8,9},{9,8},{10,11... | collective-permute-start | bytes 393224 | tf_op jit(solution)/shard_map/ppermute | solution.py:324
  55.2 8.6 %collective-permute-start.19 = (bf16[256,256]{1,0:T(8,128)(2,1)S(1)}, bf16[256,256]{1,0:T(8,128)(2,1)S(1)}, u32[]{:S(2)}, u32[]{:S(2)}) collective-permute-start(bf16[256,256]{1,0:T(8,128)(2,1)S(1)} %get-tuple-element.92), channel_id=1, source_target_pairs={{0,2},{1,3},{2,0},{3,1},{4,6},{5,7},{6,4},{7,5},{8,10},{9,11},{10,... | collective-permute-start | bytes 393224 | tf_op jit(solution)/shard_map/ppermute | solution.py:324
  59.8 6.2 %collective-permute-start.20 = (bf16[256,256]{1,0:T(8,128)(2,1)S(1)}, bf16[256,256]{1,0:T(8,128)(2,1)S(1)}, u32[]{:S(2)}, u32[]{:S(2)}) collective-permute-start(bf16[256,256]{1,0:T(8,128)(2,1)S(1)} %get-tuple-element.93), channel_id=1, source_target_pairs={{0,3},{1,2},{2,1},{3,0},{4,7},{5,6},{6,5},{7,4},{8,11},{9,10},{10,... | collective-permute-start | bytes 393224 | tf_op jit(solution)/shard_map/ppermute | solution.py:324
  63.8 3.2 %copy-start.4 = (bf16[256,256]{1,0:T(8,128)(2,1)}, bf16[256,256]{1,0:T(8,128)(2,1)S(1)}, u32[]{:S(2)}) copy-start(bf16[256,256]{1,0:T(8,128)(2,1)S(1)} %collective-permute-done.19) | copy-start | bytes 393220
  66.0 1.0 %copy-start.6 = (bf16[256,256]{1,0:T(8,128)(2,1)}, bf16[256,256]{1,0:T(8,128)(2,1)S(1)}, u32[]{:S(2)}) copy-start(bf16[256,256]{1,0:T(8,128)(2,1)S(1)} %collective-permute-done.20) | copy-start | bytes 393220
  68.0 18.4 %copy-start.5 = (bf16[256,256]{1,0:T(8,128)(2,1)S(1)}, bf16[256,256]{1,0:T(8,128)(2,1)}, u32[]{:S(2)}) copy-start(bf16[256,256]{1,0:T(8,128)(2,1)} %copy-done.4) | copy-start | bytes 393220
  68.0 18.3 %copy-start.7 = (bf16[256,256]{1,0:T(8,128)(2,1)S(1)}, bf16[256,256]{1,0:T(8,128)(2,1)}, u32[]{:S(2)}) copy-start(bf16[256,256]{1,0:T(8,128)(2,1)} %copy-done.6) | copy-start | bytes 393220
  68.0 3.1 %collective-permute-start.22 = (bf16[4,640,256]{2,1,0:T(8,128)(2,1)S(1)}, bf16[4,640,256]{2,1,0:T(8,128)(2,1)S(1)}, u32[]{:S(2)}, u32[]{:S(2)}) collective-permute-start(bf16[4,640,256]{2,1,0:T(8,128)(2,1)S(1)} %pad_maximum_fusion.late), channel_id=1, source_target_pairs={{0,4},{4,0},{8,12},{12,8},{16,20},{20,16},{24,28},{28,24},{32,36},... | collective-permute-start | bytes 3932168 | tf_op jit(solution)/shard_map/ppermute | solution.py:340
  68.1 4.9 %collective-permute-start.21 = (bf16[4,640,256]{2,1,0:T(8,128)(2,1)S(1)}, bf16[4,640,256]{2,1,0:T(8,128)(2,1)S(1)}, u32[]{:S(2)}, u32[]{:S(2)}) collective-permute-start(bf16[4,640,256]{2,1,0:T(8,128)(2,1)S(1)} %all-to-all-done.early), channel_id=1, source_target_pairs={{0,4},{4,0},{8,12},{12,8},{16,20},{20,16},{24,28},{28,24},{32,36},... | collective-permute-start | bytes 3932168 | tf_op jit(solution)/shard_map/ppermute | solution.py:340
  75.9 8.4 %collective-permute-start.23 = (bf16[18,16,384]{2,1,0:T(8,128)(2,1)S(1)}, bf16[18,16,384]{2,1,0:T(8,128)(2,1)S(1)}, u32[]{:S(2)}, u32[]{:S(2)}) collective-permute-start(bf16[18,16,384]{2,1,0:T(8,128)(2,1)S(1)} %get-tuple-element.101), channel_id=1, source_target_pairs={{0,8},{4,12},{8,0},{12,4},{16,24},{20,28},{24,16},{28,20},{32,40},... | collective-permute-start | bytes 663560 | tf_op jit(solution)/shard_map/ppermute | solution.py:329
  76.0 13.7 %collective-permute-start.26 = (bf16[18,16,384]{2,1,0:T(8,128)(2,1)S(1)}, bf16[18,16,384]{2,1,0:T(8,128)(2,1)S(1)}, u32[]{:S(2)}, u32[]{:S(2)}) collective-permute-start(bf16[18,16,384]{2,1,0:T(8,128)(2,1)S(1)} %get-tuple-element.112), channel_id=1, source_target_pairs={{0,16},{4,20},{8,24},{12,28},{16,0},{20,4},{24,8},{28,12},{32,48},... | collective-permute-start | bytes 663560 | tf_op jit(solution)/shard_map/ppermute | solution.py:329
  79.4 13.6 %collective-permute-start.27 = (bf16[18,16,384]{2,1,0:T(8,128)(2,1)S(1)}, bf16[18,16,384]{2,1,0:T(8,128)(2,1)S(1)}, u32[]{:S(2)}, u32[]{:S(2)}) collective-permute-start(bf16[18,16,384]{2,1,0:T(8,128)(2,1)S(1)} %get-tuple-element.113), channel_id=1, source_target_pairs={{0,24},{4,28},{8,16},{12,20},{16,8},{20,12},{24,0},{28,4},{32,56},... | collective-permute-start | bytes 663560 | tf_op jit(solution)/shard_map/ppermute | solution.py:329
  84.3 9.5 %collective-permute-start.24 = (bf16[128,256]{1,0:T(8,128)(2,1)S(1)}, bf16[128,256]{1,0:T(8,128)(2,1)S(1)}, u32[]{:S(2)}, u32[]{:S(2)}) collective-permute-start(bf16[128,256]{1,0:T(8,128)(2,1)S(1)} %get-tuple-element.104), channel_id=1, source_target_pairs={{4,8},{8,4},{12,16},{16,12},{20,24},{24,20},{28,32},{32,28},{36,40... | collective-permute-start | bytes 196616 | tf_op jit(solution)/shard_map/ppermute | solution.py:307
  84.9 8.9 %collective-permute-start.25 = (bf16[128,256]{1,0:T(8,128)(2,1)S(1)}, bf16[128,256]{1,0:T(8,128)(2,1)S(1)}, u32[]{:S(2)}, u32[]{:S(2)}) collective-permute-start(bf16[128,256]{1,0:T(8,128)(2,1)S(1)} %get-tuple-element.105), channel_id=1, source_target_pairs={{0,4},{4,0},{8,12},{12,8},{16,20},{20,16},{24,28},{28,24},{32,36},... | collective-permute-start | bytes 196616 | tf_op jit(solution)/shard_map/ppermute | solution.py:307
